TPU v7x, 512 devices: a whole 4x4x16 slice. The times are simulated.
512 devices in a mesh: grp: 32 (over z_hi, y, core), aux: 16 (over x, z_lo).
Axes of the slice: x: 4, y: 4, z: 16 (z_hi: 4, z_lo: 4; z = z_hi * 4 + z_lo), core: 2. Of those that a mesh axis runs over, the one named last changes fastest.
Arguments:
- half_ints: float32 [2560, 128, 1280], P('aux', 'grp'), may hold values from -0.9 to 0.9
- virt_coeff: float32 [1280, 640], P('aux'), may hold values from -0.15625 to 0.15625
- occ_energy: float32 [128], replicated, may hold values from -2 to -0.3
- vir_energy: float32 [640], replicated, may hold values from 0.1 to 3
- aux_sizes: int32 [16], replicated, may hold values from 1 to 160, 1920 in all
- pair_root: int32 [4], replicated, may hold values from 0 to 31
Outputs:
- gamma: float32 [2560, 81920], P(None, ('grp', 'aux'))
Inputs may be any that keep to these rules, and one draw needn't show every extreme that they name: aux_sizes sums to 1920 and its largest entry is exactly 160.
All inputs are finite; a program needn't handle non-finite values.
Results may differ from a plain program's by a relative error of at most 0.0003.
Values sent between devices are 32-bit elements; how exact they have to be, the bound alone decides.
No kernel may reach another device: no remote copies, remote signals or barrier semaphores. Data moves between devices by JAX's collectives and lax.ppermute only.
A program may use at most 128 MiB of HBM per device.

v0:
```python
import jax
import jax.numpy as jnp
from jax import lax
from jax.experimental import pallas as pl
from jax.experimental.pallas import tpu as pltpu
from jax.sharding import Mesh, PartitionSpec as P


ZHI, Y, CORE, X, ZLO = 4, 4, 2, 4, 4
AXES = ("zh", "y", "c", "x", "zl")
FAST = lax.Precision.HIGH


def route(dz=0, dzh=0, dy=0, dc=0):
    pairs = []
    for zh in range(ZHI):
        for y in range(Y):
            for c in range(CORE):
                for x in range(X):
                    for zl in range(ZLO):
                        z = (zh * ZLO + zl + dz + dzh * ZLO) % (ZHI * ZLO)
                        source = (((zh * Y + y) * CORE + c) * X + x) * ZLO + zl
                        target = (((z // ZLO * Y + (y + dy) % Y) * CORE + (c ^ dc)) * X + x) * ZLO + z % ZLO
                        pairs.append((source, target))
    return pairs


def moved(block, **delta):
    return lax.ppermute(block, AXES, route(**delta))


def gathered(block, axis):
    count = lax.axis_size(axis)
    return lax.all_to_all(jnp.broadcast_to(block[None], (count,) + block.shape), axis, 0, 0)


def pick(blocks, place):
    return lax.dynamic_index_in_dim(blocks, place, 0, keepdims=False)


def ring_y(block):
    return [block, moved(block, dy=-1), moved(block, dy=2), moved(block, dy=1)]


def both_cores(block, other, core):
    return jnp.where(core == 0, jnp.stack([block, other]), jnp.stack([other, block]))


def own_core_part(half_ints, pair_root, c):
    rows_dev, slots, basis_count = half_ints.shape
    step = rows_dev // (Y * CORE * 4)
    split = half_ints.reshape(Y, step, CORE, 4, slots, basis_count)
    mine = lax.dynamic_index_in_dim(split, c, 2, keepdims=False)
    other = moved(lax.dynamic_index_in_dim(split, 1 - c, 2, keepdims=False), dc=1)
    return jnp.where((pair_root % CORE)[:, None] == c, mine, other)


def own_y_part(part, pair_root, y):
    distance = ((pair_root // CORE - y) % Y)[:, None]
    chosen = pick(part, y)
    for hop in range(1, Y):
        came = moved(pick(part, (y - hop) % Y), dy=-hop)
        chosen = jnp.where(distance == hop, came, chosen)
    return chosen.reshape(-1, *chosen.shape[2:]).transpose(1, 0, 2)


def split_float(value):
    high = value.astype(jnp.bfloat16)
    return high, (value - high.astype(jnp.float32)).astype(jnp.bfloat16)


def three_pass(left, right, dims):
    left_high, left_low = split_float(left)
    right_high, right_low = split_float(right)

    def product(p, q):
        return lax.dot_general(p, q, (dims, ((), ())), preferred_element_type=jnp.float32)

    return product(left_high, right_high) + product(left_high, right_low) + product(left_low, right_high)


def pair_kernel(place_ref, *refs):
    near, far, held_ref, pair_ref, partner_ref = refs[:Y], refs[Y : 2 * Y], refs[2 * Y], refs[2 * Y + 1], refs[2 * Y + 2]
    y, c = place_ref[0], place_ref[1]
    part_rows, vir_count = near[0].shape[1:]
    tiles = part_rows // 8
    band = 2 * part_rows // X
    lower = lax.broadcasted_iota(jnp.int32, (tiles, 8, vir_count), 1) < 4
    first = c == 0
    for hop in range(Y):
        mine = near[hop][0].reshape(tiles, 8, vir_count)
        other = far[hop][0].reshape(tiles, 8, vir_count)
        zero = jnp.where(first, mine, other)
        one = jnp.where(first, other, mine)
        even = jnp.where(lower, zero, pltpu.roll(one, 4, 1))
        odd = jnp.where(lower, pltpu.roll(zero, 4, 1), one)
        rows = jnp.stack([even, odd], 1).reshape(X, band, vir_count)
        start = pl.multiple_of(lax.rem(y + hop, Y) * band, 8)
        partner_ref[:, 0, pl.ds(start, band), :] = rows
    block = partner_ref[:, 0].reshape(X * Y * band, vir_count)
    product = three_pass(held_ref[0], block, ((1,), (0,)))

    @pl.when(pl.program_id(0) == 0)
    def _():
        pair_ref[...] = product

    @pl.when(pl.program_id(0) > 0)
    def _():
        pair_ref[...] += product


def pair_with_partner(near, far, held, y, c):
    part_rows, vir_count = near[0].shape[1:]
    width_dev, lanes = held.shape[1:]
    rows_dev = part_rows * Y * CORE // X
    part = pl.BlockSpec((1, part_rows, vir_count), lambda z: (z, 0, 0))
    pair, partner = pl.pallas_call(
        pair_kernel,
        grid=(ZLO,),
        out_shape=(
            jax.ShapeDtypeStruct((width_dev, vir_count), jnp.float32),
            jax.ShapeDtypeStruct((X, ZLO, rows_dev, vir_count), jnp.float32),
        ),
        in_specs=[pl.BlockSpec(memory_space=pltpu.SMEM)]
        + [part] * (2 * Y)
        + [pl.BlockSpec((1, width_dev, lanes), lambda z: (z, 0, 0))],
        out_specs=(
            pl.BlockSpec((width_dev, vir_count), lambda z: (0, 0)),
            pl.BlockSpec((X, 1, rows_dev, vir_count), lambda z: (0, z, 0, 0)),
        ),
        compiler_params=pltpu.CompilerParams(
            dimension_semantics=("arbitrary",), vmem_limit_bytes=24 << 20
        ),
        cost_estimate=pl.CostEstimate(
            flops=6 * width_dev * X * ZLO * rows_dev * vir_count, bytes_accessed=16 << 20, transcendentals=0
        ),
        name="pair_kernel",
    )(jnp.stack([y, c]).astype(jnp.int32), *(pltpu.with_memory_space_constraint(v, pltpu.HBM) for v in (*near, *far, held)))
    return pair, partner.reshape(X * ZLO * rows_dev, vir_count)


def shards(half_ints, virt_coeff, occ_energy, vir_energy, aux_sizes, pair_root):
    rows_dev, occ_grp, basis_count = half_ints.shape
    vir_count = virt_coeff.shape[1]
    zh, y, c, x, zl = (lax.axis_index(a) for a in AXES)
    width_dev = vir_count // ZLO
    step = rows_dev // (Y * CORE * 4)
    root = pick(pair_root, x)

    coeff_rows = virt_coeff.shape[0] // CORE
    coeff = gathered(lax.dynamic_slice_in_dim(virt_coeff, c * coeff_rows, coeff_rows, 0), "zl")
    raw = own_core_part(half_ints, pair_root, c)
    coeff, raw = lax.optimization_barrier((coeff, raw))
    raw = own_y_part(raw, pair_root, y)
    coeff = gathered(coeff, "x")
    raw = lax.all_to_all(raw, "x", 0, 0).reshape(X * step * 4, basis_count)
    coeff = both_cores(coeff, moved(coeff, dc=1), c)
    coeff = coeff.transpose(1, 2, 0, 3, 4).reshape(basis_count, vir_count)

    part = jnp.dot(raw, coeff, precision=FAST, preferred_element_type=jnp.float32)
    sizes = lax.dynamic_index_in_dim(aux_sizes.reshape(X, ZLO), zl, 1)[:, :, None]
    place = y * (rows_dev // Y) + lax.iota(jnp.int32, step)[:, None] * 8 + c * 4 + lax.iota(jnp.int32, 4)[None, :]
    part = part * (place < sizes).astype(jnp.float32).reshape(-1, 1)

    own_size = pick(aux_sizes, x * ZLO + zl)
    live_rows = (lax.iota(jnp.int32, rows_dev) < own_size).astype(jnp.float32)
    transformed = jnp.einsum("pim,ma->ipa", half_ints, coeff, precision=FAST, preferred_element_type=jnp.float32)
    transformed = transformed * live_rows[None, :, None]

    half = part.shape[0] // 2
    up, down = moved(part, dzh=1), moved(part, dzh=-1)
    up, down, transformed = lax.optimization_barrier((up, down, transformed))
    low, high = moved(up[:half], dzh=1), moved(down[half:], dzh=-1)
    orbital_rows = lax.all_to_all(transformed, "x", 0, 0).reshape(X * rows_dev, vir_count)
    distance = (zh - root // (Y * CORE)) % ZHI
    across = jnp.concatenate([low, high], 0)
    part = jnp.where(distance == 0, part, jnp.where(distance == 1, up, jnp.where(distance == 2, across, down)))
    near = gathered(part, "zl")
    near, orbital_rows = lax.optimization_barrier((near, orbital_rows))
    near = ring_y(near)
    far = [moved(r, dc=1) for r in near]

    held = orbital_rows.T.reshape(ZLO, width_dev, X * rows_dev)
    held = lax.all_to_all(held, "zl", 0, 0)

    pair_rows, partner = pair_with_partner(near, far, held, y, c)
    sent = pair_rows.reshape(width_dev, ZLO, width_dev).transpose(1, 0, 2)
    came = lax.all_to_all(sent, "zl", 0, 0)
    pair_cols = came.transpose(2, 0, 1).reshape(width_dev, vir_count)

    own_orbital = ((zh * Y + y) * CORE + c) * occ_grp + x
    partner_orbital = root * occ_grp + x
    occ_sum = pick(occ_energy, own_orbital) + pick(occ_energy, partner_orbital)
    vir_rows = lax.dynamic_slice_in_dim(vir_energy, zl * width_dev, width_dev)
    denominator = occ_sum - vir_rows[:, None] - vir_energy[None, :]
    amplitude = (2.0 * pair_rows - pair_cols) / denominator
    return jnp.dot(partner, amplitude.T, precision=FAST, preferred_element_type=jnp.float32)


def solution(mesh):
    fine = Mesh(mesh.devices.reshape(ZHI, Y, CORE, X, ZLO), AXES)
    groups, functions = ("zh", "y", "c"), ("x", "zl")
    return jax.shard_map(
        shards,
        mesh=fine,
        in_specs=(P(functions, groups, None), P(functions, None), P(), P(), P(), P()),
        out_specs=P(None, groups + functions),
        check_vma=False,
    )
```

profile of v0, /device:TPU:1, one launch (start us, length us, event | category | flops | bytes accessed | tf_op | source)
XLA Modules:
  0.0 287.2 jit_solution(17515577817150254660)
XLA Ops:
  0.0 2.9 dynamic-slice_bitcast_fusion
  2.9 8.7 %collective-permute-start = (f32[4,5,4,4,1280]{4,3,2,1,0:T(4,128)}, f32[4,5,4,4,1280]{4,3,2,1,0:T(4,128)}, u32[]{:S(2)}, u32[]{:S(2)}) collective-permute-start(f32[4,5,4,4,1280]{4,3,2,1,0:T(4,128)} %dynamic-slice_bitcast_fusion), channel_id=1, source_target_pairs={{0,16},{1,17},{2,18},{3,19},{4,20},{5,21},{6,22},{7,23},{8,24},{9,... | collective-permute-start | bytes 4915208 | tf_op jit(solution)/shard_map/ppermute | solution.py:29
  12.5 4.1 %all-to-all-start = ((f32[4,40,640]{2,1,0:T(8,128)}), f32[4,40,640]{2,1,0:T(8,128)}, u32[]{:S(2)}, u32[]{:S(2)}) async-start(f32[4,40,640]{2,1,0:T(8,128)} %broadcast_in_dim.54), calls=%async_computation | async-start | bytes 819200 | tf_op jit(solution)/shard_map/all_to_all | solution.py:34
  16.6 3.5 %bitcast_select_fusion = f32[4,5,4,4,1280]{4,3,2,1,0:T(4,128)} fusion(f32[4,5,4,4,1280]{4,3,2,1,0:T(4,128)} %collective-permute-done, f32[4,5,2,4,4,1280]{5,4,3,2,1,0:T(4,128)S(1)} %bitcast.53, s32[]{:T(128)S(6)} %select_n.133, pred[4]{0:T(512)(128)(4,1)S(1)} %get-tuple-element.32), kind=kLoop, calls=%fused_computation.3 | loop fusion | flops 409600 | bytes 4915208 | tf_op jit(solution)/shard_map/jit(_where)/select_n | solution.py:55
  20.1 8.6 %all-to-all-done = f32[4,40,640]{2,1,0:T(8,128)} async-done(((f32[4,40,640]{2,1,0:T(8,128)}), f32[4,40,640]{2,1,0:T(8,128)}, u32[]{:S(2)}, u32[]{:S(2)}) %all-to-all-start) | async-done | bytes 409632 | tf_op jit(solution)/shard_map/all_to_all | solution.py:34
  28.7 2.3 broadcast_in_dim.58
  31.0 4.4 %all-to-all-start.2 = ((f32[4,4,40,640]{3,2,1,0:T(8,128)}), f32[4,4,40,640]{3,2,1,0:T(8,128)}, u32[]{:S(2)}, u32[]{:S(2)}) async-start(f32[4,4,40,640]{3,2,1,0:T(8,128)} %broadcast_in_dim.58), calls=%async_computation.2 | async-start | bytes 3276800 | tf_op jit(solution)/shard_map/all_to_all | solution.py:34
  36.4 19.7 %all-to-all-done.2 = f32[4,4,40,640]{3,2,1,0:T(8,128)} async-done(((f32[4,4,40,640]{3,2,1,0:T(8,128)}), f32[4,4,40,640]{3,2,1,0:T(8,128)}, u32[]{:S(2)}, u32[]{:S(2)}) %all-to-all-start.2) | async-done | bytes 1638432 | tf_op jit(solution)/shard_map/all_to_all | solution.py:34
  56.1 3.6 %collective-permute-start.4 = (f32[4,4,40,640]{3,2,1,0:T(8,128)}, f32[4,4,40,640]{3,2,1,0:T(8,128)}, u32[]{:S(2)}, u32[]{:S(2)}) collective-permute-start(f32[4,4,40,640]{3,2,1,0:T(8,128)} %all-to-all-done.2), channel_id=1, source_target_pairs={{0,16},{1,17},{2,18},{3,19},{4,20},{5,21},{6,22},{7,23},{8,24},{9,... | collective-permute-start | bytes 4915208 | tf_op jit(solution)/shard_map/ppermute | solution.py:29
  59.7 1.3 dynamic-slice_bitcast_fusion.1
  61.1 1.9 collective-permute-start.3
  63.0 1.9 collective-permute-start.2
  64.9 3.4 %collective-permute-start.1 = (f32[5,4,4,1280]{3,2,1,0:T(4,128)S(1)}, f32[5,4,4,1280]{3,2,1,0:T(4,128)S(1)}, u32[]{:S(2)}, u32[]{:S(2)}) collective-permute-start(f32[5,4,4,1280]{3,2,1,0:T(4,128)S(1)} %get-tuple-element.27), channel_id=1, source_target_pairs={{0,32},{1,33},{2,34},{3,35},{4,36},{5,37},{6,38},{7,39},{8,40},{9,... | collective-permute-start | bytes 1228808 | tf_op jit(solution)/shard_map/ppermute | solution.py:29
  68.4 5.6 %collective-permute-done.3 = f32[5,4,4,1280]{3,2,1,0:T(4,128)S(1)} collective-permute-done((f32[5,4,4,1280]{3,2,1,0:T(4,128)S(1)}, f32[5,4,4,1280]{3,2,1,0:T(4,128)S(1)}, u32[]{:S(2)}, u32[]{:S(2)}) %collective-permute-start.3) | collective-permute-done | bytes 409632 | tf_op jit(solution)/shard_map/ppermute | solution.py:29
  74.0 3.5 %collective-permute-done.2 = f32[5,4,4,1280]{3,2,1,0:T(4,128)S(1)} collective-permute-done((f32[5,4,4,1280]{3,2,1,0:T(4,128)S(1)}, f32[5,4,4,1280]{3,2,1,0:T(4,128)S(1)}, u32[]{:S(2)}, u32[]{:S(2)}) %collective-permute-start.2) | collective-permute-done | bytes 409632 | tf_op jit(solution)/shard_map/ppermute | solution.py:29
  77.4 9.1 %collective-permute-done.1 = f32[5,4,4,1280]{3,2,1,0:T(4,128)S(1)} collective-permute-done((f32[5,4,4,1280]{3,2,1,0:T(4,128)S(1)}, f32[5,4,4,1280]{3,2,1,0:T(4,128)S(1)}, u32[]{:S(2)}, u32[]{:S(2)}) %collective-permute-start.1) | collective-permute-done | bytes 409632 | tf_op jit(solution)/shard_map/ppermute | solution.py:29
  86.6 1.3 fusion.5
  88.8 4.1 %all-to-all-start.1 = ((f32[4,20,1280]{2,1,0:T(8,128)}), f32[4,20,1280]{2,1,0:T(8,128)}, u32[]{:S(2)}, u32[]{:S(2)}) async-start(f32[4,20,1280]{2,1,0:T(8,128)} %copy.21), calls=%async_computation.1 | async-start | bytes 983040 | tf_op jit(solution)/shard_map/all_to_all | solution.py:156
  93.8 8.0 %all-to-all-done.1 = f32[4,20,1280]{2,1,0:T(8,128)} async-done(((f32[4,20,1280]{2,1,0:T(8,128)}), f32[4,20,1280]{2,1,0:T(8,128)}, u32[]{:S(2)}, u32[]{:S(2)}) %all-to-all-start.1) | async-done | bytes 409632 | tf_op jit(solution)/shard_map/all_to_all | solution.py:156
  101.7 1.8 reshape.103
  103.6 3.3 %maximum_select_fusion = f32[2,4,4,40,640]{4,3,0,2,1:T(8,128)S(1)} fusion(f32[1,4,4,40,640]{4,3,0,2,1:T(8,128)} %bitcast.13, f32[1,4,4,40,640]{4,3,0,2,1:T(8,128)} %bitcast.12, pred[]{:T(512)S(6)} %eq.45), kind=kLoop, calls=%fused_computation | loop fusion | flops 2457600 | bytes 6553601 | tf_op jit(solution)/shard_map/jit(_where)/select_n | solution.py:46
  106.9 1.3 convolution_multiply_fusion
  108.2 9.8 %collective-permute-start.6 = (f32[80,640]{1,0:T(8,128)S(1)}, f32[80,640]{1,0:T(8,128)S(1)}, u32[]{:S(2)}, u32[]{:S(2)}) collective-permute-start(f32[80,640]{1,0:T(8,128)S(1)} %convolution_multiply_fusion), channel_id=1, source_target_pairs={{0,384},{1,385},{2,386},{3,387},{4,388},{5,389},{6,390},{7,391},{8... | collective-permute-start | bytes 614408 | tf_op jit(solution)/shard_map/ppermute | solution.py:29
  118.0 1.9 collective-permute-start.5
  119.9 5.5 %multiply_bitcast_fusion = f32[4,160,640]{2,1,0:T(8,128)} fusion(f32[1280,640,1]{1,0,2:T(8,128)S(1)} %bitcast.51, f32[160,4,1280]{2,1,0:T(4,128)S(1)} %copy-done.2, f32[160]{0:T(256)S(1)} %compare_convert_fusion.1), kind=kOutput, calls=%fused_computation.4 | convolution fusion | flops 3146137600 | bytes 8192640 | tf_op jit(solution)/shard_map/pim,ma->ipa/dot_general | solution.py:167
  125.4 7.8 %collective-permute-done.6 = f32[80,640]{1,0:T(8,128)S(1)} collective-permute-done((f32[80,640]{1,0:T(8,128)S(1)}, f32[80,640]{1,0:T(8,128)S(1)}, u32[]{:S(2)}, u32[]{:S(2)}) %collective-permute-start.6) | collective-permute-done | bytes 204832 | tf_op jit(solution)/shard_map/ppermute | solution.py:29
  133.9 9.6 %collective-permute-done.5 = f32[80,640]{1,0:T(8,128)} collective-permute-done((f32[80,640]{1,0:T(8,128)S(1)}, f32[80,640]{1,0:T(8,128)}, u32[]{:S(2)}, u32[]{:S(2)}) %collective-permute-start.5) | collective-permute-done | bytes 204832 | tf_op jit(solution)/shard_map/ppermute | solution.py:29
  143.5 3.7 %all-to-all-start.4 = ((f32[4,160,640]{2,1,0:T(8,128)}), f32[4,160,640]{2,1,0:T(8,128)S(1)}, u32[]{:S(2)}, u32[]{:S(2)}) async-start(f32[4,160,640]{2,1,0:T(8,128)} %multiply_bitcast_fusion), calls=%async_computation.4 | async-start | bytes 3276800 | tf_op jit(solution)/shard_map/all_to_all | solution.py:174
  148.1 2.2 collective-permute-start.8
  150.3 7.0 %collective-permute-start.7 = (f32[40,640]{1,0:T(8,128)S(1)}, f32[40,640]{1,0:T(8,128)S(1)}, u32[]{:S(2)}, u32[]{:S(2)}) collective-permute-start(f32[40,640]{1,0:T(8,128)S(1)} %slice.6), channel_id=1, source_target_pairs={{0,128},{1,129},{2,130},{3,131},{4,132},{5,133},{6,134},{7,135},{8... | collective-permute-start | bytes 307208 | tf_op jit(solution)/shard_map/ppermute | solution.py:29
  160.6 7.5 %all-to-all-done.4 = f32[4,160,640]{2,1,0:T(8,128)S(1)} async-done(((f32[4,160,640]{2,1,0:T(8,128)}), f32[4,160,640]{2,1,0:T(8,128)S(1)}, u32[]{:S(2)}, u32[]{:S(2)}) %all-to-all-start.4) | async-done | bytes 1638432 | tf_op jit(solution)/shard_map/all_to_all | solution.py:174
  168.2 22.2 %all_to_all.35.refs_0_ = f32[4,80,640]{2,1,0:T(8,128)S(1)} all-to-all(f32[4,80,640]{2,1,0:T(8,128)S(1)} %broadcast_in_dim.59), channel_id=1, replica_groups=mesh['zh'=4,'y'=4,'c'=2,'x'=4,'zl'=4] {'zl'}, dimensions={0} | all-to-all | bytes 1638400 | tf_op jit(solution)/shard_map/all_to_all | solution.py:34
  190.4 1.7 copy.23
  192.1 3.6 %all-to-all-start.5 = ((f32[4,160,640]{2,1,0:T(8,128)}), f32[4,160,640]{2,1,0:T(8,128)S(1)}, u32[]{:S(2)}, u32[]{:S(2)}) async-start(f32[4,160,640]{2,1,0:T(8,128)} %bitcast.22), calls=%async_computation.5 | async-start | bytes 3276800 | tf_op jit(solution)/shard_map/all_to_all | solution.py:184
  195.6 1.9 collective-permute-start.11
  197.6 2.3 collective-permute-start.10
  199.8 4.2 %collective-permute-start.9 = (f32[4,80,640]{2,1,0:T(8,128)S(1)}, f32[4,80,640]{2,1,0:T(8,128)S(1)}, u32[]{:S(2)}, u32[]{:S(2)}) collective-permute-start(f32[4,80,640]{2,1,0:T(8,128)S(1)} %all_to_all.35.refs_0_), channel_id=1, source_target_pairs={{0,96},{1,97},{2,98},{3,99},{4,100},{5,101},{6,102},{7,103},{8,104... | collective-permute-start | bytes 2457608 | tf_op jit(solution)/shard_map/ppermute | solution.py:29
  204.1 4.4 %collective-permute-start.12 = (f32[4,80,640]{2,1,0:T(8,128)S(1)}, f32[4,80,640]{2,1,0:T(8,128)S(1)}, u32[]{:S(2)}, u32[]{:S(2)}) collective-permute-start(f32[4,80,640]{2,1,0:T(8,128)S(1)} %all_to_all.35.refs_0_), channel_id=1, source_target_pairs={{0,16},{1,17},{2,18},{3,19},{4,20},{5,21},{6,22},{7,23},{8,24},{9,... | collective-permute-start | bytes 2457608 | tf_op jit(solution)/shard_map/ppermute | solution.py:29
  208.5 10.1 %collective-permute-done.11.refs_3_ = f32[4,80,640]{2,1,0:T(8,128)S(1)} collective-permute-done((f32[4,80,640]{2,1,0:T(8,128)S(1)}, f32[4,80,640]{2,1,0:T(8,128)S(1)}, u32[]{:S(2)}, u32[]{:S(2)}) %collective-permute-start.11) | collective-permute-done | bytes 819232 | tf_op jit(solution)/shard_map/ppermute | solution.py:29
  218.6 20.2 %collective-permute-start.15 = (f32[4,80,640]{2,1,0:T(8,128)S(1)}, f32[4,80,640]{2,1,0:T(8,128)S(1)}, u32[]{:S(2)}, u32[]{:S(2)}) collective-permute-start(f32[4,80,640]{2,1,0:T(8,128)S(1)} %collective-permute-done.11.refs_3_), channel_id=1, source_target_pairs={{0,16},{1,17},{2,18},{3,19},{4,20},{5,21},{6,22},{7,23},{8,24},{9,... | collective-permute-start | bytes 2457608 | tf_op jit(solution)/shard_map/ppermute | solution.py:29
  238.9 1.9 collective-permute-start.14
  240.8 2.6 collective-permute-start.13
  245.6 1.2 copy-done.3
  246.8 6.9 %pair_kernel.1 = (f32[160,640]{1,0:T(8,128)S(1)}, f32[4,4,160,640]{3,2,1,0:T(8,128)S(1)}) custom-call(s32[2]{0:T(128)S(1)} %pad_add_fusion.place_ref, f32[4,80,640]{2,1,0:T(8,128)} %copy-done.4, f32[4,80,640]{2,1,0:T(8,128)} %copy-done.8, f32[4,80,640]{2,1,0:T(8,128)} %copy-done.7, f32[4,80,640]{2,1,0:T(8,128)} %copy-done.6, f32[4,80,640]{2,1,0:T(8,128)} %copy-done.9, ...), custom_call_target="tpu_custom_call" | custom-call | flops 1572864000 | bytes 16777216 | tf_op jit(solution)/shard_map/pair_kernel/pallas_call | solution.py:117
  253.7 2.7 copy-done.1
  257.9 4.5 %all-to-all-start.6 = ((f32[4,160,160]{2,1,0:T(8,128)}), f32[4,160,160]{2,1,0:T(8,128)S(1)}, u32[]{:S(2)}, u32[]{:S(2)}) async-start(f32[4,160,160]{2,1,0:T(8,128)} %bitcast.48), calls=%async_computation.6 | async-start | bytes 1310720 | tf_op jit(solution)/shard_map/all_to_all | solution.py:188
  265.1 14.3 %all-to-all-done.6 = f32[4,160,160]{2,1,0:T(8,128)S(1)} async-done(((f32[4,160,160]{2,1,0:T(8,128)}), f32[4,160,160]{2,1,0:T(8,128)S(1)}, u32[]{:S(2)}, u32[]{:S(2)}) %all-to-all-start.6) | async-done | bytes 409632 | tf_op jit(solution)/shard_map/all_to_all | solution.py:188
  279.6 7.6 %fusion.6 = f32[2560,160]{0,1:T(8,128)} fusion(f32[2560,640]{1,0:T(8,128)} %bitcast.49, f32[160,640]{1,0:T(8,128)S(1)} %copy.26, f32[160,640]{1,0:T(8,128)S(1)} %get-tuple-element.22, f32[640]{0:T(1024)S(1)} %copy-done.16, f32[160]{0:T(256)S(1)} %dynamic-slice_subtract_fusion), kind=kOutput, calls=%fused_computation.11 | convolution fusion | flops 1573273600 | bytes 9014400 | tf_op jit(solution)/shard_map/dot_general | solution.py:197
  (73 shorter events, 10.4 us)
Async XLA Ops:
  0.0 11.6 %copy-start = (f32[80,640]{1,0:T(8,128)S(1)}, f32[80,640]{1,0:T(8,128)}, u32[]{:S(2)}) copy-start(f32[80,640]{1,0:T(8,128)} %param.7) | copy-start | bytes 614404
  0.0 16.6 %copy-start.2 = (f32[160,4,1280]{2,1,0:T(4,128)S(1)}, f32[160,4,1280]{2,1,0:T(4,128)}, u32[]{:S(2)}) copy-start(f32[160,4,1280]{2,1,0:T(4,128)} %param.6) | copy-start | bytes 9830404
  0.0 16.6 %copy-start.19 = (s32[4]{0:T(128)S(1)}, s32[4]{0:T(128)}, u32[]{:S(2)}) copy-start(s32[4]{0:T(128)} %param.11) | copy-start | bytes 52
  2.9 13.7 %collective-permute-start = (f32[4,5,4,4,1280]{4,3,2,1,0:T(4,128)}, f32[4,5,4,4,1280]{4,3,2,1,0:T(4,128)}, u32[]{:S(2)}, u32[]{:S(2)}) collective-permute-start(f32[4,5,4,4,1280]{4,3,2,1,0:T(4,128)} %dynamic-slice_bitcast_fusion), channel_id=1, source_target_pairs={{0,16},{1,17},{2,18},{3,19},{4,20},{5,21},{6,22},{7,23},{8,24},{9,... | collective-permute-start | bytes 4915208 | tf_op jit(solution)/shard_map/ppermute | solution.py:29
  12.5 16.3 %all-to-all-start = ((f32[4,40,640]{2,1,0:T(8,128)}), f32[4,40,640]{2,1,0:T(8,128)}, u32[]{:S(2)}, u32[]{:S(2)}) async-start(f32[4,40,640]{2,1,0:T(8,128)} %broadcast_in_dim.54), calls=%async_computation | async-start | bytes 819200 | tf_op jit(solution)/shard_map/all_to_all | solution.py:34
  20.1 15.4 %copy-start.18 = (s32[16]{0:T(128)S(1)}, s32[16]{0:T(128)}, u32[]{:S(2)}) copy-start(s32[16]{0:T(128)} %param.10) | copy-start | bytes 196
  31.0 25.1 %all-to-all-start.2 = ((f32[4,4,40,640]{3,2,1,0:T(8,128)}), f32[4,4,40,640]{3,2,1,0:T(8,128)}, u32[]{:S(2)}, u32[]{:S(2)}) async-start(f32[4,4,40,640]{3,2,1,0:T(8,128)} %broadcast_in_dim.58), calls=%async_computation.2 | async-start | bytes 3276800 | tf_op jit(solution)/shard_map/all_to_all | solution.py:34
  56.1 47.5 %collective-permute-start.4 = (f32[4,4,40,640]{3,2,1,0:T(8,128)}, f32[4,4,40,640]{3,2,1,0:T(8,128)}, u32[]{:S(2)}, u32[]{:S(2)}) collective-permute-start(f32[4,4,40,640]{3,2,1,0:T(8,128)} %all-to-all-done.2), channel_id=1, source_target_pairs={{0,16},{1,17},{2,18},{3,19},{4,20},{5,21},{6,22},{7,23},{8,24},{9,... | collective-permute-start | bytes 4915208 | tf_op jit(solution)/shard_map/ppermute | solution.py:29
  61.1 12.9 %collective-permute-start.3 = (f32[5,4,4,1280]{3,2,1,0:T(4,128)S(1)}, f32[5,4,4,1280]{3,2,1,0:T(4,128)S(1)}, u32[]{:S(2)}, u32[]{:S(2)}) collective-permute-start(f32[5,4,4,1280]{3,2,1,0:T(4,128)S(1)} %get-tuple-element.25), channel_id=1, source_target_pairs={{0,96},{1,97},{2,98},{3,99},{4,100},{5,101},{6,102},{7,103},{8,104... | collective-permute-start | bytes 1228808 | tf_op jit(solution)/shard_map/ppermute | solution.py:29
  63.0 14.4 %collective-permute-start.2 = (f32[5,4,4,1280]{3,2,1,0:T(4,128)S(1)}, f32[5,4,4,1280]{3,2,1,0:T(4,128)S(1)}, u32[]{:S(2)}, u32[]{:S(2)}) collective-permute-start(f32[5,4,4,1280]{3,2,1,0:T(4,128)S(1)} %get-tuple-element.26), channel_id=1, source_target_pairs={{0,64},{1,65},{2,66},{3,67},{4,68},{5,69},{6,70},{7,71},{8,72},{9,... | collective-permute-start | bytes 1228808 | tf_op jit(solution)/shard_map/ppermute | solution.py:29
  64.9 21.7 %collective-permute-start.1 = (f32[5,4,4,1280]{3,2,1,0:T(4,128)S(1)}, f32[5,4,4,1280]{3,2,1,0:T(4,128)S(1)}, u32[]{:S(2)}, u32[]{:S(2)}) collective-permute-start(f32[5,4,4,1280]{3,2,1,0:T(4,128)S(1)} %get-tuple-element.27), channel_id=1, source_target_pairs={{0,32},{1,33},{2,34},{3,35},{4,36},{5,37},{6,38},{7,39},{8,40},{9,... | collective-permute-start | bytes 1228808 | tf_op jit(solution)/shard_map/ppermute | solution.py:29
  88.8 13.0 %all-to-all-start.1 = ((f32[4,20,1280]{2,1,0:T(8,128)}), f32[4,20,1280]{2,1,0:T(8,128)}, u32[]{:S(2)}, u32[]{:S(2)}) async-start(f32[4,20,1280]{2,1,0:T(8,128)} %copy.21), calls=%async_computation.1 | async-start | bytes 983040 | tf_op jit(solution)/shard_map/all_to_all | solution.py:156
  103.6 3.3 %copy-start.5 = (f32[80,1280]{1,0:T(8,128)S(1)}, f32[80,1280]{1,0:T(8,128)}, u32[]{:S(2)}) copy-start(f32[80,1280]{1,0:T(8,128)} %reshape.103) | copy-start | bytes 1228804
  108.2 17.3 %copy-start.12 = (f32[80,640]{1,0:T(8,128)}, f32[80,640]{1,0:T(8,128)S(1)}, u32[]{:S(2)}) copy-start(f32[80,640]{1,0:T(8,128)S(1)} %convolution_multiply_fusion) | copy-start | bytes 614404
  108.2 25.1 %collective-permute-start.6 = (f32[80,640]{1,0:T(8,128)S(1)}, f32[80,640]{1,0:T(8,128)S(1)}, u32[]{:S(2)}, u32[]{:S(2)}) collective-permute-start(f32[80,640]{1,0:T(8,128)S(1)} %convolution_multiply_fusion), channel_id=1, source_target_pairs={{0,384},{1,385},{2,386},{3,387},{4,388},{5,389},{6,390},{7,391},{8... | collective-permute-start | bytes 614408 | tf_op jit(solution)/shard_map/ppermute | solution.py:29
  118.0 25.5 %collective-permute-start.5 = (f32[80,640]{1,0:T(8,128)S(1)}, f32[80,640]{1,0:T(8,128)}, u32[]{:S(2)}, u32[]{:S(2)}) collective-permute-start(f32[80,640]{1,0:T(8,128)S(1)} %convolution_multiply_fusion), channel_id=1, source_target_pairs={{0,128},{1,129},{2,130},{3,131},{4,132},{5,133},{6,134},{7,135},{8... | collective-permute-start | bytes 614408 | tf_op jit(solution)/shard_map/ppermute | solution.py:29
  133.2 0.7 copy-start.14
  133.9 26.6 %copy-start.13 = (f32[80,640]{1,0:T(8,128)S(1)}, f32[80,640]{1,0:T(8,128)}, u32[]{:S(2)}) copy-start(f32[80,640]{1,0:T(8,128)} %copy-done.12) | copy-start | bytes 614404
  143.5 4.6 %copy-start.15 = (f32[80,640]{1,0:T(8,128)S(1)}, f32[80,640]{1,0:T(8,128)}, u32[]{:S(2)}) copy-start(f32[80,640]{1,0:T(8,128)} %copy-done.14) | copy-start | bytes 614404
  143.5 24.7 %all-to-all-start.4 = ((f32[4,160,640]{2,1,0:T(8,128)}), f32[4,160,640]{2,1,0:T(8,128)S(1)}, u32[]{:S(2)}, u32[]{:S(2)}) async-start(f32[4,160,640]{2,1,0:T(8,128)} %multiply_bitcast_fusion), calls=%async_computation.4 | async-start | bytes 3276800 | tf_op jit(solution)/shard_map/all_to_all | solution.py:174
  148.1 12.4 %collective-permute-start.8 = (f32[40,640]{1,0:T(8,128)S(1)}, f32[40,640]{1,0:T(8,128)S(1)}, u32[]{:S(2)}, u32[]{:S(2)}) collective-permute-start(f32[40,640]{1,0:T(8,128)S(1)} %slice.7), channel_id=1, source_target_pairs={{0,384},{1,385},{2,386},{3,387},{4,388},{5,389},{6,390},{7,391},{8... | collective-permute-start | bytes 307208 | tf_op jit(solution)/shard_map/ppermute | solution.py:29
  150.3 10.2 %collective-permute-start.7 = (f32[40,640]{1,0:T(8,128)S(1)}, f32[40,640]{1,0:T(8,128)S(1)}, u32[]{:S(2)}, u32[]{:S(2)}) collective-permute-start(f32[40,640]{1,0:T(8,128)S(1)} %slice.6), channel_id=1, source_target_pairs={{0,128},{1,129},{2,130},{3,131},{4,132},{5,133},{6,134},{7,135},{8... | collective-permute-start | bytes 307208 | tf_op jit(solution)/shard_map/ppermute | solution.py:29
  190.4 13.7 %copy-start.4 = (f32[4,80,640]{2,1,0:T(8,128)}, f32[4,80,640]{2,1,0:T(8,128)S(1)}, u32[]{:S(2)}) copy-start(f32[4,80,640]{2,1,0:T(8,128)S(1)} %all_to_all.35.refs_0_) | copy-start | bytes 2457604
  192.1 53.6 %all-to-all-start.5 = ((f32[4,160,640]{2,1,0:T(8,128)}), f32[4,160,640]{2,1,0:T(8,128)S(1)}, u32[]{:S(2)}, u32[]{:S(2)}) async-start(f32[4,160,640]{2,1,0:T(8,128)} %bitcast.22), calls=%async_computation.5 | async-start | bytes 3276800 | tf_op jit(solution)/shard_map/all_to_all | solution.py:184
  195.6 23.0 %collective-permute-start.11 = (f32[4,80,640]{2,1,0:T(8,128)S(1)}, f32[4,80,640]{2,1,0:T(8,128)S(1)}, u32[]{:S(2)}, u32[]{:S(2)}) collective-permute-start(f32[4,80,640]{2,1,0:T(8,128)S(1)} %all_to_all.35.refs_0_), channel_id=1, source_target_pairs={{0,32},{1,33},{2,34},{3,35},{4,36},{5,37},{6,38},{7,39},{8,40},{9,... | collective-permute-start | bytes 2457608 | tf_op jit(solution)/shard_map/ppermute | solution.py:29
  197.6 41.3 %collective-permute-start.10 = (f32[4,80,640]{2,1,0:T(8,128)S(1)}, f32[4,80,640]{2,1,0:T(8,128)S(1)}, u32[]{:S(2)}, u32[]{:S(2)}) collective-permute-start(f32[4,80,640]{2,1,0:T(8,128)S(1)} %all_to_all.35.refs_0_), channel_id=1, source_target_pairs={{0,64},{1,65},{2,66},{3,67},{4,68},{5,69},{6,70},{7,71},{8,72},{9,... | collective-permute-start | bytes 2457608 | tf_op jit(solution)/shard_map/ppermute | solution.py:29
  199.8 41.0 %collective-permute-start.9 = (f32[4,80,640]{2,1,0:T(8,128)S(1)}, f32[4,80,640]{2,1,0:T(8,128)S(1)}, u32[]{:S(2)}, u32[]{:S(2)}) collective-permute-start(f32[4,80,640]{2,1,0:T(8,128)S(1)} %all_to_all.35.refs_0_), channel_id=1, source_target_pairs={{0,96},{1,97},{2,98},{3,99},{4,100},{5,101},{6,102},{7,103},{8,104... | collective-permute-start | bytes 2457608 | tf_op jit(solution)/shard_map/ppermute | solution.py:29
  204.1 39.4 %collective-permute-start.12 = (f32[4,80,640]{2,1,0:T(8,128)S(1)}, f32[4,80,640]{2,1,0:T(8,128)S(1)}, u32[]{:S(2)}, u32[]{:S(2)}) collective-permute-start(f32[4,80,640]{2,1,0:T(8,128)S(1)} %all_to_all.35.refs_0_), channel_id=1, source_target_pairs={{0,16},{1,17},{2,18},{3,19},{4,20},{5,21},{6,22},{7,23},{8,24},{9,... | collective-permute-start | bytes 2457608 | tf_op jit(solution)/shard_map/ppermute | solution.py:29
  218.6 24.9 %copy-start.6 = (f32[4,80,640]{2,1,0:T(8,128)}, f32[4,80,640]{2,1,0:T(8,128)S(1)}, u32[]{:S(2)}) copy-start(f32[4,80,640]{2,1,0:T(8,128)S(1)} %collective-permute-done.11.refs_3_) | copy-start | bytes 2457604
  218.6 24.9 %collective-permute-start.15 = (f32[4,80,640]{2,1,0:T(8,128)S(1)}, f32[4,80,640]{2,1,0:T(8,128)S(1)}, u32[]{:S(2)}, u32[]{:S(2)}) collective-permute-start(f32[4,80,640]{2,1,0:T(8,128)S(1)} %collective-permute-done.11.refs_3_), channel_id=1, source_target_pairs={{0,16},{1,17},{2,18},{3,19},{4,20},{5,21},{6,22},{7,23},{8,24},{9,... | collective-permute-start | bytes 2457608 | tf_op jit(solution)/shard_map/ppermute | solution.py:29
  238.9 4.7 %copy-start.7 = (f32[4,80,640]{2,1,0:T(8,128)}, f32[4,80,640]{2,1,0:T(8,128)S(1)}, u32[]{:S(2)}) copy-start(f32[4,80,640]{2,1,0:T(8,128)S(1)} %collective-permute-done.10.refs_2_) | copy-start | bytes 2457604
  238.9 4.6 %collective-permute-start.14 = (f32[4,80,640]{2,1,0:T(8,128)S(1)}, f32[4,80,640]{2,1,0:T(8,128)S(1)}, u32[]{:S(2)}, u32[]{:S(2)}) collective-permute-start(f32[4,80,640]{2,1,0:T(8,128)S(1)} %collective-permute-done.10.refs_2_), channel_id=1, source_target_pairs={{0,16},{1,17},{2,18},{3,19},{4,20},{5,21},{6,22},{7,23},{8,24},{9,... | collective-permute-start | bytes 2457608 | tf_op jit(solution)/shard_map/ppermute | solution.py:29
  240.8 2.7 copy-start.8
  240.8 4.8 %collective-permute-start.13 = (f32[4,80,640]{2,1,0:T(8,128)S(1)}, f32[4,80,640]{2,1,0:T(8,128)}, u32[]{:S(2)}, u32[]{:S(2)}) collective-permute-start(f32[4,80,640]{2,1,0:T(8,128)S(1)} %collective-permute-done.9.refs_1_), channel_id=1, source_target_pairs={{0,16},{1,17},{2,18},{3,19},{4,20},{5,21},{6,22},{7,23},{8,24},{9,... | collective-permute-start | bytes 2457608 | tf_op jit(solution)/shard_map/ppermute | solution.py:29
  243.5 0.9 copy-start.9
  243.5 1.2 copy-start.10
  244.7 0.9 copy-start.11
  245.6 1.2 copy-start.3
  253.7 2.7 copy-start.1
  256.4 6.6 %copy-start.17 = (f32[128]{0:T(128)S(1)}, f32[128]{0:T(128)}, u32[]{:S(2)}) copy-start(f32[128]{0:T(128)} %param.8) | copy-start | bytes 1540
  256.4 8.6 %copy-start.16 = (f32[640]{0:T(1024)S(1)}, f32[640]{0:T(1024)}, u32[]{:S(2)}) copy-start(f32[640]{0:T(1024)} %param.9) | copy-start | bytes 7684
  257.9 21.5 %all-to-all-start.6 = ((f32[4,160,160]{2,1,0:T(8,128)}), f32[4,160,160]{2,1,0:T(8,128)S(1)}, u32[]{:S(2)}, u32[]{:S(2)}) async-start(f32[4,160,160]{2,1,0:T(8,128)} %bitcast.48), calls=%async_computation.6 | async-start | bytes 1310720 | tf_op jit(solution)/shard_map/all_to_all | solution.py:188
where the time goes:
time: 289 us; the launch traced here: 287 us
  waiting for transfers between devices  104 us (36%)
  starting transfers between devices  102 us (35%)
  local copies, waits for them, and re-layouts  23.2 us (8%)
  blocking collectives  22.2 us (8%)
  matrix products  14.4 us (5%)
  other arithmetic  9.17 us (3%)
  Pallas kernels  6.89 us (2%)
  between operations  5.1 us (2%)
    ppermute x16, starting transfers between devices, moved(): return lax.ppermute(block, AXES, route(**delta))  78 us
    ppermute x16, waiting for transfers between devices, moved(): return lax.ppermute(block, AXES, route(**delta))  45.7 us
    all_to_all x2, waiting for transfers between devices, gathered(): lax.all_to_all(jnp.broadcast_to(block[None], (count,) + block.shape), axi...  28.3 us
    all_to_all x1, blocking collectives, gathered(): lax.all_to_all(jnp.broadcast_to(block[None], (count,) + block.shape), axi...  22.2 us
    all_to_all x1, waiting for transfers between devices, shards(): came = lax.all_to_all(sent, 'zl', 0, 0)  14.3 us
    all_to_all x2, starting transfers between devices, gathered(): lax.all_to_all(jnp.broadcast_to(block[None], (count,) + block.shape), axi...  8.46 us
    all_to_all x1, waiting for transfers between devices, shards(): raw = lax.all_to_all(raw, 'x', 0, 0).reshape(X * step * 4, basis_count)  7.96 us
    dot_general x1, matrix products, shards(): jnp.dot(partner, amplitude.T, precision=FAST, preferred_element_type=jnp....  7.58 us
  transfers between devices with their start and end apart: 22, of which 11 were waited for; matrix products, arithmetic and copies ran while one was open for 7% of the time, Pallas kernels for 0%

commit v1 on v0

--- a/solution.py
+++ b/solution.py
@@ -9,6 +9,7 @@
 ZHI, Y, CORE, X, ZLO = 4, 4, 2, 4, 4
 AXES = ("zh", "y", "c", "x", "zl")
 FAST = lax.Precision.HIGH
+LANES = 128
 
 
 def route(dz=0, dzh=0, dy=0, dc=0):
@@ -70,17 +71,15 @@
 
 
 def three_pass(left, right, dims):
-    left_high, left_low = split_float(left)
-    right_high, right_low = split_float(right)
-
     def product(p, q):
         return lax.dot_general(p, q, (dims, ((), ())), preferred_element_type=jnp.float32)
 
-    return product(left_high, right_high) + product(left_high, right_low) + product(left_low, right_high)
+    return product(left[0], right[0]) + product(left[0], right[1]) + product(left[1], right[0])
 
 
 def pair_kernel(place_ref, *refs):
-    near, far, held_ref, pair_ref, partner_ref = refs[:Y], refs[Y : 2 * Y], refs[2 * Y], refs[2 * Y + 1], refs[2 * Y + 2]
+    near, far, held_ref = refs[:Y], refs[Y : 2 * Y], refs[2 * Y]
+    pair_ref, sent_ref, high_ref, low_ref, rows_ref = refs[2 * Y + 1 :]
     y, c = place_ref[0], place_ref[1]
     part_rows, vir_count = near[0].shape[1:]
     tiles = part_rows // 8
@@ -96,47 +95,121 @@
         odd = jnp.where(lower, pltpu.roll(zero, 4, 1), one)
         rows = jnp.stack([even, odd], 1).reshape(X, band, vir_count)
         start = pl.multiple_of(lax.rem(y + hop, Y) * band, 8)
-        partner_ref[:, 0, pl.ds(start, band), :] = rows
-    block = partner_ref[:, 0].reshape(X * Y * band, vir_count)
-    product = three_pass(held_ref[0], block, ((1,), (0,)))
-
-    @pl.when(pl.program_id(0) == 0)
+        rows_ref[:, pl.ds(start, band), :] = rows
+    block = split_float(rows_ref[...].reshape(X * Y * band, vir_count))
+    high_ref[:, 0] = block[0].reshape(X, Y * band, vir_count)
+    low_ref[:, 0] = block[1].reshape(X, Y * band, vir_count)
+    product = three_pass(split_float(held_ref[0]), block, ((1,), (0,)))
+    step = pl.program_id(0)
+
+    @pl.when(step == 0)
     def _():
         pair_ref[...] = product
 
-    @pl.when(pl.program_id(0) > 0)
+    @pl.when(step > 0)
     def _():
         pair_ref[...] += product
+
+    @pl.when(step == ZLO - 1)
+    def _():
+        width = pair_ref.shape[0]
+        for target in range(ZLO):
+            part = pair_ref[:, target * width : (target + 1) * width]
+            sent_ref[target, :width] = part[:, :LANES]
+            quarter = width // 4
+            side = part[:, LANES:]
+            sent_ref[target, width:] = jnp.concatenate(
+                [side[g * quarter : (g + 1) * quarter] for g in range(4)], 1
+            )
 
 
 def pair_with_partner(near, far, held, y, c):
     part_rows, vir_count = near[0].shape[1:]
     width_dev, lanes = held.shape[1:]
     rows_dev = part_rows * Y * CORE // X
+    packed = (ZLO, width_dev * width_dev // LANES, LANES)
     part = pl.BlockSpec((1, part_rows, vir_count), lambda z: (z, 0, 0))
-    pair, partner = pl.pallas_call(
+    wide = pl.BlockSpec((X, 1, rows_dev, vir_count), lambda z: (0, z, 0, 0))
+    operands = [pltpu.with_memory_space_constraint(v, pltpu.HBM) for v in (*near, *far, held)]
+    return pl.pallas_call(
         pair_kernel,
         grid=(ZLO,),
         out_shape=(
             jax.ShapeDtypeStruct((width_dev, vir_count), jnp.float32),
-            jax.ShapeDtypeStruct((X, ZLO, rows_dev, vir_count), jnp.float32),
+            jax.ShapeDtypeStruct(packed, jnp.float32),
+            pltpu.HBM((X, ZLO, rows_dev, vir_count), jnp.bfloat16),
+            pltpu.HBM((X, ZLO, rows_dev, vir_count), jnp.bfloat16),
         ),
         in_specs=[pl.BlockSpec(memory_space=pltpu.SMEM)]
         + [part] * (2 * Y)
         + [pl.BlockSpec((1, width_dev, lanes), lambda z: (z, 0, 0))],
         out_specs=(
             pl.BlockSpec((width_dev, vir_count), lambda z: (0, 0)),
-            pl.BlockSpec((X, 1, rows_dev, vir_count), lambda z: (0, z, 0, 0)),
-        ),
-        compiler_params=pltpu.CompilerParams(
-            dimension_semantics=("arbitrary",), vmem_limit_bytes=24 << 20
-        ),
+            pl.BlockSpec(packed, lambda z: (0, 0, 0)),
+            wide,
+            wide,
+        ),
+        scratch_shapes=[pltpu.VMEM((X, rows_dev, vir_count), jnp.float32)],
+        compiler_params=pltpu.CompilerParams(dimension_semantics=("arbitrary",), vmem_limit_bytes=26 << 20),
         cost_estimate=pl.CostEstimate(
             flops=6 * width_dev * X * ZLO * rows_dev * vir_count, bytes_accessed=16 << 20, transcendentals=0
         ),
         name="pair_kernel",
-    )(jnp.stack([y, c]).astype(jnp.int32), *(pltpu.with_memory_space_constraint(v, pltpu.HBM) for v in (*near, *far, held)))
-    return pair, partner.reshape(X * ZLO * rows_dev, vir_count)
+    )(jnp.stack([y, c]).astype(jnp.int32), *operands)
+
+
+def density_kernel(pair_ref, came_ref, row_ref, column_ref, high_ref, low_ref, gamma_ref, cols_ref, amp_ref):
+    width = pair_ref.shape[0]
+
+    @pl.when(pl.program_id(0) == 0)
+    def _():
+        quarter = width // 4
+        fill = width - LANES
+        cols_ref[...] = jnp.zeros_like(cols_ref)
+        for source in range(ZLO):
+            rows = slice(source * width, (source + 1) * width)
+            cols_ref[rows, :LANES] = came_ref[source, :width]
+            side = came_ref[source, width:]
+            for g in range(4):
+                part = slice(source * width + g * quarter, source * width + (g + 1) * quarter)
+                cols_ref[part, LANES:width] = side[:, g * fill : (g + 1) * fill]
+        columns = cols_ref[...].T[:width]
+        amplitude = (2.0 * pair_ref[...] - columns) / (row_ref[...] - column_ref[...])
+        high, low = split_float(amplitude)
+        amp_ref[0] = high
+        amp_ref[1] = low
+
+    block = (high_ref[0].reshape(-1, high_ref.shape[-1]), low_ref[0].reshape(-1, low_ref.shape[-1]))
+    gamma_ref[...] = three_pass((amp_ref[0], amp_ref[1]), block, ((1,), (1,)))
+
+
+def densities(pair, came, row_part, column_part, high, low):
+    width_dev, vir_count = pair.shape
+    rows_dev = high.shape[2]
+    whole = pl.BlockSpec((1, ZLO, rows_dev, vir_count), lambda x: (x, 0, 0, 0))
+    return pl.pallas_call(
+        density_kernel,
+        grid=(X,),
+        out_shape=jax.ShapeDtypeStruct((width_dev, X * ZLO * rows_dev), jnp.float32),
+        in_specs=[
+            pl.BlockSpec((width_dev, vir_count), lambda x: (0, 0)),
+            pl.BlockSpec(came.shape, lambda x: (0, 0, 0)),
+            pl.BlockSpec((width_dev, 1), lambda x: (0, 0)),
+            pl.BlockSpec((1, vir_count), lambda x: (0, 0)),
+            whole,
+            whole,
+        ],
+        out_specs=pl.BlockSpec((width_dev, ZLO * rows_dev), lambda x: (0, x)),
+        scratch_shapes=[
+            pltpu.VMEM((ZLO * width_dev, 2 * LANES), jnp.float32),
+            pltpu.VMEM((2, width_dev, vir_count), jnp.bfloat16),
+        ],
+        compiler_params=pltpu.CompilerParams(dimension_semantics=("arbitrary",), vmem_limit_bytes=20 << 20),
+        cost_estimate=pl.CostEstimate(
+            flops=6 * width_dev * X * ZLO * rows_dev * vir_count, bytes_accessed=10 << 20, transcendentals=0
+        ),
+        name="density_kernel",
+    )(pair, came, row_part, column_part, *(pltpu.with_memory_space_constraint(v, pltpu.HBM) for v in (high, low)))
 
 
 def shards(half_ints, virt_coeff, occ_energy, vir_energy, aux_sizes, pair_root):
@@ -150,7 +223,6 @@
     coeff_rows = virt_coeff.shape[0] // CORE
     coeff = gathered(lax.dynamic_slice_in_dim(virt_coeff, c * coeff_rows, coeff_rows, 0), "zl")
     raw = own_core_part(half_ints, pair_root, c)
-    coeff, raw = lax.optimization_barrier((coeff, raw))
     raw = own_y_part(raw, pair_root, y)
     coeff = gathered(coeff, "x")
     raw = lax.all_to_all(raw, "x", 0, 0).reshape(X * step * 4, basis_count)
@@ -168,8 +240,8 @@
     transformed = transformed * live_rows[None, :, None]
 
     half = part.shape[0] // 2
-    up, down = moved(part, dzh=1), moved(part, dzh=-1)
-    up, down, transformed = lax.optimization_barrier((up, down, transformed))
+    up = moved(part, dzh=1)
+    down = moved(part, dzh=-1)
     low, high = moved(up[:half], dzh=1), moved(down[half:], dzh=-1)
     orbital_rows = lax.all_to_all(transformed, "x", 0, 0).reshape(X * rows_dev, vir_count)
     distance = (zh - root // (Y * CORE)) % ZHI
@@ -183,18 +255,14 @@
     held = orbital_rows.T.reshape(ZLO, width_dev, X * rows_dev)
     held = lax.all_to_all(held, "zl", 0, 0)
 
-    pair_rows, partner = pair_with_partner(near, far, held, y, c)
-    sent = pair_rows.reshape(width_dev, ZLO, width_dev).transpose(1, 0, 2)
+    pair_rows, sent, high, low = pair_with_partner(near, far, held, y, c)
     came = lax.all_to_all(sent, "zl", 0, 0)
-    pair_cols = came.transpose(2, 0, 1).reshape(width_dev, vir_count)
 
     own_orbital = ((zh * Y + y) * CORE + c) * occ_grp + x
     partner_orbital = root * occ_grp + x
     occ_sum = pick(occ_energy, own_orbital) + pick(occ_energy, partner_orbital)
     vir_rows = lax.dynamic_slice_in_dim(vir_energy, zl * width_dev, width_dev)
-    denominator = occ_sum - vir_rows[:, None] - vir_energy[None, :]
-    amplitude = (2.0 * pair_rows - pair_cols) / denominator
-    return jnp.dot(partner, amplitude.T, precision=FAST, preferred_element_type=jnp.float32)
+    return densities(pair_rows, came, (occ_sum - vir_rows)[:, None], vir_energy[None, :], high, low).T
 
 
 def solution(mesh):

time: 289 us -> 265 us (0.917)
  the two profiles are of different devices: /device:TPU:1 before, /device:TPU:4 now
where the time goes in v1:
time: 265 us; the launch traced here: 263 us
  waiting for transfers between devices  95.1 us (36%)
  starting transfers between devices  89.3 us (34%)
  blocking collectives  23.7 us (9%)
  local copies, waits for them, and re-layouts  18.6 us (7%)
  Pallas kernels  16.2 us (6%)
  other arithmetic  7.89 us (3%)
  matrix products  7.86 us (3%)
  between operations  4.83 us (2%)
    ppermute x16, waiting for transfers between devices, moved(): return lax.ppermute(block, AXES, route(**delta))  61.4 us
    ppermute x16, starting transfers between devices, moved(): return lax.ppermute(block, AXES, route(**delta))  57.8 us
    all_to_all x2, waiting for transfers between devices, gathered(): lax.all_to_all(jnp.broadcast_to(block[None], (count,) + block.shape), axi...  23.7 us
    all_to_all x1, blocking collectives, gathered(): lax.all_to_all(jnp.broadcast_to(block[None], (count,) + block.shape), axi...  23.7 us
    all_to_all x2, starting transfers between devices, gathered(): lax.all_to_all(jnp.broadcast_to(block[None], (count,) + block.shape), axi...  11.3 us
    all_to_all x1, waiting for transfers between devices, shards(): came = lax.all_to_all(sent, 'zl', 0, 0)  9.93 us
    pallas_call x1, Pallas kernels, pair_with_partner(): pl.pallas_call(pair_kernel, grid=(ZLO,), out_shape=(jax.ShapeDtypeStruct(...  9.18 us
    pallas_call x1, Pallas kernels, densities(): pl.pallas_call(density_kernel, grid=(X,), out_shape=jax.ShapeDtypeStruct(...  7.06 us
  transfers between devices with their start and end apart: 22, of which 11 were waited for; matrix products, arithmetic and copies ran while one was open for 10% of the time, Pallas kernels for 0%

profile of v1, /device:TPU:4, one launch (start us, length us, event | category | flops | bytes accessed | tf_op | source)
XLA Modules:
  0.0 263.4 jit_solution(15742480940164891399)
XLA Ops:
  0.0 0.9 copy-done
  1.7 5.9 %all-to-all-start.1 = ((f32[4,40,640]{2,1,0:T(8,128)}), f32[4,40,640]{2,1,0:T(8,128)}, u32[]{:S(2)}, u32[]{:S(2)}) async-start(f32[4,40,640]{2,1,0:T(8,128)} %broadcast_in_dim.61), calls=%async_computation.1 | async-start | bytes 819200 | tf_op jit(solution)/shard_map/all_to_all | solution.py:35
  7.6 2.7 %dynamic-slice_bitcast_fusion = f32[4,5,4,4,1280]{4,3,2,1,0:T(4,128)} fusion(f32[4,5,2,4,4,1280]{5,4,3,2,1,0:T(4,128)} %bitcast.45, s32[]{:T(128)S(6)} %select_n.133), kind=kLoop, calls=%fused_computation.5 | loop fusion | bytes 3276804 | tf_op jit(solution)/shard_map/jit(dynamic_index_in_dim)/squeeze | solution.py:55
  10.4 2.2 collective-permute-start
  12.5 7.2 %all-to-all-done.1 = f32[4,40,640]{2,1,0:T(8,128)} async-done(((f32[4,40,640]{2,1,0:T(8,128)}), f32[4,40,640]{2,1,0:T(8,128)}, u32[]{:S(2)}, u32[]{:S(2)}) %all-to-all-start.1) | async-done | bytes 409632 | tf_op jit(solution)/shard_map/all_to_all | solution.py:35
  19.8 2.3 broadcast_in_dim.62
  22.1 5.4 %all-to-all-start.2 = ((f32[4,4,40,640]{3,2,1,0:T(8,128)}), f32[4,4,40,640]{3,2,1,0:T(8,128)}, u32[]{:S(2)}, u32[]{:S(2)}) async-start(f32[4,4,40,640]{3,2,1,0:T(8,128)} %broadcast_in_dim.62), calls=%async_computation.2 | async-start | bytes 3276800 | tf_op jit(solution)/shard_map/all_to_all | solution.py:35
  28.3 16.5 %all-to-all-done.2 = f32[4,4,40,640]{3,2,1,0:T(8,128)} async-done(((f32[4,4,40,640]{3,2,1,0:T(8,128)}), f32[4,4,40,640]{3,2,1,0:T(8,128)}, u32[]{:S(2)}, u32[]{:S(2)}) %all-to-all-start.2) | async-done | bytes 1638432 | tf_op jit(solution)/shard_map/all_to_all | solution.py:35
  44.8 1.9 collective-permute-start.4
  46.7 2.3 bitcast_select_fusion
  49.1 3.7 %collective-permute-start.1 = (f32[5,4,4,1280]{3,2,1,0:T(4,128)S(1)}, f32[5,4,4,1280]{3,2,1,0:T(4,128)S(1)}, u32[]{:S(2)}, u32[]{:S(2)}) collective-permute-start(f32[5,4,4,1280]{3,2,1,0:T(4,128)S(1)} %get-tuple-element.21), channel_id=1, source_target_pairs={{0,32},{1,33},{2,34},{3,35},{4,36},{5,37},{6,38},{7,39},{8,40},{9,... | collective-permute-start | bytes 1228808 | tf_op jit(solution)/shard_map/ppermute | solution.py:30
  52.8 4.8 %collective-permute-start.2 = (f32[5,4,4,1280]{3,2,1,0:T(4,128)S(1)}, f32[5,4,4,1280]{3,2,1,0:T(4,128)S(1)}, u32[]{:S(2)}, u32[]{:S(2)}) collective-permute-start(f32[5,4,4,1280]{3,2,1,0:T(4,128)S(1)} %get-tuple-element.20), channel_id=1, source_target_pairs={{0,64},{1,65},{2,66},{3,67},{4,68},{5,69},{6,70},{7,71},{8,72},{9,... | collective-permute-start | bytes 1228808 | tf_op jit(solution)/shard_map/ppermute | solution.py:30
  57.7 3.3 %collective-permute-start.3 = (f32[5,4,4,1280]{3,2,1,0:T(4,128)S(1)}, f32[5,4,4,1280]{3,2,1,0:T(4,128)S(1)}, u32[]{:S(2)}, u32[]{:S(2)}) collective-permute-start(f32[5,4,4,1280]{3,2,1,0:T(4,128)S(1)} %get-tuple-element.19), channel_id=1, source_target_pairs={{0,96},{1,97},{2,98},{3,99},{4,100},{5,101},{6,102},{7,103},{8,104... | collective-permute-start | bytes 1228808 | tf_op jit(solution)/shard_map/ppermute | solution.py:30
  61.5 2.9 %collective-permute-done.1 = f32[5,4,4,1280]{3,2,1,0:T(4,128)S(1)} collective-permute-done((f32[5,4,4,1280]{3,2,1,0:T(4,128)S(1)}, f32[5,4,4,1280]{3,2,1,0:T(4,128)S(1)}, u32[]{:S(2)}, u32[]{:S(2)}) %collective-permute-start.1) | collective-permute-done | bytes 409632 | tf_op jit(solution)/shard_map/ppermute | solution.py:30
  64.4 9.9 %collective-permute-done.2 = f32[5,4,4,1280]{3,2,1,0:T(4,128)S(1)} collective-permute-done((f32[5,4,4,1280]{3,2,1,0:T(4,128)S(1)}, f32[5,4,4,1280]{3,2,1,0:T(4,128)S(1)}, u32[]{:S(2)}, u32[]{:S(2)}) %collective-permute-start.2) | collective-permute-done | bytes 409632 | tf_op jit(solution)/shard_map/ppermute | solution.py:30
  74.3 1.4 collective-permute-done.3
  76.0 0.9 copy.20
  76.8 7.1 %all-to-all-start = ((f32[4,20,1280]{2,1,0:T(8,128)}), f32[4,20,1280]{2,1,0:T(8,128)}, u32[]{:S(2)}, u32[]{:S(2)}) async-start(f32[4,20,1280]{2,1,0:T(8,128)} %copy.20), calls=%async_computation | async-start | bytes 983040 | tf_op jit(solution)/shard_map/all_to_all | solution.py:228
  83.9 3.4 %maximum_select_fusion = f32[2,4,4,40,640]{4,3,0,2,1:T(8,128)S(1)} fusion(f32[1,4,4,40,640]{4,3,0,2,1:T(8,128)} %bitcast.13, f32[1,4,4,40,640]{4,3,0,2,1:T(8,128)} %bitcast.12, pred[]{:T(512)S(6)} %eq.45), kind=kLoop, calls=%fused_computation | loop fusion | flops 2457600 | bytes 6553601 | tf_op jit(solution)/shard_map/jit(_where)/select_n | solution.py:47
  87.8 5.6 %multiply_bitcast_fusion = f32[4,160,640]{2,1,0:T(8,128)} fusion(f32[1280,640,1]{1,0,2:T(8,128)S(1)} %bitcast.43, f32[160,4,1280]{2,1,0:T(4,128)S(1)} %copy-done.2, f32[160]{0:T(256)S(1)} %compare_convert_fusion.1), kind=kOutput, calls=%fused_computation.4 | convolution fusion | flops 3146137600 | bytes 8192640 | tf_op jit(solution)/shard_map/pim,ma->ipa/dot_general | solution.py:239
  93.3 4.8 %all-to-all-start.4 = ((f32[4,160,640]{2,1,0:T(8,128)}), f32[4,160,640]{2,1,0:T(8,128)}, u32[]{:S(2)}, u32[]{:S(2)}) async-start(f32[4,160,640]{2,1,0:T(8,128)} %multiply_bitcast_fusion), calls=%async_computation.4 | async-start | bytes 3276800 | tf_op jit(solution)/shard_map/all_to_all | solution.py:246
  98.4 1.8 reshape.91
  100.2 2.3 convolution_multiply_fusion
  102.5 9.1 %collective-permute-start.5 = (f32[80,640]{1,0:T(8,128)S(1)}, f32[80,640]{1,0:T(8,128)S(1)}, u32[]{:S(2)}, u32[]{:S(2)}) collective-permute-start(f32[80,640]{1,0:T(8,128)S(1)} %convolution_multiply_fusion), channel_id=1, source_target_pairs={{0,128},{1,129},{2,130},{3,131},{4,132},{5,133},{6,134},{7,135},{8... | collective-permute-start | bytes 614408 | tf_op jit(solution)/shard_map/ppermute | solution.py:30
  111.6 4.0 %collective-permute-start.7 = (f32[80,640]{1,0:T(8,128)S(1)}, f32[80,640]{1,0:T(8,128)S(1)}, u32[]{:S(2)}, u32[]{:S(2)}) collective-permute-start(f32[80,640]{1,0:T(8,128)S(1)} %convolution_multiply_fusion), channel_id=1, source_target_pairs={{0,384},{1,385},{2,386},{3,387},{4,388},{5,389},{6,390},{7,391},{8... | collective-permute-start | bytes 614408 | tf_op jit(solution)/shard_map/ppermute | solution.py:30
  115.7 15.7 %collective-permute-done.5 = f32[80,640]{1,0:T(8,128)S(1)} collective-permute-done((f32[80,640]{1,0:T(8,128)S(1)}, f32[80,640]{1,0:T(8,128)S(1)}, u32[]{:S(2)}, u32[]{:S(2)}) %collective-permute-start.5) | collective-permute-done | bytes 204832 | tf_op jit(solution)/shard_map/ppermute | solution.py:30
  131.4 4.2 %collective-permute-start.6 = (f32[40,640]{1,0:T(8,128)S(1)}, f32[40,640]{1,0:T(8,128)S(1)}, u32[]{:S(2)}, u32[]{:S(2)}) collective-permute-start(f32[40,640]{1,0:T(8,128)S(1)} %slice.8), channel_id=1, source_target_pairs={{0,128},{1,129},{2,130},{3,131},{4,132},{5,133},{6,134},{7,135},{8... | collective-permute-start | bytes 307208 | tf_op jit(solution)/shard_map/ppermute | solution.py:30
  135.6 5.6 %collective-permute-start.8 = (f32[40,640]{1,0:T(8,128)S(1)}, f32[40,640]{1,0:T(8,128)S(1)}, u32[]{:S(2)}, u32[]{:S(2)}) collective-permute-start(f32[40,640]{1,0:T(8,128)S(1)} %slice.9), channel_id=1, source_target_pairs={{0,384},{1,385},{2,386},{3,387},{4,388},{5,389},{6,390},{7,391},{8... | collective-permute-start | bytes 307208 | tf_op jit(solution)/shard_map/ppermute | solution.py:30
  144.5 4.1 %collective-permute-done.8 = f32[40,640]{1,0:T(8,128)S(1)} collective-permute-done((f32[40,640]{1,0:T(8,128)S(1)}, f32[40,640]{1,0:T(8,128)S(1)}, u32[]{:S(2)}, u32[]{:S(2)}) %collective-permute-start.8) | collective-permute-done | bytes 102432 | tf_op jit(solution)/shard_map/ppermute | solution.py:30
  148.5 1.0 fusion.7
  149.6 23.7 %all_to_all.35.refs_0_ = f32[4,80,640]{2,1,0:T(8,128)S(1)} all-to-all(f32[4,80,640]{2,1,0:T(8,128)S(1)} %broadcast_in_dim.63), channel_id=1, replica_groups=mesh['zh'=4,'y'=4,'c'=2,'x'=4,'zl'=4] {'zl'}, dimensions={0} | all-to-all | bytes 1638400 | tf_op jit(solution)/shard_map/all_to_all | solution.py:35
  173.3 3.0 %copy.22 = f32[640,640]{0,1:T(8,128)} copy(f32[640,640]{1,0:T(8,128)} %bitcast.20) | data formatting | bytes 3276800 | tf_op jit(solution)/shard_map/optimization_barrier | solution.py:251
  176.3 3.6 %all-to-all-start.5 = ((f32[4,160,640]{2,1,0:T(8,128)}), f32[4,160,640]{2,1,0:T(8,128)S(1)}, u32[]{:S(2)}, u32[]{:S(2)}) async-start(f32[4,160,640]{2,1,0:T(8,128)} %bitcast.22), calls=%async_computation.5 | async-start | bytes 3276800 | tf_op jit(solution)/shard_map/all_to_all | solution.py:256
  179.9 5.1 %collective-permute-start.9 = (f32[4,80,640]{2,1,0:T(8,128)S(1)}, f32[4,80,640]{2,1,0:T(8,128)S(1)}, u32[]{:S(2)}, u32[]{:S(2)}) collective-permute-start(f32[4,80,640]{2,1,0:T(8,128)S(1)} %all_to_all.35.refs_0_), channel_id=1, source_target_pairs={{0,96},{1,97},{2,98},{3,99},{4,100},{5,101},{6,102},{7,103},{8,104... | collective-permute-start | bytes 2457608 | tf_op jit(solution)/shard_map/ppermute | solution.py:30
  184.9 3.8 %collective-permute-start.10 = (f32[4,80,640]{2,1,0:T(8,128)S(1)}, f32[4,80,640]{2,1,0:T(8,128)S(1)}, u32[]{:S(2)}, u32[]{:S(2)}) collective-permute-start(f32[4,80,640]{2,1,0:T(8,128)S(1)} %all_to_all.35.refs_0_), channel_id=1, source_target_pairs={{0,64},{1,65},{2,66},{3,67},{4,68},{5,69},{6,70},{7,71},{8,72},{9,... | collective-permute-start | bytes 2457608 | tf_op jit(solution)/shard_map/ppermute | solution.py:30
  188.7 1.9 collective-permute-start.11
  190.7 1.9 collective-permute-start.12
  192.6 26.1 %collective-permute-done.9.refs_1_ = f32[4,80,640]{2,1,0:T(8,128)S(1)} collective-permute-done((f32[4,80,640]{2,1,0:T(8,128)S(1)}, f32[4,80,640]{2,1,0:T(8,128)S(1)}, u32[]{:S(2)}, u32[]{:S(2)}) %collective-permute-start.9) | collective-permute-done | bytes 819232 | tf_op jit(solution)/shard_map/ppermute | solution.py:30
  218.7 1.9 collective-permute-start.13
  220.7 2.4 collective-permute-start.14
  223.1 1.2 collective-permute-done.11.refs_3_
  224.3 2.1 collective-permute-start.15
  227.7 0.9 copy-done.10
  228.7 1.2 copy-done.3
  229.8 9.2 %pair_kernel.1 = (f32[160,640]{1,0:T(8,128)S(1)}, f32[4,200,128]{2,1,0:T(8,128)}, bf16[4,4,160,640]{3,2,1,0:T(8,128)(2,1)}, bf16[4,4,160,640]{3,2,1,0:T(8,128)(2,1)}) custom-call(s32[2]{0:T(128)S(1)} %pad_add_fusion.place_ref, f32[4,80,640]{2,1,0:T(8,128)} %copy-done.4, f32[4,80,640]{2,1,0:T(8,128)} %copy-done.5, f32[4,80,640]{2,1,0:T(8,128)} %copy-done.6, ...), custom_call_target="tpu_custom_call" | custom-call | flops 1572864000 | bytes 16777216 | tf_op jit(solution)/shard_map/pair_kernel/pallas_call | solution.py:134
  239.0 4.8 %all-to-all-start.6 = ((f32[4,200,128]{2,1,0:T(8,128)}), f32[4,200,128]{2,1,0:T(8,128)S(1)}, u32[]{:S(2)}, u32[]{:S(2)}) async-start(f32[4,200,128]{2,1,0:T(8,128)} %get-tuple-element.14), calls=%async_computation.6 | async-start | bytes 819200 | tf_op jit(solution)/shard_map/all_to_all | solution.py:259
  246.5 9.9 %all-to-all-done.6.came_ref = f32[4,200,128]{2,1,0:T(8,128)S(1)} async-done(((f32[4,200,128]{2,1,0:T(8,128)}), f32[4,200,128]{2,1,0:T(8,128)S(1)}, u32[]{:S(2)}, u32[]{:S(2)}) %all-to-all-start.6) | async-done | bytes 409632 | tf_op jit(solution)/shard_map/all_to_all | solution.py:259
  256.4 7.1 %density_kernel.1 = f32[160,2560]{1,0:T(8,128)} custom-call(f32[160,640]{1,0:T(8,128)S(1)} %get-tuple-element.13.pair_ref, f32[4,200,128]{2,1,0:T(8,128)S(1)} %all-to-all-done.6.came_ref, f32[160,1]{1,0:T(8,128)S(1)} %copy.23.row_ref, f32[1,640]{1,0:T(1,128)S(1)} %broadcast_in_dim.65.column_ref, bf16[4,4,160,640]{3,2,1,0:T(8,128)(2,1)} %get-tuple-element.15.high_ref, ...), custom_call_target="tpu_custom_call" | custom-call | flops 1572864000 | bytes 10485760 | tf_op jit(solution)/shard_map/density_kernel/pallas_call | solution.py:190
  (64 shorter events, 6.2 us)
Async XLA Ops:
  0.0 0.9 copy-start
  1.7 18.0 %all-to-all-start.1 = ((f32[4,40,640]{2,1,0:T(8,128)}), f32[4,40,640]{2,1,0:T(8,128)}, u32[]{:S(2)}, u32[]{:S(2)}) async-start(f32[4,40,640]{2,1,0:T(8,128)} %broadcast_in_dim.61), calls=%async_computation.1 | async-start | bytes 819200 | tf_op jit(solution)/shard_map/all_to_all | solution.py:35
  10.3 17.1 %copy-start.14 = (s32[16]{0:T(128)S(1)}, s32[16]{0:T(128)}, u32[]{:S(2)}) copy-start(s32[16]{0:T(128)} %param.10) | copy-start | bytes 196
  10.4 18.0 %copy-start.15 = (s32[4]{0:T(128)S(1)}, s32[4]{0:T(128)}, u32[]{:S(2)}) copy-start(s32[4]{0:T(128)} %param.11) | copy-start | bytes 52
  10.4 36.4 %copy-start.1 = (f32[160,4,1280]{2,1,0:T(4,128)S(1)}, f32[160,4,1280]{2,1,0:T(4,128)}, u32[]{:S(2)}) copy-start(f32[160,4,1280]{2,1,0:T(4,128)} %param.6) | copy-start | bytes 9830404
  10.4 36.4 %collective-permute-start = (f32[4,5,4,4,1280]{4,3,2,1,0:T(4,128)}, f32[4,5,4,4,1280]{4,3,2,1,0:T(4,128)}, u32[]{:S(2)}, u32[]{:S(2)}) collective-permute-start(f32[4,5,4,4,1280]{4,3,2,1,0:T(4,128)} %dynamic-slice_bitcast_fusion), channel_id=1, source_target_pairs={{0,16},{1,17},{2,18},{3,19},{4,20},{5,21},{6,22},{7,23},{8,24},{9,... | collective-permute-start | bytes 4915208 | tf_op jit(solution)/shard_map/ppermute | solution.py:30
  22.1 22.7 %all-to-all-start.2 = ((f32[4,4,40,640]{3,2,1,0:T(8,128)}), f32[4,4,40,640]{3,2,1,0:T(8,128)}, u32[]{:S(2)}, u32[]{:S(2)}) async-start(f32[4,4,40,640]{3,2,1,0:T(8,128)} %broadcast_in_dim.62), calls=%async_computation.2 | async-start | bytes 3276800 | tf_op jit(solution)/shard_map/all_to_all | solution.py:35
  44.8 39.1 %collective-permute-start.4 = (f32[4,4,40,640]{3,2,1,0:T(8,128)}, f32[4,4,40,640]{3,2,1,0:T(8,128)}, u32[]{:S(2)}, u32[]{:S(2)}) collective-permute-start(f32[4,4,40,640]{3,2,1,0:T(8,128)} %all-to-all-done.2), channel_id=1, source_target_pairs={{0,16},{1,17},{2,18},{3,19},{4,20},{5,21},{6,22},{7,23},{8,24},{9,... | collective-permute-start | bytes 4915208 | tf_op jit(solution)/shard_map/ppermute | solution.py:30
  49.1 15.3 %collective-permute-start.1 = (f32[5,4,4,1280]{3,2,1,0:T(4,128)S(1)}, f32[5,4,4,1280]{3,2,1,0:T(4,128)S(1)}, u32[]{:S(2)}, u32[]{:S(2)}) collective-permute-start(f32[5,4,4,1280]{3,2,1,0:T(4,128)S(1)} %get-tuple-element.21), channel_id=1, source_target_pairs={{0,32},{1,33},{2,34},{3,35},{4,36},{5,37},{6,38},{7,39},{8,40},{9,... | collective-permute-start | bytes 1228808 | tf_op jit(solution)/shard_map/ppermute | solution.py:30
  52.8 21.5 %collective-permute-start.2 = (f32[5,4,4,1280]{3,2,1,0:T(4,128)S(1)}, f32[5,4,4,1280]{3,2,1,0:T(4,128)S(1)}, u32[]{:S(2)}, u32[]{:S(2)}) collective-permute-start(f32[5,4,4,1280]{3,2,1,0:T(4,128)S(1)} %get-tuple-element.20), channel_id=1, source_target_pairs={{0,64},{1,65},{2,66},{3,67},{4,68},{5,69},{6,70},{7,71},{8,72},{9,... | collective-permute-start | bytes 1228808 | tf_op jit(solution)/shard_map/ppermute | solution.py:30
  57.7 18.1 %collective-permute-start.3 = (f32[5,4,4,1280]{3,2,1,0:T(4,128)S(1)}, f32[5,4,4,1280]{3,2,1,0:T(4,128)S(1)}, u32[]{:S(2)}, u32[]{:S(2)}) collective-permute-start(f32[5,4,4,1280]{3,2,1,0:T(4,128)S(1)} %get-tuple-element.19), channel_id=1, source_target_pairs={{0,96},{1,97},{2,98},{3,99},{4,100},{5,101},{6,102},{7,103},{8,104... | collective-permute-start | bytes 1228808 | tf_op jit(solution)/shard_map/ppermute | solution.py:30
  76.8 16.5 %all-to-all-start = ((f32[4,20,1280]{2,1,0:T(8,128)}), f32[4,20,1280]{2,1,0:T(8,128)}, u32[]{:S(2)}, u32[]{:S(2)}) async-start(f32[4,20,1280]{2,1,0:T(8,128)} %copy.20), calls=%async_computation | async-start | bytes 983040 | tf_op jit(solution)/shard_map/all_to_all | solution.py:228
  83.9 3.9 %copy-start.2 = (f32[160,4,1280]{2,1,0:T(4,128)S(1)}, f32[160,4,1280]{2,1,0:T(4,128)}, u32[]{:S(2)}) copy-start(f32[160,4,1280]{2,1,0:T(4,128)} %param.6) | copy-start | bytes 9830404
  93.3 56.2 %all-to-all-start.4 = ((f32[4,160,640]{2,1,0:T(8,128)}), f32[4,160,640]{2,1,0:T(8,128)}, u32[]{:S(2)}, u32[]{:S(2)}) async-start(f32[4,160,640]{2,1,0:T(8,128)} %multiply_bitcast_fusion), calls=%async_computation.4 | async-start | bytes 3276800 | tf_op jit(solution)/shard_map/all_to_all | solution.py:246
  102.5 9.1 %copy-start.11 = (f32[80,640]{1,0:T(8,128)}, f32[80,640]{1,0:T(8,128)S(1)}, u32[]{:S(2)}) copy-start(f32[80,640]{1,0:T(8,128)S(1)} %convolution_multiply_fusion) | copy-start | bytes 614404
  102.5 28.9 %collective-permute-start.5 = (f32[80,640]{1,0:T(8,128)S(1)}, f32[80,640]{1,0:T(8,128)S(1)}, u32[]{:S(2)}, u32[]{:S(2)}) collective-permute-start(f32[80,640]{1,0:T(8,128)S(1)} %convolution_multiply_fusion), channel_id=1, source_target_pairs={{0,128},{1,129},{2,130},{3,131},{4,132},{5,133},{6,134},{7,135},{8... | collective-permute-start | bytes 614408 | tf_op jit(solution)/shard_map/ppermute | solution.py:30
  111.6 23.9 %collective-permute-start.7 = (f32[80,640]{1,0:T(8,128)S(1)}, f32[80,640]{1,0:T(8,128)S(1)}, u32[]{:S(2)}, u32[]{:S(2)}) collective-permute-start(f32[80,640]{1,0:T(8,128)S(1)} %convolution_multiply_fusion), channel_id=1, source_target_pairs={{0,384},{1,385},{2,386},{3,387},{4,388},{5,389},{6,390},{7,391},{8... | collective-permute-start | bytes 614408 | tf_op jit(solution)/shard_map/ppermute | solution.py:30
  131.4 13.0 %collective-permute-start.6 = (f32[40,640]{1,0:T(8,128)S(1)}, f32[40,640]{1,0:T(8,128)S(1)}, u32[]{:S(2)}, u32[]{:S(2)}) collective-permute-start(f32[40,640]{1,0:T(8,128)S(1)} %slice.8), channel_id=1, source_target_pairs={{0,128},{1,129},{2,130},{3,131},{4,132},{5,133},{6,134},{7,135},{8... | collective-permute-start | bytes 307208 | tf_op jit(solution)/shard_map/ppermute | solution.py:30
  135.6 12.9 %collective-permute-start.8 = (f32[40,640]{1,0:T(8,128)S(1)}, f32[40,640]{1,0:T(8,128)S(1)}, u32[]{:S(2)}, u32[]{:S(2)}) collective-permute-start(f32[40,640]{1,0:T(8,128)S(1)} %slice.9), channel_id=1, source_target_pairs={{0,384},{1,385},{2,386},{3,387},{4,388},{5,389},{6,390},{7,391},{8... | collective-permute-start | bytes 307208 | tf_op jit(solution)/shard_map/ppermute | solution.py:30
  173.3 17.4 %copy-start.4 = (f32[4,80,640]{2,1,0:T(8,128)}, f32[4,80,640]{2,1,0:T(8,128)S(1)}, u32[]{:S(2)}) copy-start(f32[4,80,640]{2,1,0:T(8,128)S(1)} %all_to_all.35.refs_0_) | copy-start | bytes 2457604
  176.3 52.4 %all-to-all-start.5 = ((f32[4,160,640]{2,1,0:T(8,128)}), f32[4,160,640]{2,1,0:T(8,128)S(1)}, u32[]{:S(2)}, u32[]{:S(2)}) async-start(f32[4,160,640]{2,1,0:T(8,128)} %bitcast.22), calls=%async_computation.5 | async-start | bytes 3276800 | tf_op jit(solution)/shard_map/all_to_all | solution.py:256
  179.9 38.9 %collective-permute-start.9 = (f32[4,80,640]{2,1,0:T(8,128)S(1)}, f32[4,80,640]{2,1,0:T(8,128)S(1)}, u32[]{:S(2)}, u32[]{:S(2)}) collective-permute-start(f32[4,80,640]{2,1,0:T(8,128)S(1)} %all_to_all.35.refs_0_), channel_id=1, source_target_pairs={{0,96},{1,97},{2,98},{3,99},{4,100},{5,101},{6,102},{7,103},{8,104... | collective-permute-start | bytes 2457608 | tf_op jit(solution)/shard_map/ppermute | solution.py:30
  184.9 35.7 %collective-permute-start.10 = (f32[4,80,640]{2,1,0:T(8,128)S(1)}, f32[4,80,640]{2,1,0:T(8,128)S(1)}, u32[]{:S(2)}, u32[]{:S(2)}) collective-permute-start(f32[4,80,640]{2,1,0:T(8,128)S(1)} %all_to_all.35.refs_0_), channel_id=1, source_target_pairs={{0,64},{1,65},{2,66},{3,67},{4,68},{5,69},{6,70},{7,71},{8,72},{9,... | collective-permute-start | bytes 2457608 | tf_op jit(solution)/shard_map/ppermute | solution.py:30
  188.7 35.6 %collective-permute-start.11 = (f32[4,80,640]{2,1,0:T(8,128)S(1)}, f32[4,80,640]{2,1,0:T(8,128)S(1)}, u32[]{:S(2)}, u32[]{:S(2)}) collective-permute-start(f32[4,80,640]{2,1,0:T(8,128)S(1)} %all_to_all.35.refs_0_), channel_id=1, source_target_pairs={{0,32},{1,33},{2,34},{3,35},{4,36},{5,37},{6,38},{7,39},{8,40},{9,... | collective-permute-start | bytes 2457608 | tf_op jit(solution)/shard_map/ppermute | solution.py:30
  190.7 35.8 %collective-permute-start.12 = (f32[4,80,640]{2,1,0:T(8,128)S(1)}, f32[4,80,640]{2,1,0:T(8,128)S(1)}, u32[]{:S(2)}, u32[]{:S(2)}) collective-permute-start(f32[4,80,640]{2,1,0:T(8,128)S(1)} %all_to_all.35.refs_0_), channel_id=1, source_target_pairs={{0,16},{1,17},{2,18},{3,19},{4,20},{5,21},{6,22},{7,23},{8,24},{9,... | collective-permute-start | bytes 2457608 | tf_op jit(solution)/shard_map/ppermute | solution.py:30
  218.7 9.9 %copy-start.5 = (f32[4,80,640]{2,1,0:T(8,128)}, f32[4,80,640]{2,1,0:T(8,128)S(1)}, u32[]{:S(2)}) copy-start(f32[4,80,640]{2,1,0:T(8,128)S(1)} %collective-permute-done.9.refs_1_) | copy-start | bytes 2457604
  218.7 7.8 %collective-permute-start.13 = (f32[4,80,640]{2,1,0:T(8,128)S(1)}, f32[4,80,640]{2,1,0:T(8,128)S(1)}, u32[]{:S(2)}, u32[]{:S(2)}) collective-permute-start(f32[4,80,640]{2,1,0:T(8,128)S(1)} %collective-permute-done.9.refs_1_), channel_id=1, source_target_pairs={{0,16},{1,17},{2,18},{3,19},{4,20},{5,21},{6,22},{7,23},{8,24},{9,... | collective-permute-start | bytes 2457608 | tf_op jit(solution)/shard_map/ppermute | solution.py:30
  220.7 5.9 %copy-start.6 = (f32[4,80,640]{2,1,0:T(8,128)}, f32[4,80,640]{2,1,0:T(8,128)S(1)}, u32[]{:S(2)}) copy-start(f32[4,80,640]{2,1,0:T(8,128)S(1)} %collective-permute-done.10.refs_2_) | copy-start | bytes 2457604
  220.7 5.9 %collective-permute-start.14 = (f32[4,80,640]{2,1,0:T(8,128)S(1)}, f32[4,80,640]{2,1,0:T(8,128)S(1)}, u32[]{:S(2)}, u32[]{:S(2)}) collective-permute-start(f32[4,80,640]{2,1,0:T(8,128)S(1)} %collective-permute-done.10.refs_2_), channel_id=1, source_target_pairs={{0,16},{1,17},{2,18},{3,19},{4,20},{5,21},{6,22},{7,23},{8,24},{9,... | collective-permute-start | bytes 2457608 | tf_op jit(solution)/shard_map/ppermute | solution.py:30
  224.3 2.2 copy-start.7
  224.3 4.3 %collective-permute-start.15 = (f32[4,80,640]{2,1,0:T(8,128)S(1)}, f32[4,80,640]{2,1,0:T(8,128)}, u32[]{:S(2)}, u32[]{:S(2)}) collective-permute-start(f32[4,80,640]{2,1,0:T(8,128)S(1)} %collective-permute-done.11.refs_3_), channel_id=1, source_target_pairs={{0,16},{1,17},{2,18},{3,19},{4,20},{5,21},{6,22},{7,23},{8,24},{9,... | collective-permute-start | bytes 2457608 | tf_op jit(solution)/shard_map/ppermute | solution.py:30
  226.5 17.9 %copy-start.12 = (f32[640]{0:T(1024)S(1)}, f32[640]{0:T(1024)}, u32[]{:S(2)}) copy-start(f32[640]{0:T(1024)} %param.9) | copy-start | bytes 7684
  226.5 18.0 %copy-start.13 = (f32[128]{0:T(128)S(1)}, f32[128]{0:T(128)}, u32[]{:S(2)}) copy-start(f32[128]{0:T(128)} %param.8) | copy-start | bytes 1540
  226.5 0.9 copy-start.8
  226.5 1.2 copy-start.9
  227.7 0.9 copy-start.10
  228.7 1.2 copy-start.3
  239.0 17.4 %all-to-all-start.6 = ((f32[4,200,128]{2,1,0:T(8,128)}), f32[4,200,128]{2,1,0:T(8,128)S(1)}, u32[]{:S(2)}, u32[]{:S(2)}) async-start(f32[4,200,128]{2,1,0:T(8,128)} %get-tuple-element.14), calls=%async_computation.6 | async-start | bytes 819200 | tf_op jit(solution)/shard_map/all_to_all | solution.py:259

commit v2 on v1

--- a/solution.py
+++ b/solution.py
@@ -40,7 +40,11 @@
 
 
 def ring_y(block):
-    return [block, moved(block, dy=-1), moved(block, dy=2), moved(block, dy=1)]
+    half = block.shape[0] // 2
+    ahead, behind = moved(block, dy=-1), moved(block, dy=1)
+    low = moved(behind[:half], dy=1)
+    high = moved(ahead[half:], dy=-1)
+    return [block, ahead, behind, low, high]
 
 
 def both_cores(block, other, core):
@@ -56,13 +60,15 @@
     return jnp.where((pair_root % CORE)[:, None] == c, mine, other)
 
 
-def own_y_part(part, pair_root, y):
-    distance = ((pair_root // CORE - y) % Y)[:, None]
-    chosen = pick(part, y)
-    for hop in range(1, Y):
-        came = moved(pick(part, (y - hop) % Y), dy=-hop)
+def own_part(part, root, here, axis):
+    count = part.shape[0]
+    distance = ((root - here) % count)[:, None]
+    pieces = [pick(part, (here - hop) % count) for hop in range(count)]
+    chosen = pieces[0]
+    for hop in range(1, count):
+        came = moved(pieces[hop], **{f"d{axis}": -hop})
         chosen = jnp.where(distance == hop, came, chosen)
-    return chosen.reshape(-1, *chosen.shape[2:]).transpose(1, 0, 2)
+    return chosen
 
 
 def split_float(value):
@@ -78,17 +84,26 @@
 
 
 def pair_kernel(place_ref, *refs):
-    near, far, held_ref = refs[:Y], refs[Y : 2 * Y], refs[2 * Y]
-    pair_ref, sent_ref, high_ref, low_ref, rows_ref = refs[2 * Y + 1 :]
+    near, far, held_ref = refs[:5], refs[5:10], refs[10]
+    pair_ref, sent_ref, high_ref, low_ref, rows_ref = refs[11:]
+    early = pl.program_id(0) < ZLO // 2
     y, c = place_ref[0], place_ref[1]
     part_rows, vir_count = near[0].shape[1:]
     tiles = part_rows // 8
     band = 2 * part_rows // X
     lower = lax.broadcasted_iota(jnp.int32, (tiles, 8, vir_count), 1) < 4
     first = c == 0
+
+    def taken(parts, hop):
+        if hop == 2:
+            rows = jnp.where(early, parts[3][0], parts[4][0])
+        else:
+            rows = parts[(0, 1, 2, 2)[hop]][0]
+        return rows.reshape(tiles, 8, vir_count)
+
     for hop in range(Y):
-        mine = near[hop][0].reshape(tiles, 8, vir_count)
-        other = far[hop][0].reshape(tiles, 8, vir_count)
+        mine = taken(near, hop)
+        other = taken(far, hop)
         zero = jnp.where(first, mine, other)
         one = jnp.where(first, other, mine)
         even = jnp.where(lower, zero, pltpu.roll(one, 4, 1))
@@ -130,7 +145,9 @@
     packed = (ZLO, width_dev * width_dev // LANES, LANES)
     part = pl.BlockSpec((1, part_rows, vir_count), lambda z: (z, 0, 0))
     wide = pl.BlockSpec((X, 1, rows_dev, vir_count), lambda z: (0, z, 0, 0))
-    operands = [pltpu.with_memory_space_constraint(v, pltpu.HBM) for v in (*near, *far, held)]
+    early = pl.BlockSpec((1, part_rows, vir_count), lambda z: (jnp.minimum(z, ZLO // 2 - 1), 0, 0))
+    late = pl.BlockSpec((1, part_rows, vir_count), lambda z: (jnp.maximum(z - ZLO // 2, 0), 0, 0))
+    operands = [pltpu.with_memory_space_constraint(v, pltpu.HBM) for v in (*near, *far)]
     return pl.pallas_call(
         pair_kernel,
         grid=(ZLO,),
@@ -141,7 +158,7 @@
             pltpu.HBM((X, ZLO, rows_dev, vir_count), jnp.bfloat16),
         ),
         in_specs=[pl.BlockSpec(memory_space=pltpu.SMEM)]
-        + [part] * (2 * Y)
+        + [part, part, part, early, late] * 2
         + [pl.BlockSpec((1, width_dev, lanes), lambda z: (z, 0, 0))],
         out_specs=(
             pl.BlockSpec((width_dev, vir_count), lambda z: (0, 0)),
@@ -155,7 +172,7 @@
             flops=6 * width_dev * X * ZLO * rows_dev * vir_count, bytes_accessed=16 << 20, transcendentals=0
         ),
         name="pair_kernel",
-    )(jnp.stack([y, c]).astype(jnp.int32), *operands)
+    )(jnp.stack([y, c]).astype(jnp.int32), *operands, held)
 
 
 def density_kernel(pair_ref, came_ref, row_ref, column_ref, high_ref, low_ref, gamma_ref, cols_ref, amp_ref):
@@ -223,30 +240,32 @@
     coeff_rows = virt_coeff.shape[0] // CORE
     coeff = gathered(lax.dynamic_slice_in_dim(virt_coeff, c * coeff_rows, coeff_rows, 0), "zl")
     raw = own_core_part(half_ints, pair_root, c)
-    raw = own_y_part(raw, pair_root, y)
+    raw = own_part(raw, pair_root // CORE % Y, y, "y")
+    raw = raw.reshape(ZHI, step, occ_grp, basis_count)
+    raw = own_part(raw, pair_root // (Y * CORE), zh, "zh").transpose(1, 0, 2)
     coeff = gathered(coeff, "x")
-    raw = lax.all_to_all(raw, "x", 0, 0).reshape(X * step * 4, basis_count)
-    coeff = both_cores(coeff, moved(coeff, dc=1), c)
+    raw = lax.all_to_all(raw, "x", 0, 0).reshape(X * step, basis_count)
+    other = moved(coeff, dc=1)
+    coeff = both_cores(coeff, other, c)
     coeff = coeff.transpose(1, 2, 0, 3, 4).reshape(basis_count, vir_count)
 
     part = jnp.dot(raw, coeff, precision=FAST, preferred_element_type=jnp.float32)
     sizes = lax.dynamic_index_in_dim(aux_sizes.reshape(X, ZLO), zl, 1)[:, :, None]
-    place = y * (rows_dev // Y) + lax.iota(jnp.int32, step)[:, None] * 8 + c * 4 + lax.iota(jnp.int32, 4)[None, :]
-    part = part * (place < sizes).astype(jnp.float32).reshape(-1, 1)
-
+    row = zh * step + lax.iota(jnp.int32, step)[None, :, None]
+    place = y * (rows_dev // Y) + row // 4 * 8 + c * 4 + row % 4
+    part = part.reshape(X, step, vir_count) * (place < sizes).astype(jnp.float32)
     own_size = pick(aux_sizes, x * ZLO + zl)
     live_rows = (lax.iota(jnp.int32, rows_dev) < own_size).astype(jnp.float32)
     transformed = jnp.einsum("pim,ma->ipa", half_ints, coeff, precision=FAST, preferred_element_type=jnp.float32)
     transformed = transformed * live_rows[None, :, None]
 
-    half = part.shape[0] // 2
-    up = moved(part, dzh=1)
-    down = moved(part, dzh=-1)
-    low, high = moved(up[:half], dzh=1), moved(down[half:], dzh=-1)
+    part = part.reshape(X * step, vir_count)
+    ring = [part]
+    for hop in range(1, ZHI):
+        ring.append(moved(part, dzh=-hop))
+    part = lax.dynamic_slice_in_dim(jnp.stack(ring * 2), (ZHI - zh) % ZHI, ZHI, 0)
+    part = part.reshape(ZHI, X, step, vir_count).transpose(1, 0, 2, 3).reshape(X * ZHI * step, vir_count)
     orbital_rows = lax.all_to_all(transformed, "x", 0, 0).reshape(X * rows_dev, vir_count)
-    distance = (zh - root // (Y * CORE)) % ZHI
-    across = jnp.concatenate([low, high], 0)
-    part = jnp.where(distance == 0, part, jnp.where(distance == 1, up, jnp.where(distance == 2, across, down)))
     near = gathered(part, "zl")
     near, orbital_rows = lax.optimization_barrier((near, orbital_rows))
     near = ring_y(near)

time: 265 us -> 278 us (1.049)
  the two profiles are of different devices: /device:TPU:4 before, /device:TPU:1 now
where the time goes in v2:
time: 278 us; the launch traced here: 276 us
  starting transfers between devices  110 us (40%)
  waiting for transfers between devices  78.2 us (28%)
  blocking collectives  28.5 us (10%)
  local copies, waits for them, and re-layouts  21.7 us (8%)
  Pallas kernels  16.1 us (6%)
  matrix products  10.2 us (4%)
  other arithmetic  9.06 us (3%)
    ppermute x20, starting transfers between devices, moved(): return lax.ppermute(block, AXES, route(**delta))  85.1 us
    ppermute x20, waiting for transfers between devices, moved(): return lax.ppermute(block, AXES, route(**delta))  35.9 us
    all_to_all x1, blocking collectives, gathered(): lax.all_to_all(jnp.broadcast_to(block[None], (count,) + block.shape), axi...  28.5 us
    all_to_all x2, waiting for transfers between devices, gathered(): lax.all_to_all(jnp.broadcast_to(block[None], (count,) + block.shape), axi...  19.7 us
    all_to_all x1, waiting for transfers between devices, shards(): lax.all_to_all(transformed, 'x', 0, 0).reshape(X * rows_dev, vir_count)  13.8 us
    pallas_call x1, Pallas kernels, pair_with_partner(): pl.pallas_call(pair_kernel, grid=(ZLO,), out_shape=(jax.ShapeDtypeStruct(...  9.03 us
    all_to_all x2, starting transfers between devices, gathered(): lax.all_to_all(jnp.broadcast_to(block[None], (count,) + block.shape), axi...  8.62 us
    all_to_all x1, waiting for transfers between devices, shards(): came = lax.all_to_all(sent, 'zl', 0, 0)  8.35 us
  transfers between devices with their start and end apart: 26, of which 11 were waited for; matrix products, arithmetic and copies ran while one was open for 10% of the time, Pallas kernels for 0%

profile of v2, /device:TPU:1, one launch (start us, length us, event | category | flops | bytes accessed | tf_op | source)
XLA Modules:
  0.0 275.9 jit_solution(14976699253205615829)
XLA Ops:
  0.0 2.8 dynamic-slice_bitcast_fusion
  2.8 8.7 %collective-permute-start = (f32[4,5,4,4,1280]{4,3,2,1,0:T(4,128)}, f32[4,5,4,4,1280]{4,3,2,1,0:T(4,128)}, u32[]{:S(2)}, u32[]{:S(2)}) collective-permute-start(f32[4,5,4,4,1280]{4,3,2,1,0:T(4,128)} %dynamic-slice_bitcast_fusion), channel_id=1, source_target_pairs={{0,16},{1,17},{2,18},{3,19},{4,20},{5,21},{6,22},{7,23},{8,24},{9,... | collective-permute-start | bytes 4915208 | tf_op jit(solution)/shard_map/ppermute | solution.py:30
  12.3 4.2 %all-to-all-start.1 = ((f32[4,40,640]{2,1,0:T(8,128)}), f32[4,40,640]{2,1,0:T(8,128)}, u32[]{:S(2)}, u32[]{:S(2)}) async-start(f32[4,40,640]{2,1,0:T(8,128)} %broadcast_in_dim.82), calls=%async_computation.1 | async-start | bytes 819200 | tf_op jit(solution)/shard_map/all_to_all | solution.py:35
  16.7 12.1 %all-to-all-done.1 = f32[4,40,640]{2,1,0:T(8,128)} async-done(((f32[4,40,640]{2,1,0:T(8,128)}), f32[4,40,640]{2,1,0:T(8,128)}, u32[]{:S(2)}, u32[]{:S(2)}) %all-to-all-start.1) | async-done | bytes 409632 | tf_op jit(solution)/shard_map/all_to_all | solution.py:35
  28.8 2.3 broadcast_in_dim.83
  31.1 4.4 %all-to-all-start.2 = ((f32[4,4,40,640]{3,2,1,0:T(8,128)}), f32[4,4,40,640]{3,2,1,0:T(8,128)}, u32[]{:S(2)}, u32[]{:S(2)}) async-start(f32[4,4,40,640]{3,2,1,0:T(8,128)} %broadcast_in_dim.83), calls=%async_computation.2 | async-start | bytes 3276800 | tf_op jit(solution)/shard_map/all_to_all | solution.py:35
  35.5 2.3 bitcast_select_fusion
  39.1 1.9 collective-permute-start.1
  41.0 1.9 collective-permute-start.2
  42.9 4.6 %collective-permute-start.3 = (f32[5,4,4,1280]{3,2,1,0:T(4,128)S(1)}, f32[5,4,4,1280]{3,2,1,0:T(4,128)}, u32[]{:S(2)}, u32[]{:S(2)}) collective-permute-start(f32[5,4,4,1280]{3,2,1,0:T(4,128)S(1)} %get-tuple-element.21), channel_id=1, source_target_pairs={{0,96},{1,97},{2,98},{3,99},{4,100},{5,101},{6,102},{7,103},{8,104... | collective-permute-start | bytes 1228808 | tf_op jit(solution)/shard_map/ppermute | solution.py:30
  48.5 7.6 %all-to-all-done.2 = f32[4,4,40,640]{3,2,1,0:T(8,128)} async-done(((f32[4,4,40,640]{3,2,1,0:T(8,128)}), f32[4,4,40,640]{3,2,1,0:T(8,128)}, u32[]{:S(2)}, u32[]{:S(2)}) %all-to-all-start.2) | async-done | bytes 1638432 | tf_op jit(solution)/shard_map/all_to_all | solution.py:35
  56.2 3.6 %collective-permute-start.7 = (f32[4,4,40,640]{3,2,1,0:T(8,128)}, f32[4,4,40,640]{3,2,1,0:T(8,128)S(1)}, u32[]{:S(2)}, u32[]{:S(2)}) collective-permute-start(f32[4,4,40,640]{3,2,1,0:T(8,128)} %all-to-all-done.2), channel_id=1, source_target_pairs={{0,16},{1,17},{2,18},{3,19},{4,20},{5,21},{6,22},{7,23},{8,24},{9,... | collective-permute-start | bytes 4915208 | tf_op jit(solution)/shard_map/ppermute | solution.py:30
  59.9 1.2 collective-permute-done.1
  61.1 2.7 collective-permute-done.3
  63.8 1.6 fusion.5
  65.5 4.8 %collective-permute-start.4 = (f32[5,4,1280]{2,0,1:T(8,128)S(1)}, f32[5,4,1280]{2,0,1:T(8,128)S(1)}, u32[]{:S(2)}, u32[]{:S(2)}) collective-permute-start(f32[5,4,1280]{2,0,1:T(8,128)S(1)} %bitcast.81), channel_id=1, source_target_pairs={{0,128},{1,129},{2,130},{3,131},{4,132},{5,133},{6,134},{7,135},{8... | collective-permute-start | bytes 307208 | tf_op jit(solution)/shard_map/ppermute | solution.py:30
  70.3 9.4 %collective-permute-start.5 = (f32[5,4,1280]{2,0,1:T(8,128)S(1)}, f32[5,4,1280]{2,0,1:T(8,128)S(1)}, u32[]{:S(2)}, u32[]{:S(2)}) collective-permute-start(f32[5,4,1280]{2,0,1:T(8,128)S(1)} %bitcast.82), channel_id=1, source_target_pairs={{0,256},{1,257},{2,258},{3,259},{4,260},{5,261},{6,262},{7,263},{8... | collective-permute-start | bytes 307208 | tf_op jit(solution)/shard_map/ppermute | solution.py:30
  79.8 5.2 %collective-permute-start.6 = (f32[5,4,1280]{2,0,1:T(8,128)S(1)}, f32[5,4,1280]{2,0,1:T(8,128)S(1)}, u32[]{:S(2)}, u32[]{:S(2)}) collective-permute-start(f32[5,4,1280]{2,0,1:T(8,128)S(1)} %bitcast.83), channel_id=1, source_target_pairs={{0,384},{1,385},{2,386},{3,387},{4,388},{5,389},{6,390},{7,391},{8... | collective-permute-start | bytes 307208 | tf_op jit(solution)/shard_map/ppermute | solution.py:30
  85.6 5.6 %collective-permute-done.4 = f32[5,4,1280]{2,0,1:T(8,128)S(1)} collective-permute-done((f32[5,4,1280]{2,0,1:T(8,128)S(1)}, f32[5,4,1280]{2,0,1:T(8,128)S(1)}, u32[]{:S(2)}, u32[]{:S(2)}) %collective-permute-start.4) | collective-permute-done | bytes 102432 | tf_op jit(solution)/shard_map/ppermute | solution.py:30
  91.2 15.8 %collective-permute-done.5 = f32[5,4,1280]{2,0,1:T(8,128)S(1)} collective-permute-done((f32[5,4,1280]{2,0,1:T(8,128)S(1)}, f32[5,4,1280]{2,0,1:T(8,128)S(1)}, u32[]{:S(2)}, u32[]{:S(2)}) %collective-permute-start.5) | collective-permute-done | bytes 102432 | tf_op jit(solution)/shard_map/ppermute | solution.py:30
  107.7 4.2 %all-to-all-start = ((f32[4,5,1280]{2,1,0:T(8,128)}), f32[4,5,1280]{2,1,0:T(8,128)}, u32[]{:S(2)}, u32[]{:S(2)}) async-start(f32[4,5,1280]{2,1,0:T(8,128)} %fusion.8), calls=%async_computation | async-start | bytes 327680 | tf_op jit(solution)/shard_map/all_to_all | solution.py:247
  113.1 3.5 %maximum_select_fusion = f32[2,4,4,40,640]{4,3,0,2,1:T(8,128)S(1)} fusion(f32[1,4,4,40,640]{4,3,0,2,1:T(8,128)} %bitcast.79, f32[1,4,4,40,640]{4,3,0,2,1:T(8,128)} %bitcast.15, pred[]{:T(512)S(6)} %eq.59), kind=kLoop, calls=%fused_computation | loop fusion | flops 2457600 | bytes 6553601 | tf_op jit(solution)/shard_map/jit(_where)/select_n | solution.py:51
  117.0 2.7 convolution_multiply_fusion
  120.6 1.5 reshape.164
  122.2 1.9 collective-permute-start.8
  124.1 4.7 %collective-permute-start.9 = (f32[20,640]{1,0:T(8,128)}, f32[20,640]{1,0:T(8,128)}, u32[]{:S(2)}, u32[]{:S(2)}) collective-permute-start(f32[20,640]{1,0:T(8,128)} %reshape.164), channel_id=1, source_target_pairs={{0,256},{1,257},{2,258},{3,259},{4,260},{5,261},{6,262},{7,263},{8... | collective-permute-start | bytes 153608 | tf_op jit(solution)/shard_map/ppermute | solution.py:30
  128.8 7.3 %collective-permute-start.10 = (f32[20,640]{1,0:T(8,128)}, f32[20,640]{1,0:T(8,128)}, u32[]{:S(2)}, u32[]{:S(2)}) collective-permute-start(f32[20,640]{1,0:T(8,128)} %reshape.164), channel_id=1, source_target_pairs={{0,128},{1,129},{2,130},{3,131},{4,132},{5,133},{6,134},{7,135},{8... | collective-permute-start | bytes 153608 | tf_op jit(solution)/shard_map/ppermute | solution.py:30
  136.0 7.5 %multiply_bitcast_fusion = f32[4,160,640]{2,1,0:T(8,128)} fusion(f32[1280,640,1]{1,0,2:T(8,128)S(1)} %bitcast.73, f32[160,4,1280]{2,1,0:T(4,128)} %param.6, f32[160]{0:T(256)S(1)} %compare_convert_fusion), kind=kOutput, calls=%fused_computation.4 | convolution fusion | flops 3146137600 | bytes 8192640 | tf_op jit(solution)/shard_map/pim,ma->ipa/dot_general | solution.py:259
  143.5 3.8 %all-to-all-start.4 = ((f32[4,160,640]{2,1,0:T(8,128)}), f32[4,160,640]{2,1,0:T(8,128)S(1)}, u32[]{:S(2)}, u32[]{:S(2)}) async-start(f32[4,160,640]{2,1,0:T(8,128)} %multiply_bitcast_fusion), calls=%async_computation.4 | async-start | bytes 3276800 | tf_op jit(solution)/shard_map/all_to_all | solution.py:268
  152.5 13.8 %all-to-all-done.4 = f32[4,160,640]{2,1,0:T(8,128)S(1)} async-done(((f32[4,160,640]{2,1,0:T(8,128)}), f32[4,160,640]{2,1,0:T(8,128)S(1)}, u32[]{:S(2)}, u32[]{:S(2)}) %all-to-all-start.4) | async-done | bytes 1638432 | tf_op jit(solution)/shard_map/all_to_all | solution.py:268
  166.4 28.5 %all_to_all.35.refs_0_ = f32[4,80,640]{2,1,0:T(8,128)S(1)} all-to-all(f32[4,80,640]{2,1,0:T(8,128)S(1)} %broadcast_in_dim.85), channel_id=1, replica_groups=mesh['zh'=4,'y'=4,'c'=2,'x'=4,'zl'=4] {'zl'}, dimensions={0} | all-to-all | bytes 1638400 | tf_op jit(solution)/shard_map/all_to_all | solution.py:35
  194.9 1.7 copy.16
  196.5 3.6 %all-to-all-start.5 = ((f32[4,160,640]{2,1,0:T(8,128)}), f32[4,160,640]{2,1,0:T(8,128)S(1)}, u32[]{:S(2)}, u32[]{:S(2)}) async-start(f32[4,160,640]{2,1,0:T(8,128)} %bitcast.76), calls=%async_computation.5 | async-start | bytes 3276800 | tf_op jit(solution)/shard_map/all_to_all | solution.py:275
  200.1 5.3 %collective-permute-start.12 = (f32[4,80,640]{2,1,0:T(8,128)S(1)}, f32[4,80,640]{2,1,0:T(8,128)S(1)}, u32[]{:S(2)}, u32[]{:S(2)}) collective-permute-start(f32[4,80,640]{2,1,0:T(8,128)S(1)} %all_to_all.35.refs_0_), channel_id=1, source_target_pairs={{0,32},{1,33},{2,34},{3,35},{4,36},{5,37},{6,38},{7,39},{8,40},{9,... | collective-permute-start | bytes 2457608 | tf_op jit(solution)/shard_map/ppermute | solution.py:30
  205.4 2.2 collective-permute-start.11
  207.6 4.8 %collective-permute-start.15 = (f32[4,80,640]{2,1,0:T(8,128)S(1)}, f32[4,80,640]{2,1,0:T(8,128)S(1)}, u32[]{:S(2)}, u32[]{:S(2)}) collective-permute-start(f32[4,80,640]{2,1,0:T(8,128)S(1)} %all_to_all.35.refs_0_), channel_id=1, source_target_pairs={{0,16},{1,17},{2,18},{3,19},{4,20},{5,21},{6,22},{7,23},{8,24},{9,... | collective-permute-start | bytes 2457608 | tf_op jit(solution)/shard_map/ppermute | solution.py:30
  212.4 9.2 %collective-permute-done.12.refs_2_ = f32[4,80,640]{2,1,0:T(8,128)S(1)} collective-permute-done((f32[4,80,640]{2,1,0:T(8,128)S(1)}, f32[4,80,640]{2,1,0:T(8,128)S(1)}, u32[]{:S(2)}, u32[]{:S(2)}) %collective-permute-start.12) | collective-permute-done | bytes 819232 | tf_op jit(solution)/shard_map/ppermute | solution.py:30
  221.6 2.8 %collective-permute-start.13 = (f32[2,80,640]{2,1,0:T(8,128)S(1)}, f32[2,80,640]{2,1,0:T(8,128)S(1)}, u32[]{:S(2)}, u32[]{:S(2)}) collective-permute-start(f32[2,80,640]{2,1,0:T(8,128)S(1)} %slice.8), channel_id=1, source_target_pairs={{0,32},{1,33},{2,34},{3,35},{4,36},{5,37},{6,38},{7,39},{8,40},{9,... | collective-permute-start | bytes 1228808 | tf_op jit(solution)/shard_map/ppermute | solution.py:30
  224.5 3.7 %collective-permute-start.14 = (f32[2,80,640]{2,1,0:T(8,128)S(1)}, f32[2,80,640]{2,1,0:T(8,128)S(1)}, u32[]{:S(2)}, u32[]{:S(2)}) collective-permute-start(f32[2,80,640]{2,1,0:T(8,128)S(1)} %slice.9), channel_id=1, source_target_pairs={{0,96},{1,97},{2,98},{3,99},{4,100},{5,101},{6,102},{7,103},{8,104... | collective-permute-start | bytes 1228808 | tf_op jit(solution)/shard_map/ppermute | solution.py:30
  228.2 5.7 %collective-permute-start.16 = (f32[4,80,640]{2,1,0:T(8,128)S(1)}, f32[4,80,640]{2,1,0:T(8,128)S(1)}, u32[]{:S(2)}, u32[]{:S(2)}) collective-permute-start(f32[4,80,640]{2,1,0:T(8,128)S(1)} %collective-permute-done.11.refs_1_), channel_id=1, source_target_pairs={{0,16},{1,17},{2,18},{3,19},{4,20},{5,21},{6,22},{7,23},{8,24},{9,... | collective-permute-start | bytes 2457608 | tf_op jit(solution)/shard_map/ppermute | solution.py:30
  233.9 1.9 collective-permute-start.17
  235.9 2.7 collective-permute-start.18
  238.6 2.1 collective-permute-start.19
  240.8 1.4 collective-permute-done.19.refs_9_
  243.9 9.0 %pair_kernel.1 = (f32[160,640]{1,0:T(8,128)S(1)}, f32[4,200,128]{2,1,0:T(8,128)}, bf16[4,4,160,640]{3,2,1,0:T(8,128)(2,1)}, bf16[4,4,160,640]{3,2,1,0:T(8,128)(2,1)}) custom-call(s32[2]{0:T(128)S(1)} %pad_add_fusion.place_ref, f32[4,80,640]{2,1,0:T(8,128)} %copy-done.3, f32[4,80,640]{2,1,0:T(8,128)} %copy-done.5, f32[4,80,640]{2,1,0:T(8,128)} %copy-done.4, ...), custom_call_target="tpu_custom_call" | custom-call | flops 1572864000 | bytes 16777216 | tf_op jit(solution)/shard_map/pair_kernel/pallas_call | solution.py:151
  252.9 4.2 %all-to-all-start.6 = ((f32[4,200,128]{2,1,0:T(8,128)}), f32[4,200,128]{2,1,0:T(8,128)S(1)}, u32[]{:S(2)}, u32[]{:S(2)}) async-start(f32[4,200,128]{2,1,0:T(8,128)} %get-tuple-element.14), calls=%async_computation.6 | async-start | bytes 819200 | tf_op jit(solution)/shard_map/all_to_all | solution.py:278
  260.5 8.3 %all-to-all-done.6.came_ref = f32[4,200,128]{2,1,0:T(8,128)S(1)} async-done(((f32[4,200,128]{2,1,0:T(8,128)}), f32[4,200,128]{2,1,0:T(8,128)S(1)}, u32[]{:S(2)}, u32[]{:S(2)}) %all-to-all-start.6) | async-done | bytes 409632 | tf_op jit(solution)/shard_map/all_to_all | solution.py:278
  268.8 7.1 %density_kernel.1 = f32[160,2560]{1,0:T(8,128)} custom-call(f32[160,640]{1,0:T(8,128)S(1)} %get-tuple-element.13.pair_ref, f32[4,200,128]{2,1,0:T(8,128)S(1)} %all-to-all-done.6.came_ref, f32[160,1]{1,0:T(8,128)S(1)} %copy.17.row_ref, f32[1,640]{1,0:T(1,128)S(1)} %broadcast_in_dim.87.column_ref, bf16[4,4,160,640]{3,2,1,0:T(8,128)(2,1)} %get-tuple-element.15.high_ref, ...), custom_call_target="tpu_custom_call" | custom-call | flops 1572864000 | bytes 10485760 | tf_op jit(solution)/shard_map/density_kernel/pallas_call | solution.py:207
  (89 shorter events, 15.6 us)
Async XLA Ops:
  0.0 11.5 %copy-start = (f32[80,640]{1,0:T(8,128)S(1)}, f32[80,640]{1,0:T(8,128)}, u32[]{:S(2)}) copy-start(f32[80,640]{1,0:T(8,128)} %param.7) | copy-start | bytes 614404
  0.0 16.7 %copy-start.16 = (s32[4]{0:T(128)S(1)}, s32[4]{0:T(128)}, u32[]{:S(2)}) copy-start(s32[4]{0:T(128)} %param.11) | copy-start | bytes 52
  2.8 32.7 %collective-permute-start = (f32[4,5,4,4,1280]{4,3,2,1,0:T(4,128)}, f32[4,5,4,4,1280]{4,3,2,1,0:T(4,128)}, u32[]{:S(2)}, u32[]{:S(2)}) collective-permute-start(f32[4,5,4,4,1280]{4,3,2,1,0:T(4,128)} %dynamic-slice_bitcast_fusion), channel_id=1, source_target_pairs={{0,16},{1,17},{2,18},{3,19},{4,20},{5,21},{6,22},{7,23},{8,24},{9,... | collective-permute-start | bytes 4915208 | tf_op jit(solution)/shard_map/ppermute | solution.py:30
  11.5 23.9 %copy-start.1 = (f32[160,4,1280]{2,1,0:T(4,128)S(1)}, f32[160,4,1280]{2,1,0:T(4,128)}, u32[]{:S(2)}) copy-start(f32[160,4,1280]{2,1,0:T(4,128)} %param.6) | copy-start | bytes 9830404
  12.3 16.4 %all-to-all-start.1 = ((f32[4,40,640]{2,1,0:T(8,128)}), f32[4,40,640]{2,1,0:T(8,128)}, u32[]{:S(2)}, u32[]{:S(2)}) async-start(f32[4,40,640]{2,1,0:T(8,128)} %broadcast_in_dim.82), calls=%async_computation.1 | async-start | bytes 819200 | tf_op jit(solution)/shard_map/all_to_all | solution.py:35
  31.1 25.1 %all-to-all-start.2 = ((f32[4,4,40,640]{3,2,1,0:T(8,128)}), f32[4,4,40,640]{3,2,1,0:T(8,128)}, u32[]{:S(2)}, u32[]{:S(2)}) async-start(f32[4,4,40,640]{3,2,1,0:T(8,128)} %broadcast_in_dim.83), calls=%async_computation.2 | async-start | bytes 3276800 | tf_op jit(solution)/shard_map/all_to_all | solution.py:35
  35.5 12.1 %copy-start.15 = (s32[16]{0:T(128)S(1)}, s32[16]{0:T(128)}, u32[]{:S(2)}) copy-start(s32[16]{0:T(128)} %param.10) | copy-start | bytes 196
  37.8 1.2 copy-start.2
  39.1 22.0 %collective-permute-start.1 = (f32[5,4,4,1280]{3,2,1,0:T(4,128)S(1)}, f32[5,4,4,1280]{3,2,1,0:T(4,128)S(1)}, u32[]{:S(2)}, u32[]{:S(2)}) collective-permute-start(f32[5,4,4,1280]{3,2,1,0:T(4,128)S(1)} %get-tuple-element.23), channel_id=1, source_target_pairs={{0,32},{1,33},{2,34},{3,35},{4,36},{5,37},{6,38},{7,39},{8,40},{9,... | collective-permute-start | bytes 1228808 | tf_op jit(solution)/shard_map/ppermute | solution.py:30
  41.0 20.1 %collective-permute-start.2 = (f32[5,4,4,1280]{3,2,1,0:T(4,128)S(1)}, f32[5,4,4,1280]{3,2,1,0:T(4,128)}, u32[]{:S(2)}, u32[]{:S(2)}) collective-permute-start(f32[5,4,4,1280]{3,2,1,0:T(4,128)S(1)} %get-tuple-element.22), channel_id=1, source_target_pairs={{0,64},{1,65},{2,66},{3,67},{4,68},{5,69},{6,70},{7,71},{8,72},{9,... | collective-permute-start | bytes 1228808 | tf_op jit(solution)/shard_map/ppermute | solution.py:30
  42.9 20.9 %collective-permute-start.3 = (f32[5,4,4,1280]{3,2,1,0:T(4,128)S(1)}, f32[5,4,4,1280]{3,2,1,0:T(4,128)}, u32[]{:S(2)}, u32[]{:S(2)}) collective-permute-start(f32[5,4,4,1280]{3,2,1,0:T(4,128)S(1)} %get-tuple-element.21), channel_id=1, source_target_pairs={{0,96},{1,97},{2,98},{3,99},{4,100},{5,101},{6,102},{7,103},{8,104... | collective-permute-start | bytes 1228808 | tf_op jit(solution)/shard_map/ppermute | solution.py:30
  56.2 55.7 %collective-permute-start.7 = (f32[4,4,40,640]{3,2,1,0:T(8,128)}, f32[4,4,40,640]{3,2,1,0:T(8,128)S(1)}, u32[]{:S(2)}, u32[]{:S(2)}) collective-permute-start(f32[4,4,40,640]{3,2,1,0:T(8,128)} %all-to-all-done.2), channel_id=1, source_target_pairs={{0,16},{1,17},{2,18},{3,19},{4,20},{5,21},{6,22},{7,23},{8,24},{9,... | collective-permute-start | bytes 4915208 | tf_op jit(solution)/shard_map/ppermute | solution.py:30
  65.5 25.7 %collective-permute-start.4 = (f32[5,4,1280]{2,0,1:T(8,128)S(1)}, f32[5,4,1280]{2,0,1:T(8,128)S(1)}, u32[]{:S(2)}, u32[]{:S(2)}) collective-permute-start(f32[5,4,1280]{2,0,1:T(8,128)S(1)} %bitcast.81), channel_id=1, source_target_pairs={{0,128},{1,129},{2,130},{3,131},{4,132},{5,133},{6,134},{7,135},{8... | collective-permute-start | bytes 307208 | tf_op jit(solution)/shard_map/ppermute | solution.py:30
  70.3 36.6 %collective-permute-start.5 = (f32[5,4,1280]{2,0,1:T(8,128)S(1)}, f32[5,4,1280]{2,0,1:T(8,128)S(1)}, u32[]{:S(2)}, u32[]{:S(2)}) collective-permute-start(f32[5,4,1280]{2,0,1:T(8,128)S(1)} %bitcast.82), channel_id=1, source_target_pairs={{0,256},{1,257},{2,258},{3,259},{4,260},{5,261},{6,262},{7,263},{8... | collective-permute-start | bytes 307208 | tf_op jit(solution)/shard_map/ppermute | solution.py:30
  79.8 27.2 %collective-permute-start.6 = (f32[5,4,1280]{2,0,1:T(8,128)S(1)}, f32[5,4,1280]{2,0,1:T(8,128)S(1)}, u32[]{:S(2)}, u32[]{:S(2)}) collective-permute-start(f32[5,4,1280]{2,0,1:T(8,128)S(1)} %bitcast.83), channel_id=1, source_target_pairs={{0,384},{1,385},{2,386},{3,387},{4,388},{5,389},{6,390},{7,391},{8... | collective-permute-start | bytes 307208 | tf_op jit(solution)/shard_map/ppermute | solution.py:30
  107.7 9.3 %all-to-all-start = ((f32[4,5,1280]{2,1,0:T(8,128)}), f32[4,5,1280]{2,1,0:T(8,128)}, u32[]{:S(2)}, u32[]{:S(2)}) async-start(f32[4,5,1280]{2,1,0:T(8,128)} %fusion.8), calls=%async_computation | async-start | bytes 327680 | tf_op jit(solution)/shard_map/all_to_all | solution.py:247
  111.9 1.2 copy-start.6
  122.2 25.1 %collective-permute-start.8 = (f32[20,640]{1,0:T(8,128)}, f32[20,640]{1,0:T(8,128)}, u32[]{:S(2)}, u32[]{:S(2)}) collective-permute-start(f32[20,640]{1,0:T(8,128)} %reshape.164), channel_id=1, source_target_pairs={{0,384},{1,385},{2,386},{3,387},{4,388},{5,389},{6,390},{7,391},{8... | collective-permute-start | bytes 153608 | tf_op jit(solution)/shard_map/ppermute | solution.py:30
  124.1 24.1 %collective-permute-start.9 = (f32[20,640]{1,0:T(8,128)}, f32[20,640]{1,0:T(8,128)}, u32[]{:S(2)}, u32[]{:S(2)}) collective-permute-start(f32[20,640]{1,0:T(8,128)} %reshape.164), channel_id=1, source_target_pairs={{0,256},{1,257},{2,258},{3,259},{4,260},{5,261},{6,262},{7,263},{8... | collective-permute-start | bytes 153608 | tf_op jit(solution)/shard_map/ppermute | solution.py:30
  128.8 20.2 %collective-permute-start.10 = (f32[20,640]{1,0:T(8,128)}, f32[20,640]{1,0:T(8,128)}, u32[]{:S(2)}, u32[]{:S(2)}) collective-permute-start(f32[20,640]{1,0:T(8,128)} %reshape.164), channel_id=1, source_target_pairs={{0,128},{1,129},{2,130},{3,131},{4,132},{5,133},{6,134},{7,135},{8... | collective-permute-start | bytes 153608 | tf_op jit(solution)/shard_map/ppermute | solution.py:30
  143.5 22.8 %all-to-all-start.4 = ((f32[4,160,640]{2,1,0:T(8,128)}), f32[4,160,640]{2,1,0:T(8,128)S(1)}, u32[]{:S(2)}, u32[]{:S(2)}) async-start(f32[4,160,640]{2,1,0:T(8,128)} %multiply_bitcast_fusion), calls=%async_computation.4 | async-start | bytes 3276800 | tf_op jit(solution)/shard_map/all_to_all | solution.py:268
  194.9 12.7 %copy-start.3 = (f32[4,80,640]{2,1,0:T(8,128)}, f32[4,80,640]{2,1,0:T(8,128)S(1)}, u32[]{:S(2)}) copy-start(f32[4,80,640]{2,1,0:T(8,128)S(1)} %all_to_all.35.refs_0_) | copy-start | bytes 2457604
  196.5 47.3 %all-to-all-start.5 = ((f32[4,160,640]{2,1,0:T(8,128)}), f32[4,160,640]{2,1,0:T(8,128)S(1)}, u32[]{:S(2)}, u32[]{:S(2)}) async-start(f32[4,160,640]{2,1,0:T(8,128)} %bitcast.76), calls=%async_computation.5 | async-start | bytes 3276800 | tf_op jit(solution)/shard_map/all_to_all | solution.py:275
  200.1 21.5 %collective-permute-start.12 = (f32[4,80,640]{2,1,0:T(8,128)S(1)}, f32[4,80,640]{2,1,0:T(8,128)S(1)}, u32[]{:S(2)}, u32[]{:S(2)}) collective-permute-start(f32[4,80,640]{2,1,0:T(8,128)S(1)} %all_to_all.35.refs_0_), channel_id=1, source_target_pairs={{0,32},{1,33},{2,34},{3,35},{4,36},{5,37},{6,38},{7,39},{8,40},{9,... | collective-permute-start | bytes 2457608 | tf_op jit(solution)/shard_map/ppermute | solution.py:30
  205.4 19.1 %collective-permute-start.11 = (f32[4,80,640]{2,1,0:T(8,128)S(1)}, f32[4,80,640]{2,1,0:T(8,128)S(1)}, u32[]{:S(2)}, u32[]{:S(2)}) collective-permute-start(f32[4,80,640]{2,1,0:T(8,128)S(1)} %all_to_all.35.refs_0_), channel_id=1, source_target_pairs={{0,96},{1,97},{2,98},{3,99},{4,100},{5,101},{6,102},{7,103},{8,104... | collective-permute-start | bytes 2457608 | tf_op jit(solution)/shard_map/ppermute | solution.py:30
  207.6 33.2 %collective-permute-start.15 = (f32[4,80,640]{2,1,0:T(8,128)S(1)}, f32[4,80,640]{2,1,0:T(8,128)S(1)}, u32[]{:S(2)}, u32[]{:S(2)}) collective-permute-start(f32[4,80,640]{2,1,0:T(8,128)S(1)} %all_to_all.35.refs_0_), channel_id=1, source_target_pairs={{0,16},{1,17},{2,18},{3,19},{4,20},{5,21},{6,22},{7,23},{8,24},{9,... | collective-permute-start | bytes 2457608 | tf_op jit(solution)/shard_map/ppermute | solution.py:30
  221.6 20.6 %copy-start.4 = (f32[4,80,640]{2,1,0:T(8,128)}, f32[4,80,640]{2,1,0:T(8,128)S(1)}, u32[]{:S(2)}) copy-start(f32[4,80,640]{2,1,0:T(8,128)S(1)} %collective-permute-done.12.refs_2_) | copy-start | bytes 2457604
  221.6 14.2 %collective-permute-start.13 = (f32[2,80,640]{2,1,0:T(8,128)S(1)}, f32[2,80,640]{2,1,0:T(8,128)S(1)}, u32[]{:S(2)}, u32[]{:S(2)}) collective-permute-start(f32[2,80,640]{2,1,0:T(8,128)S(1)} %slice.8), channel_id=1, source_target_pairs={{0,32},{1,33},{2,34},{3,35},{4,36},{5,37},{6,38},{7,39},{8,40},{9,... | collective-permute-start | bytes 1228808 | tf_op jit(solution)/shard_map/ppermute | solution.py:30
  224.5 17.7 %copy-start.5 = (f32[4,80,640]{2,1,0:T(8,128)}, f32[4,80,640]{2,1,0:T(8,128)S(1)}, u32[]{:S(2)}) copy-start(f32[4,80,640]{2,1,0:T(8,128)S(1)} %collective-permute-done.11.refs_1_) | copy-start | bytes 2457604
  224.5 14.0 %collective-permute-start.14 = (f32[2,80,640]{2,1,0:T(8,128)S(1)}, f32[2,80,640]{2,1,0:T(8,128)S(1)}, u32[]{:S(2)}, u32[]{:S(2)}) collective-permute-start(f32[2,80,640]{2,1,0:T(8,128)S(1)} %slice.9), channel_id=1, source_target_pairs={{0,96},{1,97},{2,98},{3,99},{4,100},{5,101},{6,102},{7,103},{8,104... | collective-permute-start | bytes 1228808 | tf_op jit(solution)/shard_map/ppermute | solution.py:30
  228.2 14.0 %collective-permute-start.16 = (f32[4,80,640]{2,1,0:T(8,128)S(1)}, f32[4,80,640]{2,1,0:T(8,128)S(1)}, u32[]{:S(2)}, u32[]{:S(2)}) collective-permute-start(f32[4,80,640]{2,1,0:T(8,128)S(1)} %collective-permute-done.11.refs_1_), channel_id=1, source_target_pairs={{0,16},{1,17},{2,18},{3,19},{4,20},{5,21},{6,22},{7,23},{8,24},{9,... | collective-permute-start | bytes 2457608 | tf_op jit(solution)/shard_map/ppermute | solution.py:30
  233.9 9.9 %collective-permute-start.17 = (f32[4,80,640]{2,1,0:T(8,128)S(1)}, f32[4,80,640]{2,1,0:T(8,128)}, u32[]{:S(2)}, u32[]{:S(2)}) collective-permute-start(f32[4,80,640]{2,1,0:T(8,128)S(1)} %collective-permute-done.12.refs_2_), channel_id=1, source_target_pairs={{0,16},{1,17},{2,18},{3,19},{4,20},{5,21},{6,22},{7,23},{8,24},{9,... | collective-permute-start | bytes 2457608 | tf_op jit(solution)/shard_map/ppermute | solution.py:30
  235.8 8.0 %copy-start.9 = (f32[2,80,640]{2,1,0:T(8,128)}, f32[2,80,640]{2,1,0:T(8,128)S(1)}, u32[]{:S(2)}) copy-start(f32[2,80,640]{2,1,0:T(8,128)S(1)} %collective-permute-done.13.refs_3_) | copy-start | bytes 1228804
  235.9 4.9 %collective-permute-start.18 = (f32[2,80,640]{2,1,0:T(8,128)S(1)}, f32[2,80,640]{2,1,0:T(8,128)S(1)}, u32[]{:S(2)}, u32[]{:S(2)}) collective-permute-start(f32[2,80,640]{2,1,0:T(8,128)S(1)} %collective-permute-done.13.refs_3_), channel_id=1, source_target_pairs={{0,16},{1,17},{2,18},{3,19},{4,20},{5,21},{6,22},{7,23},{8,24},{9,... | collective-permute-start | bytes 1228808 | tf_op jit(solution)/shard_map/ppermute | solution.py:30
  238.5 3.7 %copy-start.10 = (f32[2,80,640]{2,1,0:T(8,128)}, f32[2,80,640]{2,1,0:T(8,128)S(1)}, u32[]{:S(2)}) copy-start(f32[2,80,640]{2,1,0:T(8,128)S(1)} %collective-permute-done.14.refs_4_) | copy-start | bytes 1228804
  238.6 3.6 %collective-permute-start.19 = (f32[2,80,640]{2,1,0:T(8,128)S(1)}, f32[2,80,640]{2,1,0:T(8,128)S(1)}, u32[]{:S(2)}, u32[]{:S(2)}) collective-permute-start(f32[2,80,640]{2,1,0:T(8,128)S(1)} %collective-permute-done.14.refs_4_), channel_id=1, source_target_pairs={{0,16},{1,17},{2,18},{3,19},{4,20},{5,21},{6,22},{7,23},{8,24},{9,... | collective-permute-start | bytes 1228808 | tf_op jit(solution)/shard_map/ppermute | solution.py:30
  240.7 17.6 %copy-start.13 = (f32[640]{0:T(1024)S(1)}, f32[640]{0:T(1024)}, u32[]{:S(2)}) copy-start(f32[640]{0:T(1024)} %param.9) | copy-start | bytes 7684
  240.7 17.6 %copy-start.14 = (f32[128]{0:T(128)S(1)}, f32[128]{0:T(128)}, u32[]{:S(2)}) copy-start(f32[128]{0:T(128)} %param.8) | copy-start | bytes 1540
  240.7 1.5 copy-start.7
  240.8 1.5 copy-start.11
  242.2 0.7 copy-start.12
  242.9 0.9 copy-start.8
  252.9 15.9 %all-to-all-start.6 = ((f32[4,200,128]{2,1,0:T(8,128)}), f32[4,200,128]{2,1,0:T(8,128)S(1)}, u32[]{:S(2)}, u32[]{:S(2)}) async-start(f32[4,200,128]{2,1,0:T(8,128)} %get-tuple-element.14), calls=%async_computation.6 | async-start | bytes 819200 | tf_op jit(solution)/shard_map/all_to_all | solution.py:278

commit v3 on v2

--- a/solution.py
+++ b/solution.py
@@ -2,6 +2,7 @@
 import jax.numpy as jnp
 from jax import lax
 from jax.experimental import pallas as pl
+from jax.experimental.layout import Layout, with_layout_constraint
 from jax.experimental.pallas import tpu as pltpu
 from jax.sharding import Mesh, PartitionSpec as P
 
@@ -12,7 +13,7 @@
 LANES = 128
 
 
-def route(dz=0, dzh=0, dy=0, dc=0):
+def route(dz=0, dzh=0, dy=0, dc=0, dx=0):
     pairs = []
     for zh in range(ZHI):
         for y in range(Y):
@@ -21,7 +22,7 @@
                     for zl in range(ZLO):
                         z = (zh * ZLO + zl + dz + dzh * ZLO) % (ZHI * ZLO)
                         source = (((zh * Y + y) * CORE + c) * X + x) * ZLO + zl
-                        target = (((z // ZLO * Y + (y + dy) % Y) * CORE + (c ^ dc)) * X + x) * ZLO + z % ZLO
+                        target = (((z // ZLO * Y + (y + dy) % Y) * CORE + (c ^ dc)) * X + (x + dx) % X) * ZLO + z % ZLO
                         pairs.append((source, target))
     return pairs
 
@@ -45,10 +46,6 @@
     low = moved(behind[:half], dy=1)
     high = moved(ahead[half:], dy=-1)
     return [block, ahead, behind, low, high]
-
-
-def both_cores(block, other, core):
-    return jnp.where(core == 0, jnp.stack([block, other]), jnp.stack([other, block]))
 
 
 def own_core_part(half_ints, pair_root, c):
@@ -76,6 +73,32 @@
     return high, (value - high.astype(jnp.float32)).astype(jnp.bfloat16)
 
 
+def coefficient_kernel(place_ref, *refs):
+    own, other, out_ref = refs[:X], refs[X : 2 * X], refs[2 * X]
+    x, c = place_ref[0], place_ref[1]
+    for hop in range(X):
+        block = lax.rem(x + hop, X)
+        out_ref[block, 0, c] = own[hop][0]
+        out_ref[block, 0, 1 - c] = other[hop][0]
+
+
+def coefficients(own, other, x, c):
+    siblings, rows, vir_count = own[0].shape
+    operands = [pltpu.with_memory_space_constraint(v, pltpu.HBM) for v in (*own, *other)]
+    out = pl.pallas_call(
+        coefficient_kernel,
+        grid=(siblings,),
+        out_shape=jax.ShapeDtypeStruct((X, siblings, CORE, rows, vir_count), jnp.float32),
+        in_specs=[pl.BlockSpec(memory_space=pltpu.SMEM)]
+        + [pl.BlockSpec((1, rows, vir_count), lambda z: (z, 0, 0))] * (2 * X),
+        out_specs=pl.BlockSpec((X, 1, CORE, rows, vir_count), lambda z: (0, z, 0, 0, 0)),
+        compiler_params=pltpu.CompilerParams(dimension_semantics=("arbitrary",), vmem_limit_bytes=8 << 20),
+        cost_estimate=pl.CostEstimate(flops=0, bytes_accessed=8 << 20, transcendentals=0),
+        name="coefficient_kernel",
+    )(jnp.stack([x, c]).astype(jnp.int32), *operands)
+    return out.reshape(X * siblings * CORE * rows, vir_count)
+
+
 def three_pass(left, right, dims):
     def product(p, q):
         return lax.dot_general(p, q, (dims, ((), ())), preferred_element_type=jnp.float32)
@@ -87,7 +110,7 @@
     near, far, held_ref = refs[:5], refs[5:10], refs[10]
     pair_ref, sent_ref, high_ref, low_ref, rows_ref = refs[11:]
     early = pl.program_id(0) < ZLO // 2
-    y, c = place_ref[0], place_ref[1]
+    y, c, x = place_ref[0], place_ref[1], place_ref[2]
     part_rows, vir_count = near[0].shape[1:]
     tiles = part_rows // 8
     band = 2 * part_rows // X
@@ -114,6 +137,8 @@
     block = split_float(rows_ref[...].reshape(X * Y * band, vir_count))
     high_ref[:, 0] = block[0].reshape(X, Y * band, vir_count)
     low_ref[:, 0] = block[1].reshape(X, Y * band, vir_count)
+    turned = [lax.rem(x + hop, X) for hop in range(X)]
+    block = tuple(jnp.concatenate([ref[index, 0] for index in turned], 0) for ref in (high_ref, low_ref))
     product = three_pass(split_float(held_ref[0]), block, ((1,), (0,)))
     step = pl.program_id(0)
 
@@ -138,7 +163,7 @@
             )
 
 
-def pair_with_partner(near, far, held, y, c):
+def pair_with_partner(near, far, held, y, c, x):
     part_rows, vir_count = near[0].shape[1:]
     width_dev, lanes = held.shape[1:]
     rows_dev = part_rows * Y * CORE // X
@@ -172,7 +197,7 @@
             flops=6 * width_dev * X * ZLO * rows_dev * vir_count, bytes_accessed=16 << 20, transcendentals=0
         ),
         name="pair_kernel",
-    )(jnp.stack([y, c]).astype(jnp.int32), *operands, held)
+    )(jnp.stack([y, c, x]).astype(jnp.int32), *operands, held)
 
 
 def density_kernel(pair_ref, came_ref, row_ref, column_ref, high_ref, low_ref, gamma_ref, cols_ref, amp_ref):
@@ -242,12 +267,20 @@
     raw = own_core_part(half_ints, pair_root, c)
     raw = own_part(raw, pair_root // CORE % Y, y, "y")
     raw = raw.reshape(ZHI, step, occ_grp, basis_count)
-    raw = own_part(raw, pair_root // (Y * CORE), zh, "zh").transpose(1, 0, 2)
-    coeff = gathered(coeff, "x")
+    root_zh = (pair_root // (Y * CORE))[:, None]
+    parts = lax.all_to_all(raw, "zh", 0, 0)
+    raw = parts[0]
+    for place in range(1, ZHI):
+        raw = jnp.where(root_zh == place, parts[place], raw)
+    raw = raw.transpose(1, 0, 2)
+    ring = [coeff]
+    for hop in range(1, X):
+        ring.append(moved(coeff, dx=-hop))
     raw = lax.all_to_all(raw, "x", 0, 0).reshape(X * step, basis_count)
-    other = moved(coeff, dc=1)
-    coeff = both_cores(coeff, other, c)
-    coeff = coeff.transpose(1, 2, 0, 3, 4).reshape(basis_count, vir_count)
+    other = []
+    for block in ring:
+        other.append(moved(block, dc=1))
+    coeff = coefficients(ring, other, x, c)
 
     part = jnp.dot(raw, coeff, precision=FAST, preferred_element_type=jnp.float32)
     sizes = lax.dynamic_index_in_dim(aux_sizes.reshape(X, ZLO), zl, 1)[:, :, None]
@@ -257,24 +290,23 @@
     own_size = pick(aux_sizes, x * ZLO + zl)
     live_rows = (lax.iota(jnp.int32, rows_dev) < own_size).astype(jnp.float32)
     transformed = jnp.einsum("pim,ma->ipa", half_ints, coeff, precision=FAST, preferred_element_type=jnp.float32)
-    transformed = transformed * live_rows[None, :, None]
+    transformed = with_layout_constraint(transformed * live_rows[None, :, None], Layout((0, 1, 2)))
 
     part = part.reshape(X * step, vir_count)
-    ring = [part]
-    for hop in range(1, ZHI):
-        ring.append(moved(part, dzh=-hop))
-    part = lax.dynamic_slice_in_dim(jnp.stack(ring * 2), (ZHI - zh) % ZHI, ZHI, 0)
+    part = gathered(part, "zh")
     part = part.reshape(ZHI, X, step, vir_count).transpose(1, 0, 2, 3).reshape(X * ZHI * step, vir_count)
-    orbital_rows = lax.all_to_all(transformed, "x", 0, 0).reshape(X * rows_dev, vir_count)
+    owned = [pick(transformed, x)]
+    for hop in range(1, X):
+        owned.append(moved(pick(transformed, (x - hop) % X), dx=-hop))
+    orbital_rows = jnp.concatenate(owned, 0)
     near = gathered(part, "zl")
-    near, orbital_rows = lax.optimization_barrier((near, orbital_rows))
+    held = orbital_rows.T.reshape(ZLO, width_dev, X * rows_dev)
+    near, held = lax.optimization_barrier((near, held))
     near = ring_y(near)
     far = [moved(r, dc=1) for r in near]
-
-    held = orbital_rows.T.reshape(ZLO, width_dev, X * rows_dev)
     held = lax.all_to_all(held, "zl", 0, 0)
 
-    pair_rows, sent, high, low = pair_with_partner(near, far, held, y, c)
+    pair_rows, sent, high, low = pair_with_partner(near, far, held, y, c, x)
     came = lax.all_to_all(sent, "zl", 0, 0)
 
     own_orbital = ((zh * Y + y) * CORE + c) * occ_grp + x

time: 278 us -> 263 us (0.946)
  waiting for transfers between devices: 78.2 us -> 58.9 us
  starting transfers between devices: 110 us -> 121 us
  Pallas kernels: 16.1 us -> 20.1 us
  local copies, waits for them, and re-layouts: 21.7 us -> 17.8 us
  blocking collectives: 28.5 us -> 25.5 us
    all_to_all x2, waiting for transfers between devices: 19.7 us -> 0.01 us  [gathered(): lax.all_to_all(jnp.broadcast_to(block[None], (count,) + block.shape), axi...]
    ppermute x20 -> x23, waiting for transfers between devices: 35.9 us -> 50.3 us  [moved(): return lax.ppermute(block, AXES, route(**delta))]
    all_to_all x1, waiting for transfers between devices: 13.8 us -> 0.01 us  [shards(): parts = lax.all_to_all(raw, 'zh', 0, 0)]
    all_to_all x1, starting transfers between devices: 3.8 us -> 9.6 us  [shards(): parts = lax.all_to_all(raw, 'zh', 0, 0)]
    unnamed x41 -> x42, local copies, waits for them, and re-layouts: 8.16 us -> 4.51 us
    select_n x1 -> x0, other arithmetic: 3.49 us -> none  [both_cores(): jnp.where(core == 0, jnp.stack([block, other]), jnp.stack([other, block]))]
    pallas_call x0 -> x1, Pallas kernels: none -> 2.99 us  [coefficients(): pl.pallas_call(coefficient_kernel, grid=(siblings,), out_shape=jax.ShapeD...]
    all_to_all x1, blocking collectives: 28.5 us -> 25.5 us  [gathered(): lax.all_to_all(jnp.broadcast_to(block[None], (count,) + block.shape), axi...]
  transfers between devices with their start and end apart: 26 -> 29, of which waited for: 11 -> 10; matrix products, arithmetic and copies ran while one was open for 10% -> 7% of each run, Pallas kernels for 0% -> 1%
where the time goes in v3:
time: 263 us; the launch traced here: 262 us
  starting transfers between devices  121 us (46%)
  waiting for transfers between devices  58.9 us (22%)
  blocking collectives  25.5 us (10%)
  Pallas kernels  20.1 us (8%)
  local copies, waits for them, and re-layouts  17.8 us (7%)
  matrix products  9.31 us (4%)
  other arithmetic  6.4 us (2%)
  between operations  2.64 us (1%)
    ppermute x23, starting transfers between devices, moved(): return lax.ppermute(block, AXES, route(**delta))  86.8 us
    ppermute x23, waiting for transfers between devices, moved(): return lax.ppermute(block, AXES, route(**delta))  50.3 us
    all_to_all x1, blocking collectives, gathered(): lax.all_to_all(jnp.broadcast_to(block[None], (count,) + block.shape), axi...  25.5 us
    all_to_all x2, starting transfers between devices, gathered(): lax.all_to_all(jnp.broadcast_to(block[None], (count,) + block.shape), axi...  11.5 us
    pallas_call x1, Pallas kernels, pair_with_partner(): pl.pallas_call(pair_kernel, grid=(ZLO,), out_shape=(jax.ShapeDtypeStruct(...  10 us
    all_to_all x1, starting transfers between devices, shards(): parts = lax.all_to_all(raw, 'zh', 0, 0)  9.6 us
    all_to_all x1, waiting for transfers between devices, shards(): came = lax.all_to_all(sent, 'zl', 0, 0)  8.2 us
    pallas_call x1, Pallas kernels, densities(): pl.pallas_call(density_kernel, grid=(X,), out_shape=jax.ShapeDtypeStruct(...  7.06 us
  transfers between devices with their start and end apart: 29, of which 10 were waited for; matrix products, arithmetic and copies ran while one was open for 7% of the time, Pallas kernels for 1%

profile of v3, /device:TPU:1, one launch (start us, length us, event | category | flops | bytes accessed | tf_op | source)
XLA Modules:
  0.0 261.7 jit_solution(8092536964778758484)
XLA Ops:
  0.0 2.9 %dynamic-slice_bitcast_fusion = f32[4,5,4,4,1280]{4,3,2,1,0:T(4,128)} fusion(f32[4,5,2,4,4,1280]{5,4,3,2,1,0:T(4,128)} %bitcast.74, s32[]{:T(128)S(6)} %select_n.160), kind=kLoop, calls=%fused_computation.5 | loop fusion | bytes 3276804 | tf_op jit(solution)/shard_map/jit(dynamic_index_in_dim)/squeeze | solution.py:56
  2.9 8.9 %collective-permute-start = (f32[4,5,4,4,1280]{4,3,2,1,0:T(4,128)}, f32[4,5,4,4,1280]{4,3,2,1,0:T(4,128)}, u32[]{:S(2)}, u32[]{:S(2)}) collective-permute-start(f32[4,5,4,4,1280]{4,3,2,1,0:T(4,128)} %dynamic-slice_bitcast_fusion), channel_id=1, source_target_pairs={{0,16},{1,17},{2,18},{3,19},{4,20},{5,21},{6,22},{7,23},{8,24},{9,... | collective-permute-start | bytes 4915208 | tf_op jit(solution)/shard_map/ppermute | solution.py:31
  12.6 4.1 %all-to-all-start.2 = ((f32[4,40,640]{2,1,0:T(8,128)}), f32[4,40,640]{2,1,0:T(8,128)}, u32[]{:S(2)}, u32[]{:S(2)}) async-start(f32[4,40,640]{2,1,0:T(8,128)} %broadcast_in_dim.83), calls=%async_computation.2 | async-start | bytes 819200 | tf_op jit(solution)/shard_map/all_to_all | solution.py:36
  16.8 2.3 bitcast_select_fusion
  20.4 1.9 collective-permute-start.1
  22.3 1.9 collective-permute-start.2
  24.2 4.6 %collective-permute-start.3 = (f32[5,4,4,1280]{3,2,1,0:T(4,128)S(1)}, f32[5,4,4,1280]{3,2,1,0:T(4,128)S(1)}, u32[]{:S(2)}, u32[]{:S(2)}) collective-permute-start(f32[5,4,4,1280]{3,2,1,0:T(4,128)S(1)} %get-tuple-element.25), channel_id=1, source_target_pairs={{0,96},{1,97},{2,98},{3,99},{4,100},{5,101},{6,102},{7,103},{8,104... | collective-permute-start | bytes 1228808 | tf_op jit(solution)/shard_map/ppermute | solution.py:31
  28.8 14.4 %collective-permute-done.1 = f32[5,4,4,1280]{3,2,1,0:T(4,128)S(1)} collective-permute-done((f32[5,4,4,1280]{3,2,1,0:T(4,128)S(1)}, f32[5,4,4,1280]{3,2,1,0:T(4,128)S(1)}, u32[]{:S(2)}, u32[]{:S(2)}) %collective-permute-start.1) | collective-permute-done | bytes 409632 | tf_op jit(solution)/shard_map/ppermute | solution.py:31
  43.3 2.3 collective-permute-done.3
  45.5 2.1 fusion.5
  47.6 9.6 %all-to-all-start = ((f32[4,5,4,1280]{3,2,1,0:T(4,128)}), f32[4,5,4,1280]{3,2,1,0:T(4,128)S(1)}, u32[]{:S(2)}, u32[]{:S(2)}) async-start(f32[4,5,4,1280]{3,2,1,0:T(4,128)} %bitcast.10), calls=%async_computation | async-start | bytes 819200 | tf_op jit(solution)/shard_map/all_to_all | solution.py:271
  57.5 3.1 %collective-permute-start.6 = (f32[4,40,640]{2,1,0:T(8,128)}, f32[4,40,640]{2,1,0:T(8,128)S(1)}, u32[]{:S(2)}, u32[]{:S(2)}) collective-permute-start(f32[4,40,640]{2,1,0:T(8,128)} %all-to-all-done.2.refs_0_), channel_id=1, source_target_pairs={{0,4},{1,5},{2,6},{3,7},{4,8},{5,9},{6,10},{7,11},{8,12},{9,13},{1... | collective-permute-start | bytes 1228808 | tf_op jit(solution)/shard_map/ppermute | solution.py:31
  60.6 3.4 %collective-permute-start.4 = (f32[4,40,640]{2,1,0:T(8,128)}, f32[4,40,640]{2,1,0:T(8,128)S(1)}, u32[]{:S(2)}, u32[]{:S(2)}) collective-permute-start(f32[4,40,640]{2,1,0:T(8,128)} %all-to-all-done.2.refs_0_), channel_id=1, source_target_pairs={{0,12},{1,13},{2,14},{3,15},{4,0},{5,1},{6,2},{7,3},{8,4},{9,5},{1... | collective-permute-start | bytes 1228808 | tf_op jit(solution)/shard_map/ppermute | solution.py:31
  64.0 3.4 %collective-permute-start.5 = (f32[4,40,640]{2,1,0:T(8,128)}, f32[4,40,640]{2,1,0:T(8,128)S(1)}, u32[]{:S(2)}, u32[]{:S(2)}) collective-permute-start(f32[4,40,640]{2,1,0:T(8,128)} %all-to-all-done.2.refs_0_), channel_id=1, source_target_pairs={{0,8},{1,9},{2,10},{3,11},{4,12},{5,13},{6,14},{7,15},{8,0},{9,1},... | collective-permute-start | bytes 1228808 | tf_op jit(solution)/shard_map/ppermute | solution.py:31
  67.6 4.1 %collective-permute-start.7 = (f32[4,40,640]{2,1,0:T(8,128)}, f32[4,40,640]{2,1,0:T(8,128)S(1)}, u32[]{:S(2)}, u32[]{:S(2)}) collective-permute-start(f32[4,40,640]{2,1,0:T(8,128)} %all-to-all-done.2.refs_0_), channel_id=1, source_target_pairs={{0,16},{1,17},{2,18},{3,19},{4,20},{5,21},{6,22},{7,23},{8,24},{9,... | collective-permute-start | bytes 1228808 | tf_op jit(solution)/shard_map/ppermute | solution.py:31
  71.7 3.8 %collective-permute-start.10 = (f32[4,40,640]{2,1,0:T(8,128)S(1)}, f32[4,40,640]{2,1,0:T(8,128)S(1)}, u32[]{:S(2)}, u32[]{:S(2)}) collective-permute-start(f32[4,40,640]{2,1,0:T(8,128)S(1)} %collective-permute-done.6.refs_3_), channel_id=1, source_target_pairs={{0,16},{1,17},{2,18},{3,19},{4,20},{5,21},{6,22},{7,23},{8,24},{9,... | collective-permute-start | bytes 1228808 | tf_op jit(solution)/shard_map/ppermute | solution.py:31
  75.5 9.2 %collective-permute-start.8 = (f32[4,40,640]{2,1,0:T(8,128)S(1)}, f32[4,40,640]{2,1,0:T(8,128)S(1)}, u32[]{:S(2)}, u32[]{:S(2)}) collective-permute-start(f32[4,40,640]{2,1,0:T(8,128)S(1)} %collective-permute-done.4.refs_1_), channel_id=1, source_target_pairs={{0,16},{1,17},{2,18},{3,19},{4,20},{5,21},{6,22},{7,23},{8,24},{9,... | collective-permute-start | bytes 1228808 | tf_op jit(solution)/shard_map/ppermute | solution.py:31
  84.7 1.9 collective-permute-start.9
  87.6 4.5 %all-to-all-start.1 = ((f32[4,5,1280]{2,1,0:T(8,128)}), f32[4,5,1280]{2,1,0:T(8,128)}, u32[]{:S(2)}, u32[]{:S(2)}) async-start(f32[4,5,1280]{2,1,0:T(8,128)} %fusion.9), calls=%async_computation.1 | async-start | bytes 327680 | tf_op jit(solution)/shard_map/all_to_all | solution.py:279
  94.0 3.0 %coefficient_kernel.1 = f32[4,4,2,40,640]{4,3,2,1,0:T(8,128)S(1)} custom-call(s32[2]{0:T(128)S(1)} %pad_add_fusion.1.place_ref, f32[4,40,640]{2,1,0:T(8,128)} %all-to-all-done.2.refs_0_, f32[4,40,640]{2,1,0:T(8,128)} %copy-done.8, f32[4,40,640]{2,1,0:T(8,128)} %copy-done.9, f32[4,40,640]{2,1,0:T(8,128)} %copy-done.7, f32[4,40,640]{2,1,0:T(8,128)} %copy-done.10, ...), custom_call_target="tpu_custom_call" | custom-call | bytes 8388608 | tf_op jit(solution)/shard_map/coefficient_kernel/pallas_call | solution.py:88
  97.3 2.7 %convolution_multiply_fusion = f32[4,5,640]{2,1,0:T(8,128)} fusion(f32[4,5,1280]{2,1,0:T(8,128)} %all-to-all-done.1, f32[1280,640,1]{1,0,2:T(8,128)S(1)} %bitcast.72, f32[4,5]{1,0:T(4,128)S(1)} %compare_convert_fusion.1), kind=kOutput, calls=%fused_computation.6 | convolution fusion | flops 98316800 | bytes 3430480 | tf_op jit(solution)/shard_map/dot_general | solution.py:285
  100.9 25.5 %all_to_all.35 = f32[4,20,640]{2,1,0:T(8,128)S(1)} all-to-all(f32[4,20,640]{2,1,0:T(8,128)S(1)} %broadcast_in_dim.85), channel_id=1, replica_groups=mesh['zh'=4,'y'=4,'c'=2,'x'=4,'zl'=4] {'zh'}, dimensions={0} | all-to-all | bytes 409600 | tf_op jit(solution)/shard_map/all_to_all | solution.py:36
  127.3 1.7 broadcast_in_dim.86
  129.0 1.9 broadcast_in_dim.87
  130.9 7.4 %all-to-all-start.4 = ((f32[4,80,640]{2,1,0:T(8,128)}), f32[4,80,640]{2,1,0:T(8,128)}, u32[]{:S(2)}, u32[]{:S(2)}) async-start(f32[4,80,640]{2,1,0:T(8,128)} %broadcast_in_dim.87), calls=%async_computation.4 | async-start | bytes 1638400 | tf_op jit(solution)/shard_map/all_to_all | solution.py:36
  139.5 6.6 %multiply_bitcast_fusion = f32[4,160,640]{2,1,0:T(8,128)S(1)} fusion(f32[1280,640,1]{1,0,2:T(8,128)S(1)} %bitcast.73, f32[160,4,1280]{2,1,0:T(4,128)} %param.6, f32[160]{0:T(256)S(1)} %compare_convert_fusion), kind=kOutput, calls=%fused_computation.4 | convolution fusion | flops 3146137600 | bytes 8192640 | tf_op jit(solution)/shard_map/pim,ma->ipa/dot_general | solution.py:292
  146.2 7.3 %collective-permute-start.11 = (f32[160,640]{1,0:T(8,128)S(1)}, f32[160,640]{1,0:T(8,128)S(1)}, u32[]{:S(2)}, u32[]{:S(2)}) collective-permute-start(f32[160,640]{1,0:T(8,128)S(1)} %get-tuple-element.23), channel_id=1, source_target_pairs={{0,12},{1,13},{2,14},{3,15},{4,0},{5,1},{6,2},{7,3},{8,4},{9,5},{1... | collective-permute-start | bytes 1228808 | tf_op jit(solution)/shard_map/ppermute | solution.py:31
  153.5 2.5 collective-permute-start.12
  156.0 2.5 collective-permute-start.13
  158.5 4.6 %collective-permute-done.11 = f32[160,640]{1,0:T(8,128)S(1)} collective-permute-done((f32[160,640]{1,0:T(8,128)S(1)}, f32[160,640]{1,0:T(8,128)S(1)}, u32[]{:S(2)}, u32[]{:S(2)}) %collective-permute-start.11) | collective-permute-done | bytes 409632 | tf_op jit(solution)/shard_map/ppermute | solution.py:31
  163.1 3.8 %collective-permute-done.12 = f32[160,640]{1,0:T(8,128)S(1)} collective-permute-done((f32[160,640]{1,0:T(8,128)S(1)}, f32[160,640]{1,0:T(8,128)S(1)}, u32[]{:S(2)}, u32[]{:S(2)}) %collective-permute-start.12) | collective-permute-done | bytes 409632 | tf_op jit(solution)/shard_map/ppermute | solution.py:31
  166.9 10.2 %collective-permute-done.13 = f32[160,640]{1,0:T(8,128)S(1)} collective-permute-done((f32[160,640]{1,0:T(8,128)S(1)}, f32[160,640]{1,0:T(8,128)S(1)}, u32[]{:S(2)}, u32[]{:S(2)}) %collective-permute-start.13) | collective-permute-done | bytes 409632 | tf_op jit(solution)/shard_map/ppermute | solution.py:31
  177.2 1.7 copy.20
  178.9 4.5 %all-to-all-start.5 = ((f32[4,160,640]{2,1,0:T(8,128)}), f32[4,160,640]{2,1,0:T(8,128)S(1)}, u32[]{:S(2)}, u32[]{:S(2)}) async-start(f32[4,160,640]{2,1,0:T(8,128)} %bitcast.76), calls=%async_computation.5 | async-start | bytes 3276800 | tf_op jit(solution)/shard_map/all_to_all | solution.py:307
  183.4 4.8 %collective-permute-start.15 = (f32[4,80,640]{2,1,0:T(8,128)}, f32[4,80,640]{2,1,0:T(8,128)S(1)}, u32[]{:S(2)}, u32[]{:S(2)}) collective-permute-start(f32[4,80,640]{2,1,0:T(8,128)} %all-to-all-done.4.refs_0_), channel_id=1, source_target_pairs={{0,32},{1,33},{2,34},{3,35},{4,36},{5,37},{6,38},{7,39},{8,40},{9,... | collective-permute-start | bytes 2457608 | tf_op jit(solution)/shard_map/ppermute | solution.py:31
  188.2 2.1 collective-permute-start.14
  190.3 3.0 %collective-permute-start.18 = (f32[4,80,640]{2,1,0:T(8,128)}, f32[4,80,640]{2,1,0:T(8,128)S(1)}, u32[]{:S(2)}, u32[]{:S(2)}) collective-permute-start(f32[4,80,640]{2,1,0:T(8,128)} %all-to-all-done.4.refs_0_), channel_id=1, source_target_pairs={{0,16},{1,17},{2,18},{3,19},{4,20},{5,21},{6,22},{7,23},{8,24},{9,... | collective-permute-start | bytes 2457608 | tf_op jit(solution)/shard_map/ppermute | solution.py:31
  193.3 13.1 %collective-permute-done.15.refs_2_ = f32[4,80,640]{2,1,0:T(8,128)S(1)} collective-permute-done((f32[4,80,640]{2,1,0:T(8,128)}, f32[4,80,640]{2,1,0:T(8,128)S(1)}, u32[]{:S(2)}, u32[]{:S(2)}) %collective-permute-start.15) | collective-permute-done | bytes 819232 | tf_op jit(solution)/shard_map/ppermute | solution.py:31
  206.5 2.9 %collective-permute-start.16 = (f32[2,80,640]{2,1,0:T(8,128)S(1)}, f32[2,80,640]{2,1,0:T(8,128)S(1)}, u32[]{:S(2)}, u32[]{:S(2)}) collective-permute-start(f32[2,80,640]{2,1,0:T(8,128)S(1)} %slice.28), channel_id=1, source_target_pairs={{0,32},{1,33},{2,34},{3,35},{4,36},{5,37},{6,38},{7,39},{8,40},{9,... | collective-permute-start | bytes 1228808 | tf_op jit(solution)/shard_map/ppermute | solution.py:31
  209.5 3.6 %collective-permute-start.17 = (f32[2,80,640]{2,1,0:T(8,128)S(1)}, f32[2,80,640]{2,1,0:T(8,128)S(1)}, u32[]{:S(2)}, u32[]{:S(2)}) collective-permute-start(f32[2,80,640]{2,1,0:T(8,128)S(1)} %slice.29), channel_id=1, source_target_pairs={{0,96},{1,97},{2,98},{3,99},{4,100},{5,101},{6,102},{7,103},{8,104... | collective-permute-start | bytes 1228808 | tf_op jit(solution)/shard_map/ppermute | solution.py:31
  213.0 3.8 %collective-permute-start.19 = (f32[4,80,640]{2,1,0:T(8,128)S(1)}, f32[4,80,640]{2,1,0:T(8,128)S(1)}, u32[]{:S(2)}, u32[]{:S(2)}) collective-permute-start(f32[4,80,640]{2,1,0:T(8,128)S(1)} %collective-permute-done.14.refs_1_), channel_id=1, source_target_pairs={{0,16},{1,17},{2,18},{3,19},{4,20},{5,21},{6,22},{7,23},{8,24},{9,... | collective-permute-start | bytes 2457608 | tf_op jit(solution)/shard_map/ppermute | solution.py:31
  216.9 1.9 collective-permute-start.20
  219.3 4.1 %collective-permute-start.21 = (f32[2,80,640]{2,1,0:T(8,128)S(1)}, f32[2,80,640]{2,1,0:T(8,128)S(1)}, u32[]{:S(2)}, u32[]{:S(2)}) collective-permute-start(f32[2,80,640]{2,1,0:T(8,128)S(1)} %collective-permute-done.16.refs_3_), channel_id=1, source_target_pairs={{0,16},{1,17},{2,18},{3,19},{4,20},{5,21},{6,22},{7,23},{8,24},{9,... | collective-permute-start | bytes 1228808 | tf_op jit(solution)/shard_map/ppermute | solution.py:31
  223.4 2.1 collective-permute-start.22
  228.7 10.0 %pair_kernel.1 = (f32[160,640]{1,0:T(8,128)S(1)}, f32[4,200,128]{2,1,0:T(8,128)}, bf16[4,4,160,640]{3,2,1,0:T(8,128)(2,1)}, bf16[4,4,160,640]{3,2,1,0:T(8,128)(2,1)}) custom-call(s32[3]{0:T(128)S(1)} %pad_add_fusion.place_ref, f32[4,80,640]{2,1,0:T(8,128)} %all-to-all-done.4.refs_0_, f32[4,80,640]{2,1,0:T(8,128)} %copy-done.4, f32[4,80,640]{2,1,0:T(8,128)} %copy-done.3, ...), custom_call_target="tpu_custom_call" | custom-call | flops 1572864000 | bytes 16777216 | tf_op jit(solution)/shard_map/pair_kernel/pallas_call | solution.py:176
  238.7 4.3 %all-to-all-start.6 = ((f32[4,200,128]{2,1,0:T(8,128)}), f32[4,200,128]{2,1,0:T(8,128)S(1)}, u32[]{:S(2)}, u32[]{:S(2)}) async-start(f32[4,200,128]{2,1,0:T(8,128)} %get-tuple-element.14), calls=%async_computation.6 | async-start | bytes 819200 | tf_op jit(solution)/shard_map/all_to_all | solution.py:310
  246.5 8.2 %all-to-all-done.6.came_ref = f32[4,200,128]{2,1,0:T(8,128)S(1)} async-done(((f32[4,200,128]{2,1,0:T(8,128)}), f32[4,200,128]{2,1,0:T(8,128)S(1)}, u32[]{:S(2)}, u32[]{:S(2)}) %all-to-all-start.6) | async-done | bytes 409632 | tf_op jit(solution)/shard_map/all_to_all | solution.py:310
  254.7 7.1 %density_kernel.1 = f32[160,2560]{1,0:T(8,128)} custom-call(f32[160,640]{1,0:T(8,128)S(1)} %get-tuple-element.13.pair_ref, f32[4,200,128]{2,1,0:T(8,128)S(1)} %all-to-all-done.6.came_ref, f32[160,1]{1,0:T(8,128)S(1)} %copy.21.row_ref, f32[1,640]{1,0:T(1,128)S(1)} %broadcast_in_dim.89.column_ref, bf16[4,4,160,640]{3,2,1,0:T(8,128)(2,1)} %get-tuple-element.15.high_ref, ...), custom_call_target="tpu_custom_call" | custom-call | flops 1572864000 | bytes 10485760 | tf_op jit(solution)/shard_map/density_kernel/pallas_call | solution.py:232
  (93 shorter events, 13.9 us)
Async XLA Ops:
  0.0 11.7 %copy-start = (f32[80,640]{1,0:T(8,128)S(1)}, f32[80,640]{1,0:T(8,128)}, u32[]{:S(2)}) copy-start(f32[80,640]{1,0:T(8,128)} %param.7) | copy-start | bytes 614404
  0.0 16.8 %copy-start.1 = (f32[160,4,1280]{2,1,0:T(4,128)S(1)}, f32[160,4,1280]{2,1,0:T(4,128)}, u32[]{:S(2)}) copy-start(f32[160,4,1280]{2,1,0:T(4,128)} %param.6) | copy-start | bytes 9830404
  2.9 13.9 %copy-start.20 = (s32[4]{0:T(128)S(1)}, s32[4]{0:T(128)}, u32[]{:S(2)}) copy-start(s32[4]{0:T(128)} %param.11) | copy-start | bytes 52
  2.9 13.9 %collective-permute-start = (f32[4,5,4,4,1280]{4,3,2,1,0:T(4,128)}, f32[4,5,4,4,1280]{4,3,2,1,0:T(4,128)}, u32[]{:S(2)}, u32[]{:S(2)}) collective-permute-start(f32[4,5,4,4,1280]{4,3,2,1,0:T(4,128)} %dynamic-slice_bitcast_fusion), channel_id=1, source_target_pairs={{0,16},{1,17},{2,18},{3,19},{4,20},{5,21},{6,22},{7,23},{8,24},{9,... | collective-permute-start | bytes 4915208 | tf_op jit(solution)/shard_map/ppermute | solution.py:31
  12.6 35.0 %all-to-all-start.2 = ((f32[4,40,640]{2,1,0:T(8,128)}), f32[4,40,640]{2,1,0:T(8,128)}, u32[]{:S(2)}, u32[]{:S(2)}) async-start(f32[4,40,640]{2,1,0:T(8,128)} %broadcast_in_dim.83), calls=%async_computation.2 | async-start | bytes 819200 | tf_op jit(solution)/shard_map/all_to_all | solution.py:36
  19.1 1.2 copy-start.2
  20.4 36.9 %copy-start.19 = (s32[16]{0:T(128)S(1)}, s32[16]{0:T(128)}, u32[]{:S(2)}) copy-start(s32[16]{0:T(128)} %param.10) | copy-start | bytes 196
  20.4 22.9 %collective-permute-start.1 = (f32[5,4,4,1280]{3,2,1,0:T(4,128)S(1)}, f32[5,4,4,1280]{3,2,1,0:T(4,128)S(1)}, u32[]{:S(2)}, u32[]{:S(2)}) collective-permute-start(f32[5,4,4,1280]{3,2,1,0:T(4,128)S(1)} %get-tuple-element.27), channel_id=1, source_target_pairs={{0,32},{1,33},{2,34},{3,35},{4,36},{5,37},{6,38},{7,39},{8,40},{9,... | collective-permute-start | bytes 1228808 | tf_op jit(solution)/shard_map/ppermute | solution.py:31
  22.3 21.0 %collective-permute-start.2 = (f32[5,4,4,1280]{3,2,1,0:T(4,128)S(1)}, f32[5,4,4,1280]{3,2,1,0:T(4,128)S(1)}, u32[]{:S(2)}, u32[]{:S(2)}) collective-permute-start(f32[5,4,4,1280]{3,2,1,0:T(4,128)S(1)} %get-tuple-element.26), channel_id=1, source_target_pairs={{0,64},{1,65},{2,66},{3,67},{4,68},{5,69},{6,70},{7,71},{8,72},{9,... | collective-permute-start | bytes 1228808 | tf_op jit(solution)/shard_map/ppermute | solution.py:31
  24.2 21.3 %collective-permute-start.3 = (f32[5,4,4,1280]{3,2,1,0:T(4,128)S(1)}, f32[5,4,4,1280]{3,2,1,0:T(4,128)S(1)}, u32[]{:S(2)}, u32[]{:S(2)}) collective-permute-start(f32[5,4,4,1280]{3,2,1,0:T(4,128)S(1)} %get-tuple-element.25), channel_id=1, source_target_pairs={{0,96},{1,97},{2,98},{3,99},{4,100},{5,101},{6,102},{7,103},{8,104... | collective-permute-start | bytes 1228808 | tf_op jit(solution)/shard_map/ppermute | solution.py:31
  47.6 39.0 %all-to-all-start = ((f32[4,5,4,1280]{3,2,1,0:T(4,128)}), f32[4,5,4,1280]{3,2,1,0:T(4,128)S(1)}, u32[]{:S(2)}, u32[]{:S(2)}) async-start(f32[4,5,4,1280]{3,2,1,0:T(4,128)} %bitcast.10), calls=%async_computation | async-start | bytes 819200 | tf_op jit(solution)/shard_map/all_to_all | solution.py:271
  57.5 14.1 %collective-permute-start.6 = (f32[4,40,640]{2,1,0:T(8,128)}, f32[4,40,640]{2,1,0:T(8,128)S(1)}, u32[]{:S(2)}, u32[]{:S(2)}) collective-permute-start(f32[4,40,640]{2,1,0:T(8,128)} %all-to-all-done.2.refs_0_), channel_id=1, source_target_pairs={{0,4},{1,5},{2,6},{3,7},{4,8},{5,9},{6,10},{7,11},{8,12},{9,13},{1... | collective-permute-start | bytes 1228808 | tf_op jit(solution)/shard_map/ppermute | solution.py:31
  60.6 14.8 %collective-permute-start.4 = (f32[4,40,640]{2,1,0:T(8,128)}, f32[4,40,640]{2,1,0:T(8,128)S(1)}, u32[]{:S(2)}, u32[]{:S(2)}) collective-permute-start(f32[4,40,640]{2,1,0:T(8,128)} %all-to-all-done.2.refs_0_), channel_id=1, source_target_pairs={{0,12},{1,13},{2,14},{3,15},{4,0},{5,1},{6,2},{7,3},{8,4},{9,5},{1... | collective-permute-start | bytes 1228808 | tf_op jit(solution)/shard_map/ppermute | solution.py:31
  64.0 20.7 %collective-permute-start.5 = (f32[4,40,640]{2,1,0:T(8,128)}, f32[4,40,640]{2,1,0:T(8,128)S(1)}, u32[]{:S(2)}, u32[]{:S(2)}) collective-permute-start(f32[4,40,640]{2,1,0:T(8,128)} %all-to-all-done.2.refs_0_), channel_id=1, source_target_pairs={{0,8},{1,9},{2,10},{3,11},{4,12},{5,13},{6,14},{7,15},{8,0},{9,1},... | collective-permute-start | bytes 1228808 | tf_op jit(solution)/shard_map/ppermute | solution.py:31
  67.6 24.7 %collective-permute-start.7 = (f32[4,40,640]{2,1,0:T(8,128)}, f32[4,40,640]{2,1,0:T(8,128)S(1)}, u32[]{:S(2)}, u32[]{:S(2)}) collective-permute-start(f32[4,40,640]{2,1,0:T(8,128)} %all-to-all-done.2.refs_0_), channel_id=1, source_target_pairs={{0,16},{1,17},{2,18},{3,19},{4,20},{5,21},{6,22},{7,23},{8,24},{9,... | collective-permute-start | bytes 1228808 | tf_op jit(solution)/shard_map/ppermute | solution.py:31
  71.7 20.6 %copy-start.7 = (f32[4,40,640]{2,1,0:T(8,128)}, f32[4,40,640]{2,1,0:T(8,128)S(1)}, u32[]{:S(2)}) copy-start(f32[4,40,640]{2,1,0:T(8,128)S(1)} %collective-permute-done.6.refs_3_) | copy-start | bytes 1228804
  71.7 20.6 %collective-permute-start.10 = (f32[4,40,640]{2,1,0:T(8,128)S(1)}, f32[4,40,640]{2,1,0:T(8,128)S(1)}, u32[]{:S(2)}, u32[]{:S(2)}) collective-permute-start(f32[4,40,640]{2,1,0:T(8,128)S(1)} %collective-permute-done.6.refs_3_), channel_id=1, source_target_pairs={{0,16},{1,17},{2,18},{3,19},{4,20},{5,21},{6,22},{7,23},{8,24},{9,... | collective-permute-start | bytes 1228808 | tf_op jit(solution)/shard_map/ppermute | solution.py:31
  75.4 16.8 %copy-start.8 = (f32[4,40,640]{2,1,0:T(8,128)}, f32[4,40,640]{2,1,0:T(8,128)S(1)}, u32[]{:S(2)}) copy-start(f32[4,40,640]{2,1,0:T(8,128)S(1)} %collective-permute-done.4.refs_1_) | copy-start | bytes 1228804
  75.5 16.8 %collective-permute-start.8 = (f32[4,40,640]{2,1,0:T(8,128)S(1)}, f32[4,40,640]{2,1,0:T(8,128)S(1)}, u32[]{:S(2)}, u32[]{:S(2)}) collective-permute-start(f32[4,40,640]{2,1,0:T(8,128)S(1)} %collective-permute-done.4.refs_1_), channel_id=1, source_target_pairs={{0,16},{1,17},{2,18},{3,19},{4,20},{5,21},{6,22},{7,23},{8,24},{9,... | collective-permute-start | bytes 1228808 | tf_op jit(solution)/shard_map/ppermute | solution.py:31
  84.7 7.6 %copy-start.9 = (f32[4,40,640]{2,1,0:T(8,128)}, f32[4,40,640]{2,1,0:T(8,128)S(1)}, u32[]{:S(2)}) copy-start(f32[4,40,640]{2,1,0:T(8,128)S(1)} %collective-permute-done.5.refs_2_) | copy-start | bytes 1228804
  84.7 9.2 %collective-permute-start.9 = (f32[4,40,640]{2,1,0:T(8,128)S(1)}, f32[4,40,640]{2,1,0:T(8,128)}, u32[]{:S(2)}, u32[]{:S(2)}) collective-permute-start(f32[4,40,640]{2,1,0:T(8,128)S(1)} %collective-permute-done.5.refs_2_), channel_id=1, source_target_pairs={{0,16},{1,17},{2,18},{3,19},{4,20},{5,21},{6,22},{7,23},{8,24},{9,... | collective-permute-start | bytes 1228808 | tf_op jit(solution)/shard_map/ppermute | solution.py:31
  87.6 9.7 %all-to-all-start.1 = ((f32[4,5,1280]{2,1,0:T(8,128)}), f32[4,5,1280]{2,1,0:T(8,128)}, u32[]{:S(2)}, u32[]{:S(2)}) async-start(f32[4,5,1280]{2,1,0:T(8,128)} %fusion.9), calls=%async_computation.1 | async-start | bytes 327680 | tf_op jit(solution)/shard_map/all_to_all | solution.py:279
  92.2 0.9 copy-start.12
  93.2 0.8 copy-start.14
  130.9 48.0 %all-to-all-start.4 = ((f32[4,80,640]{2,1,0:T(8,128)}), f32[4,80,640]{2,1,0:T(8,128)}, u32[]{:S(2)}, u32[]{:S(2)}) async-start(f32[4,80,640]{2,1,0:T(8,128)} %broadcast_in_dim.87), calls=%async_computation.4 | async-start | bytes 1638400 | tf_op jit(solution)/shard_map/all_to_all | solution.py:36
  146.2 16.9 %collective-permute-start.11 = (f32[160,640]{1,0:T(8,128)S(1)}, f32[160,640]{1,0:T(8,128)S(1)}, u32[]{:S(2)}, u32[]{:S(2)}) collective-permute-start(f32[160,640]{1,0:T(8,128)S(1)} %get-tuple-element.23), channel_id=1, source_target_pairs={{0,12},{1,13},{2,14},{3,15},{4,0},{5,1},{6,2},{7,3},{8,4},{9,5},{1... | collective-permute-start | bytes 1228808 | tf_op jit(solution)/shard_map/ppermute | solution.py:31
  153.5 13.4 %collective-permute-start.12 = (f32[160,640]{1,0:T(8,128)S(1)}, f32[160,640]{1,0:T(8,128)S(1)}, u32[]{:S(2)}, u32[]{:S(2)}) collective-permute-start(f32[160,640]{1,0:T(8,128)S(1)} %get-tuple-element.22), channel_id=1, source_target_pairs={{0,8},{1,9},{2,10},{3,11},{4,12},{5,13},{6,14},{7,15},{8,0},{9,1},... | collective-permute-start | bytes 1228808 | tf_op jit(solution)/shard_map/ppermute | solution.py:31
  156.0 21.1 %collective-permute-start.13 = (f32[160,640]{1,0:T(8,128)S(1)}, f32[160,640]{1,0:T(8,128)S(1)}, u32[]{:S(2)}, u32[]{:S(2)}) collective-permute-start(f32[160,640]{1,0:T(8,128)S(1)} %get-tuple-element.24), channel_id=1, source_target_pairs={{0,4},{1,5},{2,6},{3,7},{4,8},{5,9},{6,10},{7,11},{8,12},{9,13},{1... | collective-permute-start | bytes 1228808 | tf_op jit(solution)/shard_map/ppermute | solution.py:31
  178.9 49.8 %all-to-all-start.5 = ((f32[4,160,640]{2,1,0:T(8,128)}), f32[4,160,640]{2,1,0:T(8,128)S(1)}, u32[]{:S(2)}, u32[]{:S(2)}) async-start(f32[4,160,640]{2,1,0:T(8,128)} %bitcast.76), calls=%async_computation.5 | async-start | bytes 3276800 | tf_op jit(solution)/shard_map/all_to_all | solution.py:307
  183.4 23.0 %collective-permute-start.15 = (f32[4,80,640]{2,1,0:T(8,128)}, f32[4,80,640]{2,1,0:T(8,128)S(1)}, u32[]{:S(2)}, u32[]{:S(2)}) collective-permute-start(f32[4,80,640]{2,1,0:T(8,128)} %all-to-all-done.4.refs_0_), channel_id=1, source_target_pairs={{0,32},{1,33},{2,34},{3,35},{4,36},{5,37},{6,38},{7,39},{8,40},{9,... | collective-permute-start | bytes 2457608 | tf_op jit(solution)/shard_map/ppermute | solution.py:31
  188.2 21.2 %collective-permute-start.14 = (f32[4,80,640]{2,1,0:T(8,128)}, f32[4,80,640]{2,1,0:T(8,128)S(1)}, u32[]{:S(2)}, u32[]{:S(2)}) collective-permute-start(f32[4,80,640]{2,1,0:T(8,128)} %all-to-all-done.4.refs_0_), channel_id=1, source_target_pairs={{0,96},{1,97},{2,98},{3,99},{4,100},{5,101},{6,102},{7,103},{8,104... | collective-permute-start | bytes 2457608 | tf_op jit(solution)/shard_map/ppermute | solution.py:31
  190.3 35.3 %collective-permute-start.18 = (f32[4,80,640]{2,1,0:T(8,128)}, f32[4,80,640]{2,1,0:T(8,128)S(1)}, u32[]{:S(2)}, u32[]{:S(2)}) collective-permute-start(f32[4,80,640]{2,1,0:T(8,128)} %all-to-all-done.4.refs_0_), channel_id=1, source_target_pairs={{0,16},{1,17},{2,18},{3,19},{4,20},{5,21},{6,22},{7,23},{8,24},{9,... | collective-permute-start | bytes 2457608 | tf_op jit(solution)/shard_map/ppermute | solution.py:31
  206.4 22.3 %copy-start.3 = (f32[4,80,640]{2,1,0:T(8,128)}, f32[4,80,640]{2,1,0:T(8,128)S(1)}, u32[]{:S(2)}) copy-start(f32[4,80,640]{2,1,0:T(8,128)S(1)} %collective-permute-done.15.refs_2_) | copy-start | bytes 2457604
  206.5 12.8 %collective-permute-start.16 = (f32[2,80,640]{2,1,0:T(8,128)S(1)}, f32[2,80,640]{2,1,0:T(8,128)S(1)}, u32[]{:S(2)}, u32[]{:S(2)}) collective-permute-start(f32[2,80,640]{2,1,0:T(8,128)S(1)} %slice.28), channel_id=1, source_target_pairs={{0,32},{1,33},{2,34},{3,35},{4,36},{5,37},{6,38},{7,39},{8,40},{9,... | collective-permute-start | bytes 1228808 | tf_op jit(solution)/shard_map/ppermute | solution.py:31
  209.4 17.6 %copy-start.4 = (f32[4,80,640]{2,1,0:T(8,128)}, f32[4,80,640]{2,1,0:T(8,128)S(1)}, u32[]{:S(2)}) copy-start(f32[4,80,640]{2,1,0:T(8,128)S(1)} %collective-permute-done.14.refs_1_) | copy-start | bytes 2457604
  209.5 13.9 %collective-permute-start.17 = (f32[2,80,640]{2,1,0:T(8,128)S(1)}, f32[2,80,640]{2,1,0:T(8,128)S(1)}, u32[]{:S(2)}, u32[]{:S(2)}) collective-permute-start(f32[2,80,640]{2,1,0:T(8,128)S(1)} %slice.29), channel_id=1, source_target_pairs={{0,96},{1,97},{2,98},{3,99},{4,100},{5,101},{6,102},{7,103},{8,104... | collective-permute-start | bytes 1228808 | tf_op jit(solution)/shard_map/ppermute | solution.py:31
  213.0 14.0 %collective-permute-start.19 = (f32[4,80,640]{2,1,0:T(8,128)S(1)}, f32[4,80,640]{2,1,0:T(8,128)S(1)}, u32[]{:S(2)}, u32[]{:S(2)}) collective-permute-start(f32[4,80,640]{2,1,0:T(8,128)S(1)} %collective-permute-done.14.refs_1_), channel_id=1, source_target_pairs={{0,16},{1,17},{2,18},{3,19},{4,20},{5,21},{6,22},{7,23},{8,24},{9,... | collective-permute-start | bytes 2457608 | tf_op jit(solution)/shard_map/ppermute | solution.py:31
  216.9 11.8 %collective-permute-start.20 = (f32[4,80,640]{2,1,0:T(8,128)S(1)}, f32[4,80,640]{2,1,0:T(8,128)}, u32[]{:S(2)}, u32[]{:S(2)}) collective-permute-start(f32[4,80,640]{2,1,0:T(8,128)S(1)} %collective-permute-done.15.refs_2_), channel_id=1, source_target_pairs={{0,16},{1,17},{2,18},{3,19},{4,20},{5,21},{6,22},{7,23},{8,24},{9,... | collective-permute-start | bytes 2457608 | tf_op jit(solution)/shard_map/ppermute | solution.py:31
  219.2 9.4 %copy-start.11 = (f32[2,80,640]{2,1,0:T(8,128)}, f32[2,80,640]{2,1,0:T(8,128)S(1)}, u32[]{:S(2)}) copy-start(f32[2,80,640]{2,1,0:T(8,128)S(1)} %collective-permute-done.16.refs_3_) | copy-start | bytes 1228804
  219.3 6.3 %collective-permute-start.21 = (f32[2,80,640]{2,1,0:T(8,128)S(1)}, f32[2,80,640]{2,1,0:T(8,128)S(1)}, u32[]{:S(2)}, u32[]{:S(2)}) collective-permute-start(f32[2,80,640]{2,1,0:T(8,128)S(1)} %collective-permute-done.16.refs_3_), channel_id=1, source_target_pairs={{0,16},{1,17},{2,18},{3,19},{4,20},{5,21},{6,22},{7,23},{8,24},{9,... | collective-permute-start | bytes 1228808 | tf_op jit(solution)/shard_map/ppermute | solution.py:31
  223.4 3.7 %copy-start.13 = (f32[2,80,640]{2,1,0:T(8,128)}, f32[2,80,640]{2,1,0:T(8,128)S(1)}, u32[]{:S(2)}) copy-start(f32[2,80,640]{2,1,0:T(8,128)S(1)} %collective-permute-done.17.refs_4_) | copy-start | bytes 1228804
  223.4 3.6 %collective-permute-start.22 = (f32[2,80,640]{2,1,0:T(8,128)S(1)}, f32[2,80,640]{2,1,0:T(8,128)S(1)}, u32[]{:S(2)}, u32[]{:S(2)}) collective-permute-start(f32[2,80,640]{2,1,0:T(8,128)S(1)} %collective-permute-done.17.refs_4_), channel_id=1, source_target_pairs={{0,16},{1,17},{2,18},{3,19},{4,20},{5,21},{6,22},{7,23},{8,24},{9,... | collective-permute-start | bytes 1228808 | tf_op jit(solution)/shard_map/ppermute | solution.py:31
  225.6 18.8 %copy-start.17 = (f32[640]{0:T(1024)S(1)}, f32[640]{0:T(1024)}, u32[]{:S(2)}) copy-start(f32[640]{0:T(1024)} %param.9) | copy-start | bytes 7684
  225.6 18.8 %copy-start.18 = (f32[128]{0:T(128)S(1)}, f32[128]{0:T(128)}, u32[]{:S(2)}) copy-start(f32[128]{0:T(128)} %param.8) | copy-start | bytes 1540
  225.6 1.5 copy-start.5
  225.6 1.5 copy-start.15
  227.8 0.9 copy-start.6
  238.7 16.0 %all-to-all-start.6 = ((f32[4,200,128]{2,1,0:T(8,128)}), f32[4,200,128]{2,1,0:T(8,128)S(1)}, u32[]{:S(2)}, u32[]{:S(2)}) async-start(f32[4,200,128]{2,1,0:T(8,128)} %get-tuple-element.14), calls=%async_computation.6 | async-start | bytes 819200 | tf_op jit(solution)/shard_map/all_to_all | solution.py:310
  (2 other events, 1.5 us)

commit v4 on v3

--- a/solution.py
+++ b/solution.py
@@ -42,7 +42,8 @@
 
 def ring_y(block):
     half = block.shape[0] // 2
-    ahead, behind = moved(block, dy=-1), moved(block, dy=1)
+    ahead = moved(block, dy=-1)
+    behind = moved(block, dy=1)
     low = moved(behind[:half], dy=1)
     high = moved(ahead[half:], dy=-1)
     return [block, ahead, behind, low, high]
@@ -292,14 +293,13 @@
     transformed = jnp.einsum("pim,ma->ipa", half_ints, coeff, precision=FAST, preferred_element_type=jnp.float32)
     transformed = with_layout_constraint(transformed * live_rows[None, :, None], Layout((0, 1, 2)))
 
-    part = part.reshape(X * step, vir_count)
-    part = gathered(part, "zh")
-    part = part.reshape(ZHI, X, step, vir_count).transpose(1, 0, 2, 3).reshape(X * ZHI * step, vir_count)
+    part = part.reshape(step, X, vir_count)
+    near = lax.all_to_all(jnp.broadcast_to(part[None], (ZHI * ZLO,) + part.shape), ("zh", "zl"), 0, 0)
+    near = near.reshape(ZHI, ZLO, X, step, vir_count).transpose(1, 2, 0, 3, 4).reshape(ZLO, X * ZHI * step, vir_count)
     owned = [pick(transformed, x)]
     for hop in range(1, X):
         owned.append(moved(pick(transformed, (x - hop) % X), dx=-hop))
     orbital_rows = jnp.concatenate(owned, 0)
-    near = gathered(part, "zl")
     held = orbital_rows.T.reshape(ZLO, width_dev, X * rows_dev)
     near, held = lax.optimization_barrier((near, held))
     near = ring_y(near)

time: 263 us -> 238 us (0.905)
  the two profiles are of different devices: /device:TPU:1 before, /device:TPU:130 now
where the time goes in v4:
time: 238 us; the launch traced here: 236 us
  starting transfers between devices  113 us (47%)
  waiting for transfers between devices  67.5 us (28%)
  Pallas kernels  20 us (8%)
  local copies, waits for them, and re-layouts  17.8 us (7%)
  matrix products  9.31 us (4%)
  other arithmetic  6.38 us (3%)
  between operations  2.39 us (1%)
    ppermute x23, starting transfers between devices, moved(): return lax.ppermute(block, AXES, route(**delta))  66.3 us
    ppermute x23, waiting for transfers between devices, moved(): return lax.ppermute(block, AXES, route(**delta))  55.5 us
    all_to_all x1, starting transfers between devices, shards(): parts = lax.all_to_all(raw, 'zh', 0, 0)  12.4 us
    all_to_all x1, starting transfers between devices, shards(): lax.all_to_all(jnp.broadcast_to(part[None], (ZHI * ZLO,) + part.shape), (...  12 us
    pallas_call x1, Pallas kernels, pair_with_partner(): pl.pallas_call(pair_kernel, grid=(ZLO,), out_shape=(jax.ShapeDtypeStruct(...  9.99 us
    all_to_all x1, waiting for transfers between devices, shards(): came = lax.all_to_all(sent, 'zl', 0, 0)  9.27 us
    pallas_call x1, Pallas kernels, densities(): pl.pallas_call(density_kernel, grid=(X,), out_shape=jax.ShapeDtypeStruct(...  7.06 us
    dot_general x1, matrix products, shards(): jnp.einsum('pim,ma->ipa', half_ints, coeff, precision=FAST, preferred_ele...  6.57 us
  transfers between devices with their start and end apart: 29, of which 14 were waited for; matrix products, arithmetic and copies ran while one was open for 8% of the time, Pallas kernels for 1%

profile of v4, /device:TPU:130, one launch (start us, length us, event | category | flops | bytes accessed | tf_op | source)
XLA Modules:
  0.0 236.4 jit_solution(15449410079027008928)
XLA Ops:
  0.0 2.9 %dynamic-slice_bitcast_fusion = f32[4,5,4,4,1280]{4,3,2,1,0:T(4,128)} fusion(f32[4,5,2,4,4,1280]{5,4,3,2,1,0:T(4,128)} %bitcast.77, s32[]{:T(128)S(6)} %select_n.160), kind=kLoop, calls=%fused_computation.5 | loop fusion | bytes 3276804 | tf_op jit(solution)/shard_map/jit(dynamic_index_in_dim)/squeeze | solution.py:57
  2.9 2.0 collective-permute-start
  5.7 5.9 %all-to-all-start.2 = ((f32[4,40,640]{2,1,0:T(8,128)}), f32[4,40,640]{2,1,0:T(8,128)}, u32[]{:S(2)}, u32[]{:S(2)}) async-start(f32[4,40,640]{2,1,0:T(8,128)} %broadcast_in_dim.76), calls=%async_computation.2 | async-start | bytes 819200 | tf_op jit(solution)/shard_map/all_to_all | solution.py:36
  11.7 2.3 bitcast_select_fusion
  15.2 3.5 %collective-permute-start.1 = (f32[5,4,4,1280]{3,2,1,0:T(4,128)S(1)}, f32[5,4,4,1280]{3,2,1,0:T(4,128)S(1)}, u32[]{:S(2)}, u32[]{:S(2)}) collective-permute-start(f32[5,4,4,1280]{3,2,1,0:T(4,128)S(1)} %get-tuple-element.27), channel_id=1, source_target_pairs={{0,32},{1,33},{2,34},{3,35},{4,36},{5,37},{6,38},{7,39},{8,40},{9,... | collective-permute-start | bytes 1228808 | tf_op jit(solution)/shard_map/ppermute | solution.py:31
  18.7 4.8 %collective-permute-start.2 = (f32[5,4,4,1280]{3,2,1,0:T(4,128)S(1)}, f32[5,4,4,1280]{3,2,1,0:T(4,128)S(1)}, u32[]{:S(2)}, u32[]{:S(2)}) collective-permute-start(f32[5,4,4,1280]{3,2,1,0:T(4,128)S(1)} %get-tuple-element.26), channel_id=1, source_target_pairs={{0,64},{1,65},{2,66},{3,67},{4,68},{5,69},{6,70},{7,71},{8,72},{9,... | collective-permute-start | bytes 1228808 | tf_op jit(solution)/shard_map/ppermute | solution.py:31
  23.6 3.3 %collective-permute-start.3 = (f32[5,4,4,1280]{3,2,1,0:T(4,128)S(1)}, f32[5,4,4,1280]{3,2,1,0:T(4,128)S(1)}, u32[]{:S(2)}, u32[]{:S(2)}) collective-permute-start(f32[5,4,4,1280]{3,2,1,0:T(4,128)S(1)} %get-tuple-element.25), channel_id=1, source_target_pairs={{0,96},{1,97},{2,98},{3,99},{4,100},{5,101},{6,102},{7,103},{8,104... | collective-permute-start | bytes 1228808 | tf_op jit(solution)/shard_map/ppermute | solution.py:31
  26.9 3.2 %collective-permute-done.1 = f32[5,4,4,1280]{3,2,1,0:T(4,128)S(1)} collective-permute-done((f32[5,4,4,1280]{3,2,1,0:T(4,128)S(1)}, f32[5,4,4,1280]{3,2,1,0:T(4,128)S(1)}, u32[]{:S(2)}, u32[]{:S(2)}) %collective-permute-start.1) | collective-permute-done | bytes 409632 | tf_op jit(solution)/shard_map/ppermute | solution.py:31
  30.0 9.9 %collective-permute-done.2 = f32[5,4,4,1280]{3,2,1,0:T(4,128)S(1)} collective-permute-done((f32[5,4,4,1280]{3,2,1,0:T(4,128)S(1)}, f32[5,4,4,1280]{3,2,1,0:T(4,128)S(1)}, u32[]{:S(2)}, u32[]{:S(2)}) %collective-permute-start.2) | collective-permute-done | bytes 409632 | tf_op jit(solution)/shard_map/ppermute | solution.py:31
  41.3 2.1 fusion.5
  43.4 12.4 %all-to-all-start = ((f32[4,5,4,1280]{3,2,1,0:T(4,128)}), f32[4,5,4,1280]{3,2,1,0:T(4,128)S(1)}, u32[]{:S(2)}, u32[]{:S(2)}) async-start(f32[4,5,4,1280]{3,2,1,0:T(4,128)} %bitcast.10), calls=%async_computation | async-start | bytes 819200 | tf_op jit(solution)/shard_map/all_to_all | solution.py:272
  56.1 3.4 %collective-permute-start.6 = (f32[4,40,640]{2,1,0:T(8,128)}, f32[4,40,640]{2,1,0:T(8,128)S(1)}, u32[]{:S(2)}, u32[]{:S(2)}) collective-permute-start(f32[4,40,640]{2,1,0:T(8,128)} %all-to-all-done.2.refs_0_), channel_id=1, source_target_pairs={{0,4},{1,5},{2,6},{3,7},{4,8},{5,9},{6,10},{7,11},{8,12},{9,13},{1... | collective-permute-start | bytes 1228808 | tf_op jit(solution)/shard_map/ppermute | solution.py:31
  59.5 2.4 %collective-permute-start.4 = (f32[4,40,640]{2,1,0:T(8,128)}, f32[4,40,640]{2,1,0:T(8,128)S(1)}, u32[]{:S(2)}, u32[]{:S(2)}) collective-permute-start(f32[4,40,640]{2,1,0:T(8,128)} %all-to-all-done.2.refs_0_), channel_id=1, source_target_pairs={{0,12},{1,13},{2,14},{3,15},{4,0},{5,1},{6,2},{7,3},{8,4},{9,5},{1... | collective-permute-start | bytes 1228808 | tf_op jit(solution)/shard_map/ppermute | solution.py:31
  62.0 4.0 %collective-permute-start.5 = (f32[4,40,640]{2,1,0:T(8,128)}, f32[4,40,640]{2,1,0:T(8,128)S(1)}, u32[]{:S(2)}, u32[]{:S(2)}) collective-permute-start(f32[4,40,640]{2,1,0:T(8,128)} %all-to-all-done.2.refs_0_), channel_id=1, source_target_pairs={{0,8},{1,9},{2,10},{3,11},{4,12},{5,13},{6,14},{7,15},{8,0},{9,1},... | collective-permute-start | bytes 1228808 | tf_op jit(solution)/shard_map/ppermute | solution.py:31
  66.1 1.9 collective-permute-start.7
  68.0 2.4 %collective-permute-done.6.refs_3_ = f32[4,40,640]{2,1,0:T(8,128)S(1)} collective-permute-done((f32[4,40,640]{2,1,0:T(8,128)}, f32[4,40,640]{2,1,0:T(8,128)S(1)}, u32[]{:S(2)}, u32[]{:S(2)}) %collective-permute-start.6) | collective-permute-done | bytes 409632 | tf_op jit(solution)/shard_map/ppermute | solution.py:31
  70.4 1.9 collective-permute-start.10
  73.3 1.9 collective-permute-start.8
  75.2 5.8 %collective-permute-done.5.refs_2_ = f32[4,40,640]{2,1,0:T(8,128)S(1)} collective-permute-done((f32[4,40,640]{2,1,0:T(8,128)}, f32[4,40,640]{2,1,0:T(8,128)S(1)}, u32[]{:S(2)}, u32[]{:S(2)}) %collective-permute-start.5) | collective-permute-done | bytes 409632 | tf_op jit(solution)/shard_map/ppermute | solution.py:31
  81.0 1.9 collective-permute-start.9
  83.9 6.6 %all-to-all-start.1 = ((f32[4,5,1280]{2,1,0:T(8,128)}), f32[4,5,1280]{2,1,0:T(8,128)}, u32[]{:S(2)}, u32[]{:S(2)}) async-start(f32[4,5,1280]{2,1,0:T(8,128)} %fusion.9), calls=%async_computation.1 | async-start | bytes 327680 | tf_op jit(solution)/shard_map/all_to_all | solution.py:280
  92.2 3.0 %coefficient_kernel.1 = f32[4,4,2,40,640]{4,3,2,1,0:T(8,128)S(1)} custom-call(s32[2]{0:T(128)S(1)} %pad_add_fusion.1.place_ref, f32[4,40,640]{2,1,0:T(8,128)} %all-to-all-done.2.refs_0_, f32[4,40,640]{2,1,0:T(8,128)} %copy-done.9, f32[4,40,640]{2,1,0:T(8,128)} %copy-done.10, f32[4,40,640]{2,1,0:T(8,128)} %copy-done.8, f32[4,40,640]{2,1,0:T(8,128)} %copy-done.11, ...), custom_call_target="tpu_custom_call" | custom-call | bytes 8388608 | tf_op jit(solution)/shard_map/coefficient_kernel/pallas_call | solution.py:89
  95.2 2.7 %convolution_multiply_fusion = f32[4,5,640]{2,1,0:T(8,128)} fusion(f32[4,5,1280]{2,1,0:T(8,128)} %all-to-all-done.1, f32[1280,640,1]{1,0,2:T(8,128)S(1)} %bitcast.75, f32[4,5]{1,0:T(4,128)S(1)} %compare_convert_fusion.1), kind=kOutput, calls=%fused_computation.6 | convolution fusion | flops 98316800 | bytes 3430480 | tf_op jit(solution)/shard_map/dot_general | solution.py:286
  99.9 12.0 %all-to-all-start.3 = ((f32[16,5,4,640]{3,2,1,0:T(4,128)}), f32[16,5,4,640]{3,2,1,0:T(4,128)}, u32[]{:S(2)}, u32[]{:S(2)}) async-start(f32[16,5,4,640]{3,2,1,0:T(4,128)} %broadcast_in_dim.78), calls=%async_computation.3 | async-start | bytes 1638400 | tf_op jit(solution)/shard_map/all_to_all | solution.py:297
  113.1 6.6 %multiply_bitcast_fusion = f32[4,160,640]{2,1,0:T(8,128)S(1)} fusion(f32[1280,640,1]{1,0,2:T(8,128)S(1)} %bitcast.76, f32[160,4,1280]{2,1,0:T(4,128)} %param.6, f32[160]{0:T(256)S(1)} %compare_convert_fusion), kind=kOutput, calls=%fused_computation.4 | convolution fusion | flops 3146137600 | bytes 8192640 | tf_op jit(solution)/shard_map/pim,ma->ipa/dot_general | solution.py:293
  119.8 3.4 %collective-permute-start.11 = (f32[160,640]{1,0:T(8,128)S(1)}, f32[160,640]{1,0:T(8,128)S(1)}, u32[]{:S(2)}, u32[]{:S(2)}) collective-permute-start(f32[160,640]{1,0:T(8,128)S(1)} %get-tuple-element.23), channel_id=1, source_target_pairs={{0,12},{1,13},{2,14},{3,15},{4,0},{5,1},{6,2},{7,3},{8,4},{9,5},{1... | collective-permute-start | bytes 1228808 | tf_op jit(solution)/shard_map/ppermute | solution.py:31
  123.2 3.4 %collective-permute-start.12 = (f32[160,640]{1,0:T(8,128)S(1)}, f32[160,640]{1,0:T(8,128)S(1)}, u32[]{:S(2)}, u32[]{:S(2)}) collective-permute-start(f32[160,640]{1,0:T(8,128)S(1)} %get-tuple-element.22), channel_id=1, source_target_pairs={{0,8},{1,9},{2,10},{3,11},{4,12},{5,13},{6,14},{7,15},{8,0},{9,1},... | collective-permute-start | bytes 1228808 | tf_op jit(solution)/shard_map/ppermute | solution.py:31
  126.6 3.7 %collective-permute-start.13 = (f32[160,640]{1,0:T(8,128)S(1)}, f32[160,640]{1,0:T(8,128)S(1)}, u32[]{:S(2)}, u32[]{:S(2)}) collective-permute-start(f32[160,640]{1,0:T(8,128)S(1)} %get-tuple-element.24), channel_id=1, source_target_pairs={{0,4},{1,5},{2,6},{3,7},{4,8},{5,9},{6,10},{7,11},{8,12},{9,13},{1... | collective-permute-start | bytes 1228808 | tf_op jit(solution)/shard_map/ppermute | solution.py:31
  130.3 2.9 %collective-permute-done.11 = f32[160,640]{1,0:T(8,128)S(1)} collective-permute-done((f32[160,640]{1,0:T(8,128)S(1)}, f32[160,640]{1,0:T(8,128)S(1)}, u32[]{:S(2)}, u32[]{:S(2)}) %collective-permute-start.11) | collective-permute-done | bytes 409632 | tf_op jit(solution)/shard_map/ppermute | solution.py:31
  133.2 8.5 %collective-permute-done.12 = f32[160,640]{1,0:T(8,128)S(1)} collective-permute-done((f32[160,640]{1,0:T(8,128)S(1)}, f32[160,640]{1,0:T(8,128)S(1)}, u32[]{:S(2)}, u32[]{:S(2)}) %collective-permute-start.12) | collective-permute-done | bytes 409632 | tf_op jit(solution)/shard_map/ppermute | solution.py:31
  141.7 2.8 %collective-permute-done.13 = f32[160,640]{1,0:T(8,128)S(1)} collective-permute-done((f32[160,640]{1,0:T(8,128)S(1)}, f32[160,640]{1,0:T(8,128)S(1)}, u32[]{:S(2)}, u32[]{:S(2)}) %collective-permute-start.13) | collective-permute-done | bytes 409632 | tf_op jit(solution)/shard_map/ppermute | solution.py:31
  146.3 2.7 %all-to-all-done.3 = f32[16,5,4,640]{3,2,1,0:T(4,128)} async-done(((f32[16,5,4,640]{3,2,1,0:T(4,128)}), f32[16,5,4,640]{3,2,1,0:T(4,128)}, u32[]{:S(2)}, u32[]{:S(2)}) %all-to-all-start.3) | async-done | bytes 819232 | tf_op jit(solution)/shard_map/all_to_all | solution.py:297
  151.5 5.2 %all-to-all-start.4 = ((f32[4,160,640]{2,1,0:T(8,128)}), f32[4,160,640]{2,1,0:T(8,128)S(1)}, u32[]{:S(2)}, u32[]{:S(2)}) async-start(f32[4,160,640]{2,1,0:T(8,128)} %bitcast.79), calls=%async_computation.4 | async-start | bytes 3276800 | tf_op jit(solution)/shard_map/all_to_all | solution.py:307
  157.9 5.1 %collective-permute-start.15 = (f32[4,80,640]{2,1,0:T(8,128)S(1)}, f32[4,80,640]{2,1,0:T(8,128)S(1)}, u32[]{:S(2)}, u32[]{:S(2)}) collective-permute-start(f32[4,80,640]{2,1,0:T(8,128)S(1)} %copy.28.refs_0_), channel_id=1, source_target_pairs={{0,32},{1,33},{2,34},{3,35},{4,36},{5,37},{6,38},{7,39},{8,40},{9,... | collective-permute-start | bytes 2457608 | tf_op jit(solution)/shard_map/ppermute | solution.py:31
  163.1 2.1 collective-permute-start.14
  165.1 1.9 collective-permute-start.18
  167.1 14.2 %collective-permute-done.15.refs_2_ = f32[4,80,640]{2,1,0:T(8,128)S(1)} collective-permute-done((f32[4,80,640]{2,1,0:T(8,128)S(1)}, f32[4,80,640]{2,1,0:T(8,128)S(1)}, u32[]{:S(2)}, u32[]{:S(2)}) %collective-permute-start.15) | collective-permute-done | bytes 819232 | tf_op jit(solution)/shard_map/ppermute | solution.py:31
  181.3 3.5 %collective-permute-start.16 = (f32[2,80,640]{2,1,0:T(8,128)S(1)}, f32[2,80,640]{2,1,0:T(8,128)S(1)}, u32[]{:S(2)}, u32[]{:S(2)}) collective-permute-start(f32[2,80,640]{2,1,0:T(8,128)S(1)} %slice.28), channel_id=1, source_target_pairs={{0,32},{1,33},{2,34},{3,35},{4,36},{5,37},{6,38},{7,39},{8,40},{9,... | collective-permute-start | bytes 1228808 | tf_op jit(solution)/shard_map/ppermute | solution.py:31
  184.9 3.6 %collective-permute-start.17 = (f32[2,80,640]{2,1,0:T(8,128)S(1)}, f32[2,80,640]{2,1,0:T(8,128)S(1)}, u32[]{:S(2)}, u32[]{:S(2)}) collective-permute-start(f32[2,80,640]{2,1,0:T(8,128)S(1)} %slice.29), channel_id=1, source_target_pairs={{0,96},{1,97},{2,98},{3,99},{4,100},{5,101},{6,102},{7,103},{8,104... | collective-permute-start | bytes 1228808 | tf_op jit(solution)/shard_map/ppermute | solution.py:31
  188.4 1.9 collective-permute-start.19
  190.4 2.4 %collective-permute-start.20 = (f32[4,80,640]{2,1,0:T(8,128)S(1)}, f32[4,80,640]{2,1,0:T(8,128)}, u32[]{:S(2)}, u32[]{:S(2)}) collective-permute-start(f32[4,80,640]{2,1,0:T(8,128)S(1)} %collective-permute-done.15.refs_2_), channel_id=1, source_target_pairs={{0,16},{1,17},{2,18},{3,19},{4,20},{5,21},{6,22},{7,23},{8,24},{9,... | collective-permute-start | bytes 2457608 | tf_op jit(solution)/shard_map/ppermute | solution.py:31
  192.8 2.1 collective-permute-done.16.refs_3_
  194.9 2.1 collective-permute-start.21
  197.0 2.2 collective-permute-start.22
  202.3 10.0 %pair_kernel.1 = (f32[160,640]{1,0:T(8,128)S(1)}, f32[4,200,128]{2,1,0:T(8,128)}, bf16[4,4,160,640]{3,2,1,0:T(8,128)(2,1)}, bf16[4,4,160,640]{3,2,1,0:T(8,128)(2,1)}) custom-call(s32[3]{0:T(128)S(1)} %pad_add_fusion.place_ref, f32[4,80,640]{2,1,0:T(8,128)} %copy-done.3, f32[4,80,640]{2,1,0:T(8,128)} %copy-done.5, f32[4,80,640]{2,1,0:T(8,128)} %copy-done.4, ...), custom_call_target="tpu_custom_call" | custom-call | flops 1572864000 | bytes 16777216 | tf_op jit(solution)/shard_map/pair_kernel/pallas_call | solution.py:177
  212.3 4.5 %all-to-all-start.5 = ((f32[4,200,128]{2,1,0:T(8,128)}), f32[4,200,128]{2,1,0:T(8,128)S(1)}, u32[]{:S(2)}, u32[]{:S(2)}) async-start(f32[4,200,128]{2,1,0:T(8,128)} %get-tuple-element.14), calls=%async_computation.5 | async-start | bytes 819200 | tf_op jit(solution)/shard_map/all_to_all | solution.py:310
  220.1 9.3 %all-to-all-done.5.came_ref = f32[4,200,128]{2,1,0:T(8,128)S(1)} async-done(((f32[4,200,128]{2,1,0:T(8,128)}), f32[4,200,128]{2,1,0:T(8,128)S(1)}, u32[]{:S(2)}, u32[]{:S(2)}) %all-to-all-start.5) | async-done | bytes 409632 | tf_op jit(solution)/shard_map/all_to_all | solution.py:310
  229.4 7.1 %density_kernel.1 = f32[160,2560]{1,0:T(8,128)} custom-call(f32[160,640]{1,0:T(8,128)S(1)} %get-tuple-element.13.pair_ref, f32[4,200,128]{2,1,0:T(8,128)S(1)} %all-to-all-done.5.came_ref, f32[160,1]{1,0:T(8,128)S(1)} %copy.29.row_ref, f32[1,640]{1,0:T(1,128)S(1)} %broadcast_in_dim.80.column_ref, bf16[4,4,160,640]{3,2,1,0:T(8,128)(2,1)} %get-tuple-element.15.high_ref, ...), custom_call_target="tpu_custom_call" | custom-call | flops 1572864000 | bytes 10485760 | tf_op jit(solution)/shard_map/density_kernel/pallas_call | solution.py:233
  (94 shorter events, 20.7 us)
Async XLA Ops:
  0.0 4.9 %copy-start = (f32[80,640]{1,0:T(8,128)S(1)}, f32[80,640]{1,0:T(8,128)}, u32[]{:S(2)}) copy-start(f32[80,640]{1,0:T(8,128)} %param.7) | copy-start | bytes 614404
  0.0 11.7 %copy-start.1 = (f32[160,4,1280]{2,1,0:T(4,128)S(1)}, f32[160,4,1280]{2,1,0:T(4,128)}, u32[]{:S(2)}) copy-start(f32[160,4,1280]{2,1,0:T(4,128)} %param.6) | copy-start | bytes 9830404
  2.9 8.8 %copy-start.21 = (s32[4]{0:T(128)S(1)}, s32[4]{0:T(128)}, u32[]{:S(2)}) copy-start(s32[4]{0:T(128)} %param.11) | copy-start | bytes 52
  2.9 8.8 %collective-permute-start = (f32[4,5,4,4,1280]{4,3,2,1,0:T(4,128)}, f32[4,5,4,4,1280]{4,3,2,1,0:T(4,128)}, u32[]{:S(2)}, u32[]{:S(2)}) collective-permute-start(f32[4,5,4,4,1280]{4,3,2,1,0:T(4,128)} %dynamic-slice_bitcast_fusion), channel_id=1, source_target_pairs={{0,16},{1,17},{2,18},{3,19},{4,20},{5,21},{6,22},{7,23},{8,24},{9,... | collective-permute-start | bytes 4915208 | tf_op jit(solution)/shard_map/ppermute | solution.py:31
  5.7 37.7 %all-to-all-start.2 = ((f32[4,40,640]{2,1,0:T(8,128)}), f32[4,40,640]{2,1,0:T(8,128)}, u32[]{:S(2)}, u32[]{:S(2)}) async-start(f32[4,40,640]{2,1,0:T(8,128)} %broadcast_in_dim.76), calls=%async_computation.2 | async-start | bytes 819200 | tf_op jit(solution)/shard_map/all_to_all | solution.py:36
  14.0 1.2 copy-start.2
  15.2 40.6 %copy-start.20 = (s32[16]{0:T(128)S(1)}, s32[16]{0:T(128)}, u32[]{:S(2)}) copy-start(s32[16]{0:T(128)} %param.10) | copy-start | bytes 196
  15.2 14.8 %collective-permute-start.1 = (f32[5,4,4,1280]{3,2,1,0:T(4,128)S(1)}, f32[5,4,4,1280]{3,2,1,0:T(4,128)S(1)}, u32[]{:S(2)}, u32[]{:S(2)}) collective-permute-start(f32[5,4,4,1280]{3,2,1,0:T(4,128)S(1)} %get-tuple-element.27), channel_id=1, source_target_pairs={{0,32},{1,33},{2,34},{3,35},{4,36},{5,37},{6,38},{7,39},{8,40},{9,... | collective-permute-start | bytes 1228808 | tf_op jit(solution)/shard_map/ppermute | solution.py:31
  18.7 21.2 %collective-permute-start.2 = (f32[5,4,4,1280]{3,2,1,0:T(4,128)S(1)}, f32[5,4,4,1280]{3,2,1,0:T(4,128)S(1)}, u32[]{:S(2)}, u32[]{:S(2)}) collective-permute-start(f32[5,4,4,1280]{3,2,1,0:T(4,128)S(1)} %get-tuple-element.26), channel_id=1, source_target_pairs={{0,64},{1,65},{2,66},{3,67},{4,68},{5,69},{6,70},{7,71},{8,72},{9,... | collective-permute-start | bytes 1228808 | tf_op jit(solution)/shard_map/ppermute | solution.py:31
  23.6 17.8 %collective-permute-start.3 = (f32[5,4,4,1280]{3,2,1,0:T(4,128)S(1)}, f32[5,4,4,1280]{3,2,1,0:T(4,128)S(1)}, u32[]{:S(2)}, u32[]{:S(2)}) collective-permute-start(f32[5,4,4,1280]{3,2,1,0:T(4,128)S(1)} %get-tuple-element.25), channel_id=1, source_target_pairs={{0,96},{1,97},{2,98},{3,99},{4,100},{5,101},{6,102},{7,103},{8,104... | collective-permute-start | bytes 1228808 | tf_op jit(solution)/shard_map/ppermute | solution.py:31
  43.4 39.5 %all-to-all-start = ((f32[4,5,4,1280]{3,2,1,0:T(4,128)}), f32[4,5,4,1280]{3,2,1,0:T(4,128)S(1)}, u32[]{:S(2)}, u32[]{:S(2)}) async-start(f32[4,5,4,1280]{3,2,1,0:T(4,128)} %bitcast.10), calls=%async_computation | async-start | bytes 819200 | tf_op jit(solution)/shard_map/all_to_all | solution.py:272
  56.1 14.3 %collective-permute-start.6 = (f32[4,40,640]{2,1,0:T(8,128)}, f32[4,40,640]{2,1,0:T(8,128)S(1)}, u32[]{:S(2)}, u32[]{:S(2)}) collective-permute-start(f32[4,40,640]{2,1,0:T(8,128)} %all-to-all-done.2.refs_0_), channel_id=1, source_target_pairs={{0,4},{1,5},{2,6},{3,7},{4,8},{5,9},{6,10},{7,11},{8,12},{9,13},{1... | collective-permute-start | bytes 1228808 | tf_op jit(solution)/shard_map/ppermute | solution.py:31
  59.5 13.8 %collective-permute-start.4 = (f32[4,40,640]{2,1,0:T(8,128)}, f32[4,40,640]{2,1,0:T(8,128)S(1)}, u32[]{:S(2)}, u32[]{:S(2)}) collective-permute-start(f32[4,40,640]{2,1,0:T(8,128)} %all-to-all-done.2.refs_0_), channel_id=1, source_target_pairs={{0,12},{1,13},{2,14},{3,15},{4,0},{5,1},{6,2},{7,3},{8,4},{9,5},{1... | collective-permute-start | bytes 1228808 | tf_op jit(solution)/shard_map/ppermute | solution.py:31
  62.0 19.0 %collective-permute-start.5 = (f32[4,40,640]{2,1,0:T(8,128)}, f32[4,40,640]{2,1,0:T(8,128)S(1)}, u32[]{:S(2)}, u32[]{:S(2)}) collective-permute-start(f32[4,40,640]{2,1,0:T(8,128)} %all-to-all-done.2.refs_0_), channel_id=1, source_target_pairs={{0,8},{1,9},{2,10},{3,11},{4,12},{5,13},{6,14},{7,15},{8,0},{9,1},... | collective-permute-start | bytes 1228808 | tf_op jit(solution)/shard_map/ppermute | solution.py:31
  66.1 24.4 %collective-permute-start.7 = (f32[4,40,640]{2,1,0:T(8,128)}, f32[4,40,640]{2,1,0:T(8,128)S(1)}, u32[]{:S(2)}, u32[]{:S(2)}) collective-permute-start(f32[4,40,640]{2,1,0:T(8,128)} %all-to-all-done.2.refs_0_), channel_id=1, source_target_pairs={{0,16},{1,17},{2,18},{3,19},{4,20},{5,21},{6,22},{7,23},{8,24},{9,... | collective-permute-start | bytes 1228808 | tf_op jit(solution)/shard_map/ppermute | solution.py:31
  70.4 20.1 %copy-start.8 = (f32[4,40,640]{2,1,0:T(8,128)}, f32[4,40,640]{2,1,0:T(8,128)S(1)}, u32[]{:S(2)}) copy-start(f32[4,40,640]{2,1,0:T(8,128)S(1)} %collective-permute-done.6.refs_3_) | copy-start | bytes 1228804
  70.4 20.1 %collective-permute-start.10 = (f32[4,40,640]{2,1,0:T(8,128)S(1)}, f32[4,40,640]{2,1,0:T(8,128)S(1)}, u32[]{:S(2)}, u32[]{:S(2)}) collective-permute-start(f32[4,40,640]{2,1,0:T(8,128)S(1)} %collective-permute-done.6.refs_3_), channel_id=1, source_target_pairs={{0,16},{1,17},{2,18},{3,19},{4,20},{5,21},{6,22},{7,23},{8,24},{9,... | collective-permute-start | bytes 1228808 | tf_op jit(solution)/shard_map/ppermute | solution.py:31
  73.3 17.2 %copy-start.9 = (f32[4,40,640]{2,1,0:T(8,128)}, f32[4,40,640]{2,1,0:T(8,128)S(1)}, u32[]{:S(2)}) copy-start(f32[4,40,640]{2,1,0:T(8,128)S(1)} %collective-permute-done.4.refs_1_) | copy-start | bytes 1228804
  73.3 17.2 %collective-permute-start.8 = (f32[4,40,640]{2,1,0:T(8,128)S(1)}, f32[4,40,640]{2,1,0:T(8,128)S(1)}, u32[]{:S(2)}, u32[]{:S(2)}) collective-permute-start(f32[4,40,640]{2,1,0:T(8,128)S(1)} %collective-permute-done.4.refs_1_), channel_id=1, source_target_pairs={{0,16},{1,17},{2,18},{3,19},{4,20},{5,21},{6,22},{7,23},{8,24},{9,... | collective-permute-start | bytes 1228808 | tf_op jit(solution)/shard_map/ppermute | solution.py:31
  81.0 9.5 %copy-start.10 = (f32[4,40,640]{2,1,0:T(8,128)}, f32[4,40,640]{2,1,0:T(8,128)S(1)}, u32[]{:S(2)}) copy-start(f32[4,40,640]{2,1,0:T(8,128)S(1)} %collective-permute-done.5.refs_2_) | copy-start | bytes 1228804
  81.0 11.2 %collective-permute-start.9 = (f32[4,40,640]{2,1,0:T(8,128)S(1)}, f32[4,40,640]{2,1,0:T(8,128)}, u32[]{:S(2)}, u32[]{:S(2)}) collective-permute-start(f32[4,40,640]{2,1,0:T(8,128)S(1)} %collective-permute-done.5.refs_2_), channel_id=1, source_target_pairs={{0,16},{1,17},{2,18},{3,19},{4,20},{5,21},{6,22},{7,23},{8,24},{9,... | collective-permute-start | bytes 1228808 | tf_op jit(solution)/shard_map/ppermute | solution.py:31
  83.9 11.4 %all-to-all-start.1 = ((f32[4,5,1280]{2,1,0:T(8,128)}), f32[4,5,1280]{2,1,0:T(8,128)}, u32[]{:S(2)}, u32[]{:S(2)}) async-start(f32[4,5,1280]{2,1,0:T(8,128)} %fusion.9), calls=%async_computation.1 | async-start | bytes 327680 | tf_op jit(solution)/shard_map/all_to_all | solution.py:280
  90.5 0.9 copy-start.13
  99.9 49.1 %all-to-all-start.3 = ((f32[16,5,4,640]{3,2,1,0:T(4,128)}), f32[16,5,4,640]{3,2,1,0:T(4,128)}, u32[]{:S(2)}, u32[]{:S(2)}) async-start(f32[16,5,4,640]{3,2,1,0:T(4,128)} %broadcast_in_dim.78), calls=%async_computation.3 | async-start | bytes 1638400 | tf_op jit(solution)/shard_map/all_to_all | solution.py:297
  119.8 13.3 %collective-permute-start.11 = (f32[160,640]{1,0:T(8,128)S(1)}, f32[160,640]{1,0:T(8,128)S(1)}, u32[]{:S(2)}, u32[]{:S(2)}) collective-permute-start(f32[160,640]{1,0:T(8,128)S(1)} %get-tuple-element.23), channel_id=1, source_target_pairs={{0,12},{1,13},{2,14},{3,15},{4,0},{5,1},{6,2},{7,3},{8,4},{9,5},{1... | collective-permute-start | bytes 1228808 | tf_op jit(solution)/shard_map/ppermute | solution.py:31
  123.2 18.5 %collective-permute-start.12 = (f32[160,640]{1,0:T(8,128)S(1)}, f32[160,640]{1,0:T(8,128)S(1)}, u32[]{:S(2)}, u32[]{:S(2)}) collective-permute-start(f32[160,640]{1,0:T(8,128)S(1)} %get-tuple-element.22), channel_id=1, source_target_pairs={{0,8},{1,9},{2,10},{3,11},{4,12},{5,13},{6,14},{7,15},{8,0},{9,1},... | collective-permute-start | bytes 1228808 | tf_op jit(solution)/shard_map/ppermute | solution.py:31
  126.6 17.9 %collective-permute-start.13 = (f32[160,640]{1,0:T(8,128)S(1)}, f32[160,640]{1,0:T(8,128)S(1)}, u32[]{:S(2)}, u32[]{:S(2)}) collective-permute-start(f32[160,640]{1,0:T(8,128)S(1)} %get-tuple-element.24), channel_id=1, source_target_pairs={{0,4},{1,5},{2,6},{3,7},{4,8},{5,9},{6,10},{7,11},{8,12},{9,13},{1... | collective-permute-start | bytes 1228808 | tf_op jit(solution)/shard_map/ppermute | solution.py:31
  151.5 50.8 %all-to-all-start.4 = ((f32[4,160,640]{2,1,0:T(8,128)}), f32[4,160,640]{2,1,0:T(8,128)S(1)}, u32[]{:S(2)}, u32[]{:S(2)}) async-start(f32[4,160,640]{2,1,0:T(8,128)} %bitcast.79), calls=%async_computation.4 | async-start | bytes 3276800 | tf_op jit(solution)/shard_map/all_to_all | solution.py:307
  157.9 44.4 %copy-start.3 = (f32[4,80,640]{2,1,0:T(8,128)}, f32[4,80,640]{2,1,0:T(8,128)S(1)}, u32[]{:S(2)}) copy-start(f32[4,80,640]{2,1,0:T(8,128)S(1)} %copy.28.refs_0_) | copy-start | bytes 2457604
  157.9 23.3 %collective-permute-start.15 = (f32[4,80,640]{2,1,0:T(8,128)S(1)}, f32[4,80,640]{2,1,0:T(8,128)S(1)}, u32[]{:S(2)}, u32[]{:S(2)}) collective-permute-start(f32[4,80,640]{2,1,0:T(8,128)S(1)} %copy.28.refs_0_), channel_id=1, source_target_pairs={{0,32},{1,33},{2,34},{3,35},{4,36},{5,37},{6,38},{7,39},{8,40},{9,... | collective-permute-start | bytes 2457608 | tf_op jit(solution)/shard_map/ppermute | solution.py:31
  163.1 21.7 %collective-permute-start.14 = (f32[4,80,640]{2,1,0:T(8,128)S(1)}, f32[4,80,640]{2,1,0:T(8,128)S(1)}, u32[]{:S(2)}, u32[]{:S(2)}) collective-permute-start(f32[4,80,640]{2,1,0:T(8,128)S(1)} %copy.28.refs_0_), channel_id=1, source_target_pairs={{0,96},{1,97},{2,98},{3,99},{4,100},{5,101},{6,102},{7,103},{8,104... | collective-permute-start | bytes 2457608 | tf_op jit(solution)/shard_map/ppermute | solution.py:31
  165.1 34.2 %collective-permute-start.18 = (f32[4,80,640]{2,1,0:T(8,128)S(1)}, f32[4,80,640]{2,1,0:T(8,128)S(1)}, u32[]{:S(2)}, u32[]{:S(2)}) collective-permute-start(f32[4,80,640]{2,1,0:T(8,128)S(1)} %copy.28.refs_0_), channel_id=1, source_target_pairs={{0,16},{1,17},{2,18},{3,19},{4,20},{5,21},{6,22},{7,23},{8,24},{9,... | collective-permute-start | bytes 2457608 | tf_op jit(solution)/shard_map/ppermute | solution.py:31
  181.3 19.4 %copy-start.4 = (f32[4,80,640]{2,1,0:T(8,128)}, f32[4,80,640]{2,1,0:T(8,128)S(1)}, u32[]{:S(2)}) copy-start(f32[4,80,640]{2,1,0:T(8,128)S(1)} %collective-permute-done.15.refs_2_) | copy-start | bytes 2457604
  181.3 13.6 %collective-permute-start.16 = (f32[2,80,640]{2,1,0:T(8,128)S(1)}, f32[2,80,640]{2,1,0:T(8,128)S(1)}, u32[]{:S(2)}, u32[]{:S(2)}) collective-permute-start(f32[2,80,640]{2,1,0:T(8,128)S(1)} %slice.28), channel_id=1, source_target_pairs={{0,32},{1,33},{2,34},{3,35},{4,36},{5,37},{6,38},{7,39},{8,40},{9,... | collective-permute-start | bytes 1228808 | tf_op jit(solution)/shard_map/ppermute | solution.py:31
  184.8 15.8 %copy-start.5 = (f32[4,80,640]{2,1,0:T(8,128)}, f32[4,80,640]{2,1,0:T(8,128)S(1)}, u32[]{:S(2)}) copy-start(f32[4,80,640]{2,1,0:T(8,128)S(1)} %collective-permute-done.14.refs_1_) | copy-start | bytes 2457604
  184.9 12.1 %collective-permute-start.17 = (f32[2,80,640]{2,1,0:T(8,128)S(1)}, f32[2,80,640]{2,1,0:T(8,128)S(1)}, u32[]{:S(2)}, u32[]{:S(2)}) collective-permute-start(f32[2,80,640]{2,1,0:T(8,128)S(1)} %slice.29), channel_id=1, source_target_pairs={{0,96},{1,97},{2,98},{3,99},{4,100},{5,101},{6,102},{7,103},{8,104... | collective-permute-start | bytes 1228808 | tf_op jit(solution)/shard_map/ppermute | solution.py:31
  188.4 12.2 %collective-permute-start.19 = (f32[4,80,640]{2,1,0:T(8,128)S(1)}, f32[4,80,640]{2,1,0:T(8,128)S(1)}, u32[]{:S(2)}, u32[]{:S(2)}) collective-permute-start(f32[4,80,640]{2,1,0:T(8,128)S(1)} %collective-permute-done.14.refs_1_), channel_id=1, source_target_pairs={{0,16},{1,17},{2,18},{3,19},{4,20},{5,21},{6,22},{7,23},{8,24},{9,... | collective-permute-start | bytes 2457608 | tf_op jit(solution)/shard_map/ppermute | solution.py:31
  190.4 11.9 %collective-permute-start.20 = (f32[4,80,640]{2,1,0:T(8,128)S(1)}, f32[4,80,640]{2,1,0:T(8,128)}, u32[]{:S(2)}, u32[]{:S(2)}) collective-permute-start(f32[4,80,640]{2,1,0:T(8,128)S(1)} %collective-permute-done.15.refs_2_), channel_id=1, source_target_pairs={{0,16},{1,17},{2,18},{3,19},{4,20},{5,21},{6,22},{7,23},{8,24},{9,... | collective-permute-start | bytes 2457608 | tf_op jit(solution)/shard_map/ppermute | solution.py:31
  194.9 7.4 %copy-start.12 = (f32[2,80,640]{2,1,0:T(8,128)}, f32[2,80,640]{2,1,0:T(8,128)S(1)}, u32[]{:S(2)}) copy-start(f32[2,80,640]{2,1,0:T(8,128)S(1)} %collective-permute-done.16.refs_3_) | copy-start | bytes 1228804
  194.9 4.5 %collective-permute-start.21 = (f32[2,80,640]{2,1,0:T(8,128)S(1)}, f32[2,80,640]{2,1,0:T(8,128)S(1)}, u32[]{:S(2)}, u32[]{:S(2)}) collective-permute-start(f32[2,80,640]{2,1,0:T(8,128)S(1)} %collective-permute-done.16.refs_3_), channel_id=1, source_target_pairs={{0,16},{1,17},{2,18},{3,19},{4,20},{5,21},{6,22},{7,23},{8,24},{9,... | collective-permute-start | bytes 1228808 | tf_op jit(solution)/shard_map/ppermute | solution.py:31
  197.0 3.7 %copy-start.14 = (f32[2,80,640]{2,1,0:T(8,128)}, f32[2,80,640]{2,1,0:T(8,128)S(1)}, u32[]{:S(2)}) copy-start(f32[2,80,640]{2,1,0:T(8,128)S(1)} %collective-permute-done.17.refs_4_) | copy-start | bytes 1228804
  197.0 3.6 %collective-permute-start.22 = (f32[2,80,640]{2,1,0:T(8,128)S(1)}, f32[2,80,640]{2,1,0:T(8,128)S(1)}, u32[]{:S(2)}, u32[]{:S(2)}) collective-permute-start(f32[2,80,640]{2,1,0:T(8,128)S(1)} %collective-permute-done.17.refs_4_), channel_id=1, source_target_pairs={{0,16},{1,17},{2,18},{3,19},{4,20},{5,21},{6,22},{7,23},{8,24},{9,... | collective-permute-start | bytes 1228808 | tf_op jit(solution)/shard_map/ppermute | solution.py:31
  199.3 18.7 %copy-start.18 = (f32[640]{0:T(1024)S(1)}, f32[640]{0:T(1024)}, u32[]{:S(2)}) copy-start(f32[640]{0:T(1024)} %param.9) | copy-start | bytes 7684
  199.3 18.7 %copy-start.19 = (f32[128]{0:T(128)S(1)}, f32[128]{0:T(128)}, u32[]{:S(2)}) copy-start(f32[128]{0:T(128)} %param.8) | copy-start | bytes 1540
  199.3 1.4 copy-start.6
  199.3 1.3 copy-start.16
  201.4 0.9 copy-start.7
  212.3 17.1 %all-to-all-start.5 = ((f32[4,200,128]{2,1,0:T(8,128)}), f32[4,200,128]{2,1,0:T(8,128)S(1)}, u32[]{:S(2)}, u32[]{:S(2)}) async-start(f32[4,200,128]{2,1,0:T(8,128)} %get-tuple-element.14), calls=%async_computation.5 | async-start | bytes 819200 | tf_op jit(solution)/shard_map/all_to_all | solution.py:310
  (3 other events, 2.3 us)
